TPU v7x, 512 devices: a whole 4x4x16 slice. The times are simulated.
512 devices in a mesh: row: 32 (over y_lo, z), col: 16 (over y_hi, x, core).
Axes of the slice: x: 4, y: 4 (y_hi: 2, y_lo: 2; y = y_hi * 2 + y_lo), z: 16, core: 2. Of those that a mesh axis runs over, the one named last changes fastest.
Arguments:
- tokens: bfloat16 [512, 8192], P('col', 'row'), may hold values from -40 to 40
- norm_gain: bfloat16 [8192], P('row'), may hold values from 0.5 to 2
- w_query: bfloat16 [8192, 8192], P('row', 'col'), may hold values from -0.0625 to 0.0625
- key_weight: bfloat16 [8192, 1024], P('row'), may hold values from -0.125 to 0.125
- value_weight: bfloat16 [8192, 1024], P('row'), may hold values from -0.0625 to 0.0625
- w_out: bfloat16 [8192, 8192], P('col', 'row'), may hold values from -0.25 to 0.25
- cached_key_rows: bfloat16 [65536, 1024], P('row'), may hold values from -120 to 120
- cached_value_rows: bfloat16 [65536, 1024], P('row'), may hold values from -9 to 9
Outputs:
- attn_out: bfloat16 [512, 8192], P('col', 'row')
All inputs are finite; a program needn't handle non-finite values.
Results may differ from a plain program's by a relative error of at most 0.039.
Values may be sent and summed in bfloat16 or wider, within the bound.
No kernel may reach another device: no remote copies, remote signals or barrier semaphores. Data moves between devices by JAX's collectives and lax.ppermute only.
A program may use at most 128 MiB of HBM per device.

v0:
```python
import math

import jax
import jax.numpy as jnp
from jax import lax
from jax.sharding import PartitionSpec as P

MODEL_WIDTH = 8192
QUERY_HEADS = 64
KEY_VALUE_HEADS = 8
HEAD_WIDTH = 128


rope_base = 500000.0
epsilon = 1e-05


def scaled_freqs(head_size):
    half = head_size // 2
    ladder = jnp.arange(half, dtype=jnp.float32) * (2.0 / head_size)
    base_freqs = jnp.power(jnp.float32(rope_base), -ladder)
    wavelen = 2.0 * math.pi / base_freqs
    smooth = (8192.0 / wavelen - 1.0) / 3.0
    middle = (1.0 - smooth) * base_freqs / 8.0 + smooth * base_freqs
    return jnp.where(
        wavelen < 2048.0, base_freqs, jnp.where(wavelen > 8192.0, base_freqs / 8.0, middle)
    )


def apply_rotary_heads(vectors, token_positions):
    half = vectors.shape[-1] // 2
    freqs = scaled_freqs(vectors.shape[-1])
    angles = token_positions.astype(jnp.float32)[:, None] * freqs[None, :]
    cosine = jnp.cos(angles)[:, None, :]
    sine = jnp.sin(angles)[:, None, :]
    first = vectors[..., :half]
    second = vectors[..., half:]
    return jnp.concatenate(
        [first * cosine - second * sine, second * cosine + first * sine], axis=-1
    )


def body(
    tokens, norm_gain, w_query, key_weight, value_weight, w_out, cached_key_rows, cached_value_rows
):
    row_count = lax.axis_size("row")
    row_index = lax.axis_index("row")
    col_index = lax.axis_index("col")
    whole = lax.all_gather(tokens, "col", axis=0, tiled=True)
    seq_total = whole.shape[0]
    tok_rows = seq_total // row_count
    cache_rows = cached_key_rows.shape[0]
    cache_total = cache_rows * row_count
    heads_here = w_query.shape[1] // HEAD_WIDTH
    group_factor = QUERY_HEADS // KEY_VALUE_HEADS
    kv_here = max(1, heads_here // group_factor)
    kv_first = col_index * heads_here // group_factor
    kv_width = kv_here * HEAD_WIDTH
    key_panel = lax.dynamic_slice_in_dim(key_weight, kv_first * HEAD_WIDTH, kv_width, 1)
    value_panel = lax.dynamic_slice_in_dim(value_weight, kv_first * HEAD_WIDTH, kv_width, 1)
    kv_panel = jnp.concatenate([key_panel, value_panel], axis=1)
    widened = whole.astype(jnp.float32)
    square_part = jnp.sum(widened * widened, axis=1)
    scaled = (widened * norm_gain.astype(jnp.float32)[None, :]).astype(jnp.bfloat16)
    query_part = jnp.dot(scaled, w_query, preferred_element_type=jnp.float32)
    row_start = row_index * tok_rows
    query_pos = cache_total + jnp.arange(seq_total, dtype=jnp.int32)
    key_pos = cache_total + row_start + jnp.arange(tok_rows, dtype=jnp.int32)
    kv_part = jnp.dot(scaled, kv_panel, preferred_element_type=jnp.float32)
    query_raw, kv_whole, square_sum = lax.psum((query_part, kv_part, square_part), "row")
    kv_raw = lax.dynamic_slice_in_dim(kv_whole, row_start, tok_rows, 0)
    inverse_root_mean = lax.rsqrt(square_sum / MODEL_WIDTH + epsilon)
    inv_rows = lax.dynamic_slice_in_dim(inverse_root_mean, row_start, tok_rows, 0)
    queries = apply_rotary_heads(
        (query_raw * inverse_root_mean[:, None]).reshape(seq_total, heads_here, HEAD_WIDTH),
        query_pos,
    ).astype(jnp.bfloat16)
    fresh_keys = apply_rotary_heads(
        (kv_raw[:, :kv_width] * inv_rows[:, None]).reshape(tok_rows, kv_here, HEAD_WIDTH), key_pos
    ).astype(jnp.bfloat16)
    fresh_values = (
        (kv_raw[:, kv_width:] * inv_rows[:, None])
        .astype(jnp.bfloat16)
        .reshape(tok_rows, kv_here, HEAD_WIDTH)
    )
    old_keys = lax.dynamic_slice_in_dim(
        cached_key_rows, kv_first * HEAD_WIDTH, kv_width, 1
    ).reshape(cache_rows, kv_here, HEAD_WIDTH)
    old_values = lax.dynamic_slice_in_dim(
        cached_value_rows, kv_first * HEAD_WIDTH, kv_width, 1
    ).reshape(cache_rows, kv_here, HEAD_WIDTH)
    key_matrix = jnp.concatenate([old_keys, fresh_keys], axis=0)
    value_matrix = jnp.concatenate([old_values, fresh_values], axis=0)
    grouped = queries.reshape(seq_total, kv_here, heads_here // kv_here, HEAD_WIDTH)
    score_scale = 1.0 / math.sqrt(HEAD_WIDTH)
    scores = (
        jnp.einsum("sknd,tkd->sknt", grouped, key_matrix, preferred_element_type=jnp.float32)
        * score_scale
    )
    slot_index = jnp.arange(cache_rows + tok_rows, dtype=jnp.int32)
    block_pos = row_start + slot_index - cache_rows
    query_index = jnp.arange(seq_total, dtype=jnp.int32)
    visible = (slot_index[None, :] < cache_rows) | (block_pos[None, :] <= query_index[:, None])
    masked = jnp.where(visible[:, None, None, :], scores, -jnp.inf)
    local_max = jnp.max(masked, axis=-1)
    row_max = lax.pmax(local_max, "row")
    weights = jnp.exp(masked - row_max[..., None])
    denom_part = jnp.sum(weights, axis=-1).reshape(seq_total, heads_here)
    numer_part = jnp.einsum(
        "sknt,tkd->sknd",
        weights.astype(jnp.bfloat16),
        value_matrix,
        preferred_element_type=jnp.float32,
    )
    numer_part = numer_part.reshape(seq_total, heads_here * HEAD_WIDTH)
    numer, denom = lax.psum((numer_part, denom_part), "row")
    context = (
        (numer.reshape(seq_total, heads_here, HEAD_WIDTH) / denom[:, :, None])
        .reshape(seq_total, heads_here * HEAD_WIDTH)
        .astype(jnp.bfloat16)
    )
    result = lax.psum_scatter(
        jnp.dot(context, w_out, preferred_element_type=jnp.float32),
        "col",
        scatter_dimension=0,
        tiled=True,
    )
    return result.astype(jnp.bfloat16)


def solution(mesh):
    placed = (
        P("col", "row"),
        P("row"),
        P("row", "col"),
        P("row", None),
        P("row", None),
        P("col", "row"),
        P("row", None),
        P("row", None),
    )
    return jax.shard_map(
        body, mesh=mesh, in_specs=placed, out_specs=P("col", "row"), check_vma=False
    )
```

profile of v0, /device:TPU:1, one launch (start us, length us, event | category | flops | bytes accessed | tf_op | source)
XLA Modules:
  0.0 726.8 jit_solution(2877151686189830898)
XLA Ops:
  6.5 0.0 copy-start
  6.5 0.0 all-reduce.6.cloned.1.call-start
  6.5 26.8 %all_gather.3 = bf16[512,256]{1,0:T(8,128)(2,1)S(1)} all-gather(bf16[32,256]{1,0:T(8,128)(2,1)} %param.8), channel_id=1, replica_groups=mesh['row'=32,'col'=16] {'col'}, dimensions={0}, use_global_device_ids=true | all-gather | bytes 278528 | tf_op jit(solution)/shard_map/all_gather | solution.py:49
  33.3 0.7 convert_element_type.54
  34.0 0.9 constant_dynamic-slice_fusion
  34.9 0.0 copy-done
  34.9 1.3 fusion.21
  36.2 1.0 fusion.23
  37.3 0.0 all-reduce.6.cloned.1.call-update
  37.3 0.0 all-reduce.4.cloned.1.call-start
  37.4 0.1 fusion.17
  37.5 56.9 %psum.36 = f32[512]{0:T(512)S(1)} all-reduce(f32[512]{0:T(512)S(1)} %fusion.17), channel_id=1, replica_groups=mesh['row'=32,'col'=16] {'row'}, use_global_device_ids=true, to_apply=%region_2.3 | all-reduce | flops 512 | bytes 4096 | tf_op jit(solution)/shard_map/psum | solution.py:70
  94.4 0.1 dynamic_slice.22
  94.5 1.9 dynamic-slice_bitcast_fusion
  96.4 1.9 dynamic-slice_bitcast_fusion.1
  98.3 1.8 multiply_cosine_fusion
  100.0 1.5 fusion.7
  101.6 174.5 %all-reduce.6.cloned.1.call-done = (f32[512,256]{1,0:T(8,128)}, f32[512,512]{1,0:T(8,128)}) async-done(((f32[512,256]{1,0:T(8,128)}, f32[512,512]{1,0:T(8,128)}), (f32[512,256]{1,0:T(8,128)}, f32[512,512]{1,0:T(8,128)})) %all-reduce.6.cloned.1.call-update) | async-done | bytes 1572880 | tf_op jit(solution)/shard_map/psum | solution.py:70
  276.1 1.4 broadcast_multiply_fusion
  277.4 0.4 reshape.287
  277.8 0.6 fusion.44
  278.4 0.8 fusion.38
  279.2 0.1 fusion.33
  279.3 1.3 subtract_convert_fusion
  280.6 0.0 copy-start.1
  280.6 8.7 %fusion.2 = (f32[512,4]{0,1:T(4,128)S(1)}, f32[2064,512,4]{1,0,2:T(8,128)}) fusion(pred[512,2064]{0,1:T(8,128)(4,1)S(1)} %fusion.7, bf16[512,4,64]{2,0,1:T(8,128)(2,1)S(1)} %get-tuple-element.8, bf16[512,4,64]{2,0,1:T(8,128)(2,1)S(1)} %get-tuple-element.7, bf16[16,1,64]{2,0,1:T(8,128)(2,1)S(1)} %get-tuple-element.14, ...), kind=kOutput, calls=%fused_computation.4 | convolution fusion | flops 1097443328 | bytes 19025920 | tf_op jit(solution)/shard_map/sknd,tkd->sknt/dot_general | solution.py:97
  289.3 49.9 %pmax.7 = f32[512,4]{0,1:T(4,128)S(1)} all-reduce(f32[512,4]{0,1:T(4,128)S(1)} %get-tuple-element.17), channel_id=1, replica_groups=mesh['row'=32,'col'=16] {'row'}, use_global_device_ids=true, to_apply=%region_5.6 | all-reduce | flops 2048 | bytes 16384 | tf_op jit(solution)/shard_map/pmax | solution.py:106
  339.2 0.0 copy-done.1
  339.2 9.9 %fusion.4 = f32[128,512,4]{1,0,2:T(8,128)} fusion(f32[2064,512,4]{1,0,2:T(8,128)} %get-tuple-element.18, f32[512,4]{0,1:T(4,128)S(1)} %pmax.7, pred[512,2064]{0,1:T(8,128)(4,1)S(1)} %fusion.7, bf16[16,1,128]{2,0,1:T(8,128)(2,1)S(1)} %get-tuple-element.11, bf16[2048,1,128]{2,0,1:T(8,128)(2,1)S(1)} %copy-done.1), kind=kOutput, calls=%fused_computation.6 | convolution fusion | flops 1100095488 | bytes 19550208 | tf_op jit(solution)/shard_map/sknt,tkd->sknd/dot_general | solution.py:109
  349.2 0.0 all-reduce.4.cloned.1.call-update
  349.2 0.0 copy-start.2
  349.2 0.2 reduce-scatter.2.cloned.1.call-start
  349.5 9.4 %fusion = f32[512,4]{0,1:T(4,128)S(1)} fusion(f32[2064,512,4]{1,0,2:T(8,128)} %get-tuple-element.18, f32[512,4]{0,1:T(4,128)S(1)} %pmax.7, pred[512,2064]{0,1:T(8,128)(4,1)S(1)} %fusion.7), kind=kLoop, calls=%fused_computation.2 | loop fusion | flops 16906240 | bytes 17981440 | tf_op jit(solution)/shard_map/reduce_sum | solution.py:108
  358.8 47.7 %psum.39 = f32[512,4]{0,1:T(4,128)S(1)} all-reduce(f32[512,4]{0,1:T(4,128)S(1)} %fusion), channel_id=1, replica_groups=mesh['row'=32,'col'=16] {'row'}, use_global_device_ids=true, to_apply=%region_8.9 | all-reduce | flops 2048 | bytes 16384 | tf_op jit(solution)/shard_map/psum | solution.py:116
  406.6 206.5 %all-reduce.4.cloned.1.call-done = f32[512,512]{0,1:T(8,128)} async-done(((f32[512,512]{0,1:T(8,128)}), f32[512,512]{0,1:T(8,128)}) %all-reduce.4.cloned.1.call-update) | async-done | bytes 1048592 | tf_op jit(solution)/shard_map/psum | solution.py:116
  613.1 1.3 fusion.8
  614.4 0.0 copy-done.2
  614.4 1.1 fusion.45
  615.5 0.0 reduce-scatter.2.cloned.1.call-update
  615.6 103.4 %reduce-scatter.2.cloned.1.call-done = f32[32,256]{1,0:T(8,128)} async-done(((f32[512,256]{1,0:T(8,128)}), f32[32,256]{1,0:T(8,128)}) %reduce-scatter.2.cloned.1.call-update) | async-done | bytes 32784 | tf_op jit(solution)/shard_map/reduce_scatter | solution.py:122
  718.9 1.4 convert_element_type.61
  (6 shorter events, 0.0 us)
Async XLA Ops:
  6.5 28.3 %copy-start = (bf16[256,512]{1,0:T(8,128)(2,1)S(1)}, bf16[256,512]{1,0:T(8,128)(2,1)}, u32[]{:S(2)}) copy-start(bf16[256,512]{1,0:T(8,128)(2,1)} %param.10) | copy-start | bytes 786436
  6.5 269.5 %all-reduce.6.cloned.1.call-start = ((), (), s32[]{:S(2)}) async-start(), calls=%async_computation.3 | async-start | bytes 3145728 | tf_op jit(solution)/shard_map/psum | solution.py:70
  37.3 575.8 %all-reduce.4.cloned.1.call-start = ((), (), s32[]{:S(2)}) async-start(), calls=%async_computation.1 | async-start | bytes 2097152 | tf_op jit(solution)/shard_map/psum | solution.py:116
  280.6 58.6 %copy-start.1 = (bf16[2048,1,128]{2,0,1:T(8,128)(2,1)S(1)}, bf16[2048,1,128]{2,0,1:T(8,128)(2,1)}, u32[]{:S(2)}) copy-start(bf16[2048,1,128]{2,0,1:T(8,128)(2,1)} %dynamic-slice_bitcast_fusion.1) | copy-start | bytes 1572868
  349.2 265.2 %copy-start.2 = (bf16[512,256]{1,0:T(8,128)(2,1)S(1)}, bf16[512,256]{1,0:T(8,128)(2,1)}, u32[]{:S(2)}) copy-start(bf16[512,256]{1,0:T(8,128)(2,1)} %param.13) | copy-start | bytes 786436
  349.2 369.7 %reduce-scatter.2.cloned.1.call-start = ((), (), s32[]{:S(2)}) async-start(), calls=%async_computation.2 | async-start | bytes 557056 | tf_op jit(solution)/shard_map/reduce_scatter | solution.py:122
Sparse Core Ops, SparseCore 0:
  37.4 238.5 all-reduce.5
  349.3 263.6 all-reduce.3
  617.7 101.1 reduce-scatter.1
where the time goes:
time: 728 us; the launch traced here: 727 us
  waiting for transfers between devices  484 us (66%)
  blocking collectives  181 us (25%)
  matrix products  22.2 us (3%)
  other arithmetic  19.8 us (3%)
  between operations  13.2 us (2%)
    psum x1, waiting for transfers between devices, body(): numer, denom = lax.psum((numer_part, denom_part), 'row')  206 us
    psum x1, waiting for transfers between devices, body(): lax.psum((query_part, kv_part, square_part), 'row')  174 us
    reduce_scatter x1, waiting for transfers between devices, body(): lax.psum_scatter(jnp.dot(context, w_out, preferred_element_type=jnp.float...  103 us
    psum x1, blocking collectives, body(): lax.psum((query_part, kv_part, square_part), 'row')  56.9 us
    pmax x1, blocking collectives, body(): row_max = lax.pmax(local_max, 'row')  49.9 us
    psum x1, blocking collectives, body(): numer, denom = lax.psum((numer_part, denom_part), 'row')  47.7 us
    all_gather x1, blocking collectives, body(): whole = lax.all_gather(tokens, 'col', axis=0, tiled=True)  26.8 us
  transfers between devices with their start and end apart: 3, of which 3 were waited for; matrix products, arithmetic and copies ran while one was open for 2% of the time, Pallas kernels for 0%

commit v1 on v0

v1 whole, which is shorter than its diff:
```python
import math

import jax
import jax.numpy as jnp
import numpy as np
from jax import lax
from jax.sharding import Mesh, PartitionSpec as P

MODEL_WIDTH = 8192
QUERY_HEADS = 64
KEY_VALUE_HEADS = 8
HEAD_WIDTH = 128
BLOCK_TOKENS = 512
CACHED_COUNT = 65536

rope_base = 500000.0
epsilon = 1e-05

NEAR = ("ylo", "zl")
NEAR_SIZE = 8
FAR_SIZE = 4
COLS = 16
HEADS_HERE = QUERY_HEADS // COLS
TOK_NEAR = BLOCK_TOKENS // NEAR_SIZE
TOK_ROW = TOK_NEAR // FAR_SIZE
Q_ROWS = HEADS_HERE * TOK_NEAR

bf16 = jnp.bfloat16
f32 = jnp.float32


def rope_tables():
    half = HEAD_WIDTH // 2
    ladder = np.arange(half, dtype=np.float32) * np.float32(2.0 / HEAD_WIDTH)
    base = np.power(np.float32(rope_base), -ladder).astype(np.float32)
    wavelen = (np.float32(2.0 * math.pi) / base).astype(np.float32)
    smooth = ((np.float32(8192.0) / wavelen - 1) / 3).astype(np.float32)
    middle = ((1 - smooth) * base / 8 + smooth * base).astype(np.float32)
    freqs = np.where(wavelen < 2048, base, np.where(wavelen > 8192, base / 8, middle))
    pos = (CACHED_COUNT + np.arange(BLOCK_TOKENS)).astype(np.float32)
    angles = (pos[:, None] * freqs.astype(np.float32)[None, :]).astype(np.float32)
    cos = np.cos(angles.astype(np.float64)).astype(np.float32)
    sin = np.sin(angles.astype(np.float64)).astype(np.float32)
    return np.concatenate([cos, cos], 1), np.concatenate([-sin, sin], 1)


COS_TABLE, SIN_TABLE = rope_tables()


def split3(x):
    hi = lax.reduce_precision(x, 8, 7)
    rest = x - hi
    mid = lax.reduce_precision(rest, 8, 7)
    return hi.astype(bf16), mid.astype(bf16), (rest - mid).astype(bf16)


def rotate(u, cos, sin):
    half = HEAD_WIDTH // 2
    swapped = jnp.concatenate([u[..., half:], u[..., :half]], axis=-1)
    return u * cos + swapped * sin


def exchange(x, axes):
    return lax.all_to_all(x, axes, 0, 0, tiled=True)


def spread(x, count, axes):
    return exchange(jnp.broadcast_to(x[None], (count,) + x.shape), axes)


def body(tokens, norm_gain, w_query, key_weight, value_weight, w_out, cached_keys, cached_values):
    near = lax.axis_index("ylo") * 4 + lax.axis_index("zl")
    far = lax.axis_index("zh")
    group = lax.axis_index("col") // 2

    whole = spread(tokens, COLS, "col").reshape(BLOCK_TOKENS, -1)
    wide = whole.astype(f32)
    squares = jnp.sum(wide * wide, axis=1)
    scaled = (wide * norm_gain.astype(f32)[None, :]).astype(bf16)
    k_panel = lax.dynamic_slice_in_dim(key_weight, group * HEAD_WIDTH, HEAD_WIDTH, 1)
    v_panel = lax.dynamic_slice_in_dim(value_weight, group * HEAD_WIDTH, HEAD_WIDTH, 1)
    panel = jnp.concatenate([w_query, k_panel, v_panel], axis=1)
    part = jnp.dot(scaled, panel, preferred_element_type=f32).astype(bf16)
    part = part.reshape(NEAR_SIZE, TOK_NEAR, HEADS_HERE + 2, HEAD_WIDTH)
    part = part.transpose(0, 2, 1, 3).reshape(NEAR_SIZE, -1, HEAD_WIDTH)
    sq = jnp.stack(split3(squares.reshape(NEAR_SIZE, TOK_NEAR)), axis=1)
    sq = jnp.pad(sq, ((0, 0), (0, 13), (0, HEAD_WIDTH - TOK_NEAR)))
    got = exchange(jnp.concatenate([part, sq], axis=1), NEAR)

    total = jnp.sum(got.astype(f32), axis=0)
    kv = total[Q_ROWS : Q_ROWS + 2 * TOK_NEAR].astype(bf16)
    kv = kv.reshape(2, FAR_SIZE, TOK_ROW, HEAD_WIDTH).transpose(1, 0, 2, 3)
    kv = kv.reshape(FAR_SIZE, 2 * TOK_ROW, HEAD_WIDTH)
    sq = jnp.sum(total[Q_ROWS + 2 * TOK_NEAR :], axis=0)
    sq = jnp.pad(jnp.stack(split3(sq)), ((0, 13), (0, 0)))
    q_part = jnp.broadcast_to(total[None, :Q_ROWS].astype(bf16), (FAR_SIZE, Q_ROWS, HEAD_WIDTH))
    sq = jnp.broadcast_to(sq[None], (FAR_SIZE,) + sq.shape)
    got = exchange(jnp.concatenate([q_part, kv, sq], axis=1), "zh")

    total = jnp.sum(got.astype(f32), axis=0)
    square_sum = jnp.sum(total[Q_ROWS + 2 * TOK_ROW :], axis=0)[:TOK_NEAR]
    inv = lax.rsqrt(square_sum / MODEL_WIDTH + epsilon)
    inv_row = lax.dynamic_slice_in_dim(inv, far * TOK_ROW, TOK_ROW)
    start = near * TOK_NEAR
    cos = lax.dynamic_slice_in_dim(jnp.asarray(COS_TABLE), start, TOK_NEAR)
    sin = lax.dynamic_slice_in_dim(jnp.asarray(SIN_TABLE), start, TOK_NEAR)
    cos_row = lax.dynamic_slice_in_dim(cos, far * TOK_ROW, TOK_ROW)
    sin_row = lax.dynamic_slice_in_dim(sin, far * TOK_ROW, TOK_ROW)
    q = total[:Q_ROWS].reshape(HEADS_HERE, TOK_NEAR, HEAD_WIDTH) * inv[None, :, None]
    q = rotate(q, cos[None], sin[None]).astype(bf16).reshape(Q_ROWS, HEAD_WIDTH)
    new_k = total[Q_ROWS : Q_ROWS + TOK_ROW] * inv_row[:, None]
    new_k = rotate(new_k, cos_row, sin_row).astype(bf16)
    new_v = (total[Q_ROWS + TOK_ROW : Q_ROWS + 2 * TOK_ROW] * inv_row[:, None]).astype(bf16)
    queries = spread(q, NEAR_SIZE, NEAR).reshape(NEAR_SIZE * Q_ROWS, HEAD_WIDTH)

    old_k = lax.dynamic_slice_in_dim(cached_keys, group * HEAD_WIDTH, HEAD_WIDTH, 1)
    old_v = lax.dynamic_slice_in_dim(cached_values, group * HEAD_WIDTH, HEAD_WIDTH, 1)
    keys = jnp.concatenate([old_k, new_k], axis=0)
    values = jnp.concatenate([old_v, new_v], axis=0)
    scores = lax.dot_general(queries, keys, (((1,), (1,)), ((), ())), preferred_element_type=f32)
    scores = scores * (1.0 / math.sqrt(HEAD_WIDTH))
    old = old_k.shape[0]
    row = jnp.arange(NEAR_SIZE * Q_ROWS, dtype=jnp.int32)
    token = row // Q_ROWS * TOK_NEAR + row % TOK_NEAR
    slot = jnp.arange(old + TOK_ROW, dtype=jnp.int32)
    new_token = start + far * TOK_ROW + slot - old
    seen = (slot[None, :] < old) | (new_token[None, :] <= token[:, None])
    scores = jnp.where(seen, scores, -jnp.inf)
    top = jnp.max(scores, axis=1, keepdims=True)
    weights = jnp.exp(scores - top)
    denom = jnp.sum(weights, axis=1)
    numer = jnp.dot(weights.astype(bf16), values, preferred_element_type=f32)
    out = (numer / denom[:, None]).astype(bf16).reshape(NEAR_SIZE, Q_ROWS, HEAD_WIDTH)
    lse = (top[:, 0] + jnp.log(denom)).reshape(NEAR_SIZE, 2, HEAD_WIDTH)
    lse = jnp.pad(jnp.concatenate(split3(lse), axis=1), ((0, 0), (0, 10), (0, 0)))
    got = exchange(jnp.concatenate([out, lse], axis=1), NEAR)

    mixed, lse = combine(got)
    lse = jnp.pad(jnp.concatenate(split3(lse), axis=0), ((0, 10), (0, 0)))
    got = spread(jnp.concatenate([mixed.astype(bf16), lse], axis=0), FAR_SIZE, "zh")
    got = got.reshape(FAR_SIZE, Q_ROWS + 16, HEAD_WIDTH)
    mixed, _ = combine(got)
    context = spread(mixed.astype(bf16), NEAR_SIZE, NEAR)
    context = context.reshape(NEAR_SIZE, HEADS_HERE, TOK_NEAR, HEAD_WIDTH)
    context = context.transpose(0, 2, 1, 3).reshape(BLOCK_TOKENS, HEADS_HERE * HEAD_WIDTH)
    part = jnp.dot(context, w_out, preferred_element_type=f32).astype(bf16)
    got = exchange(part.reshape(COLS, BLOCK_TOKENS // COLS, -1), "col")
    return jnp.sum(got.astype(f32), axis=0).astype(bf16)


def combine(got):
    count = got.shape[0]
    parts = got[:, Q_ROWS : Q_ROWS + 6].astype(f32).reshape(count, 3, 2, HEAD_WIDTH)
    lse = jnp.sum(parts, axis=1)
    top = jnp.max(lse, axis=0)
    share = jnp.exp(lse - top[None])
    total = jnp.sum(share, axis=0)
    ratio = (share / total[None]).reshape(count, Q_ROWS, 1)
    mixed = jnp.sum(got[:, :Q_ROWS].astype(f32) * ratio, axis=0)
    return mixed, top + jnp.log(total)


def solution(mesh):
    fine = Mesh(mesh.devices.reshape(2, 4, 4, COLS), ("ylo", "zh", "zl", "col"))
    row = ("ylo", "zh", "zl")
    placed = (
        P("col", row),
        P(row),
        P(row, "col"),
        P(row, None),
        P(row, None),
        P("col", row),
        P(row, None),
        P(row, None),
    )
    return jax.shard_map(
        body, mesh=fine, in_specs=placed, out_specs=P("col", row), check_vma=False
    )
```

time: 728 us -> 202 us (0.28)
  waiting for transfers between devices: 484 us -> 31.6 us
  blocking collectives: 181 us -> 102 us
  starting transfers between devices: 0.27 us -> 27.3 us
  between operations: 13.2 us -> 0.31 us
    psum x2 -> x0, waiting for transfers between devices: 381 us -> none  [the longest x1 206 us: body(): numer, denom = lax.psum((numer_part, denom_part), 'row')]
    psum x2 -> x0, blocking collectives: 105 us -> none  [the longest x1 56.9 us: body(): lax.psum((query_part, kv_part, square_part), 'row')]
    reduce_scatter x1 -> x0, waiting for transfers between devices: 103 us -> none  [body(): lax.psum_scatter(jnp.dot(context, w_out, preferred_element_type=jnp.float...]
    all_to_all x0 -> x5, blocking collectives: none -> 102 us  [exchange(): return lax.all_to_all(x, axes, 0, 0, tiled=True)]
    pmax x1 -> x0, blocking collectives: 49.9 us -> none  [body(): row_max = lax.pmax(local_max, 'row')]
    all_to_all x0 -> x3, waiting for transfers between devices: none -> 31.6 us  [exchange(): return lax.all_to_all(x, axes, 0, 0, tiled=True)]
    all_to_all x0 -> x3, starting transfers between devices: none -> 27.3 us  [exchange(): return lax.all_to_all(x, axes, 0, 0, tiled=True)]
    all_gather x1 -> x0, blocking collectives: 26.8 us -> none  [body(): whole = lax.all_gather(tokens, 'col', axis=0, tiled=True)]
  transfers between devices with their start and end apart: 3 -> 3, of which waited for: 3 -> 3; matrix products, arithmetic and copies ran while one was open for 2% -> 3% of each run, Pallas kernels for 0% -> 0%
where the time goes in v1:
time: 202 us; the launch traced here: 201 us
  blocking collectives  102 us (50%)
  waiting for transfers between devices  31.6 us (16%)
  starting transfers between devices  27.3 us (14%)
  matrix products  18.8 us (9%)
  other arithmetic  12.6 us (6%)
  local copies, waits for them, and re-layouts  8.25 us (4%)
    all_to_all x5, blocking collectives, exchange(): return lax.all_to_all(x, axes, 0, 0, tiled=True)  102 us
    all_to_all x3, waiting for transfers between devices, exchange(): return lax.all_to_all(x, axes, 0, 0, tiled=True)  31.6 us
    all_to_all x3, starting transfers between devices, exchange(): return lax.all_to_all(x, axes, 0, 0, tiled=True)  27.3 us
    dot_general x1, matrix products, body(): numer = jnp.dot(weights.astype(bf16), values, preferred_element_type=f32)  8.72 us
    dot_general x1, matrix products, body(): lax.dot_general(queries, keys, (((1,), (1,)), ((), ())), preferred_elemen...  8.5 us
    reduce_sum x1, other arithmetic, body(): denom = jnp.sum(weights, axis=1)  8.14 us
  transfers between devices with their start and end apart: 3, of which 3 were waited for; matrix products, arithmetic and copies ran while one was open for 3% of the time, Pallas kernels for 0%

profile of v1, /device:TPU:1, one launch (start us, length us, event | category | flops | bytes accessed | tf_op | source)
XLA Modules:
  0.0 200.6 jit_solution(15361119033437856181)
XLA Ops:
  0.0 0.0 copy-start
  0.0 1.5 broadcast_in_dim.15
  1.5 10.2 %all-to-all-start = ((bf16[16,32,256]{2,1,0:T(8,128)(2,1)}), bf16[16,32,256]{2,1,0:T(8,128)(2,1)S(1)}, u32[]{:S(2)}, u32[]{:S(2)}) async-start(bf16[16,32,256]{2,1,0:T(8,128)(2,1)} %broadcast_in_dim.15), calls=%async_computation | async-start | bytes 524288 | tf_op jit(solution)/shard_map/all_to_all | solution.py:64
  11.7 0.7 convert_element_type.155
  12.3 0.9 constant_dynamic-slice_fusion.4
  13.2 7.2 %all-to-all-done = bf16[16,32,256]{2,1,0:T(8,128)(2,1)S(1)} async-done(((bf16[16,32,256]{2,1,0:T(8,128)(2,1)}), bf16[16,32,256]{2,1,0:T(8,128)(2,1)S(1)}, u32[]{:S(2)}, u32[]{:S(2)}) %all-to-all-start) | async-done | bytes 262176 | tf_op jit(solution)/shard_map/all_to_all | solution.py:64
  20.5 1.3 convolution_convert_fusion
  21.8 0.9 reshape.256
  22.7 0.2 copy.30
  22.9 0.1 multiply_reduce_fusion.2
  23.0 0.1 reshape.258
  23.2 0.1 fusion.13
  23.2 24.4 %all_to_all.40 = bf16[8,400,128]{2,1,0:T(8,128)(2,1)S(1)} all-to-all(bf16[8,400,128]{2,1,0:T(8,128)(2,1)S(1)} %fusion.13), channel_id=1, replica_groups=mesh['ylo'=2,'zh'=4,'zl'=4,'col'=16] {'ylo','zl'}, dimensions={0} | all-to-all | bytes 1638400 | tf_op jit(solution)/shard_map/all_to_all | solution.py:64
  47.6 0.1 convert_reduce_fusion
  47.9 0.7 pad_maximum_fusion
  48.6 12.1 %all-to-all-start.2 = ((bf16[4,304,128]{2,1,0:T(8,128)(2,1)}), bf16[4,304,128]{2,1,0:T(8,128)(2,1)S(1)}, u32[]{:S(2)}, u32[]{:S(2)}) async-start(bf16[4,304,128]{2,1,0:T(8,128)(2,1)} %pad_maximum_fusion), calls=%async_computation.2 | async-start | bytes 622592 | tf_op jit(solution)/shard_map/all_to_all | solution.py:64
  60.7 0.8 constant_dynamic-slice_fusion.2
  61.5 17.2 %all-to-all-done.2 = bf16[4,304,128]{2,1,0:T(8,128)(2,1)S(1)} async-done(((bf16[4,304,128]{2,1,0:T(8,128)(2,1)}), bf16[4,304,128]{2,1,0:T(8,128)(2,1)S(1)}, u32[]{:S(2)}, u32[]{:S(2)}) %all-to-all-start.2) | async-done | bytes 311328 | tf_op jit(solution)/shard_map/all_to_all | solution.py:64
  78.8 0.1 broadcast_multiply_fusion
  78.8 0.1 fusion.65
  79.0 0.1 mul.134
  79.0 0.1 fusion.30
  79.2 0.9 broadcast_in_dim.18
  80.0 5.0 %all-to-all-start.3 = ((bf16[8,256,128]{2,1,0:T(8,128)(2,1)}), bf16[8,256,128]{2,1,0:T(8,128)(2,1)S(1)}, u32[]{:S(2)}, u32[]{:S(2)}) async-start(bf16[8,256,128]{2,1,0:T(8,128)(2,1)} %broadcast_in_dim.18), calls=%async_computation.3 | async-start | bytes 1048576 | tf_op jit(solution)/shard_map/all_to_all | solution.py:64
  85.0 1.1 constant_dynamic-slice_fusion.1
  86.1 1.1 constant_dynamic-slice_fusion
  87.2 0.1 dynamic_slice.36
  87.3 0.1 fusion.43
  87.4 0.1 fusion.66
  87.4 0.8 fusion.48
  88.2 7.2 %all-to-all-done.3 = bf16[8,256,128]{2,1,0:T(8,128)(2,1)S(1)} async-done(((bf16[8,256,128]{2,1,0:T(8,128)(2,1)}), bf16[8,256,128]{2,1,0:T(8,128)(2,1)S(1)}, u32[]{:S(2)}, u32[]{:S(2)}) %all-to-all-start.3) | async-done | bytes 524320 | tf_op jit(solution)/shard_map/all_to_all | solution.py:64
  95.4 8.5 %fusion.67 = (f32[2048]{0:T(1024)S(1)}, f32[2048,2064]{0,1:T(8,128)}) fusion(bf16[2048,128]{1,0:T(8,128)(2,1)S(1)} %bitcast.63, bf16[16,128]{1,0:T(8,128)(2,1)S(1)} %fusion.48, bf16[2048,128]{1,0:T(8,128)(2,1)S(1)} %constant_dynamic-slice_fusion.1, s32[2048]{0:T(1024)S(1)} %fusion.37, s32[2064]{0:T(1024)S(1)} %add_add_fusion, ...), kind=kOutput, calls=%fused_computation.126 | convolution fusion | flops 1104320512 | bytes 17987664 | tf_op jit(solution)/shard_map/dot_general | solution.py:120
  103.9 8.1 %fusion = f32[2048]{0:T(1024)S(1)} fusion(f32[2048,2064]{0,1:T(8,128)} %get-tuple-element.24, f32[2048]{0:T(1024)S(1)} %get-tuple-element.23), kind=kLoop, calls=%fused_computation.2 | loop fusion | flops 8452096 | bytes 16924672 | tf_op jit(solution)/shard_map/reduce_sum | solution.py:131
  112.1 8.7 %fusion.8 = bf16[2048,128]{1,0:T(8,128)(2,1)S(1)} fusion(f32[2048,2064]{0,1:T(8,128)} %get-tuple-element.24, f32[2048]{0:T(1024)S(1)} %get-tuple-element.23, bf16[16,128]{1,0:T(8,128)(2,1)S(1)} %get-tuple-element.5, bf16[2048,128]{1,0:T(8,128)(2,1)S(1)} %constant_dynamic-slice_fusion, f32[2048]{0:T(1024)S(1)} %fusion), kind=kOutput, calls=%fused_computation.7 | convolution fusion | flops 1092165632 | bytes 17977344 | tf_op jit(solution)/shard_map/dot_general | solution.py:132
  120.9 18.4 %all_to_all.41 = bf16[8,272,128]{2,1,0:T(8,128)(2,1)S(1)} all-to-all(bf16[8,272,128]{2,1,0:T(8,128)(2,1)S(1)} %fusion.14), channel_id=1, replica_groups=mesh['ylo'=2,'zh'=4,'zl'=4,'col'=16] {'ylo','zl'}, dimensions={0} | all-to-all | bytes 1114112 | tf_op jit(solution)/shard_map/all_to_all | solution.py:64
  139.3 0.3 multiply_reduce_fusion
  139.7 25.7 %all_to_all.42 = bf16[4,272,128]{2,1,0:T(8,128)(2,1)S(1)} all-to-all(bf16[4,272,128]{2,1,0:T(8,128)(2,1)S(1)} %broadcast_in_dim.20), channel_id=1, replica_groups=mesh['ylo'=2,'zh'=4,'zl'=4,'col'=16] {'zh'}, dimensions={0} | all-to-all | bytes 557056 | tf_op jit(solution)/shard_map/all_to_all | solution.py:64
  165.6 0.2 multiply_reduce_fusion.1
  165.8 0.1 broadcast_in_dim.21
  165.8 14.2 %all_to_all.43 = bf16[8,256,128]{2,1,0:T(8,128)(2,1)S(1)} all-to-all(bf16[8,256,128]{2,1,0:T(8,128)(2,1)S(1)} %broadcast_in_dim.21), channel_id=1, replica_groups=mesh['ylo'=2,'zh'=4,'zl'=4,'col'=16] {'ylo','zl'}, dimensions={0} | all-to-all | bytes 1048576 | tf_op jit(solution)/shard_map/all_to_all | solution.py:64
  180.0 0.4 copy.38
  180.4 0.0 copy-done
  180.4 0.3 convolution_convert_fusion.1
  180.8 19.2 %all_to_all.44 = bf16[16,32,256]{2,1,0:T(8,128)(2,1)S(1)} all-to-all(bf16[16,32,256]{2,1,0:T(8,128)(2,1)S(1)} %bitcast.69), channel_id=1, replica_groups=mesh['ylo'=2,'zh'=4,'zl'=4,'col'=16] {'col'}, dimensions={0} | all-to-all | bytes 524288 | tf_op jit(solution)/shard_map/all_to_all | solution.py:64
  200.0 0.6 reduce_sum.141
  (42 shorter events, 0.6 us)
Async XLA Ops:
  0.0 180.4 %copy-start = (bf16[512,256]{1,0:T(8,128)(2,1)S(1)}, bf16[512,256]{1,0:T(8,128)(2,1)}, u32[]{:S(2)}) copy-start(bf16[512,256]{1,0:T(8,128)(2,1)} %param.15) | copy-start | bytes 786436
  1.5 18.9 %all-to-all-start = ((bf16[16,32,256]{2,1,0:T(8,128)(2,1)}), bf16[16,32,256]{2,1,0:T(8,128)(2,1)S(1)}, u32[]{:S(2)}, u32[]{:S(2)}) async-start(bf16[16,32,256]{2,1,0:T(8,128)(2,1)} %broadcast_in_dim.15), calls=%async_computation | async-start | bytes 524288 | tf_op jit(solution)/shard_map/all_to_all | solution.py:64
  48.6 30.1 %all-to-all-start.2 = ((bf16[4,304,128]{2,1,0:T(8,128)(2,1)}), bf16[4,304,128]{2,1,0:T(8,128)(2,1)S(1)}, u32[]{:S(2)}, u32[]{:S(2)}) async-start(bf16[4,304,128]{2,1,0:T(8,128)(2,1)} %pad_maximum_fusion), calls=%async_computation.2 | async-start | bytes 622592 | tf_op jit(solution)/shard_map/all_to_all | solution.py:64
  80.0 15.4 %all-to-all-start.3 = ((bf16[8,256,128]{2,1,0:T(8,128)(2,1)}), bf16[8,256,128]{2,1,0:T(8,128)(2,1)S(1)}, u32[]{:S(2)}, u32[]{:S(2)}) async-start(bf16[8,256,128]{2,1,0:T(8,128)(2,1)} %broadcast_in_dim.18), calls=%async_computation.3 | async-start | bytes 1048576 | tf_op jit(solution)/shard_map/all_to_all | solution.py:64

commit v2 on v1

v2 whole, which is shorter than its diff:
```python
import math

import jax
import jax.numpy as jnp
import numpy as np
from jax import lax
from jax.experimental import pallas as pl
from jax.experimental.pallas import tpu as pltpu
from jax.sharding import Mesh, PartitionSpec as P

MODEL_WIDTH = 8192
QUERY_HEADS = 64
KEY_VALUE_HEADS = 8
HEAD_WIDTH = 128
BLOCK_TOKENS = 512
CACHED_COUNT = 65536

rope_base = 500000.0
epsilon = 1e-05

NEAR = ("ylo", "zl")
NEAR_SIZE = 8
FAR_SIZE = 4
COLS = 16
HEADS_HERE = QUERY_HEADS // COLS
TOK_NEAR = BLOCK_TOKENS // NEAR_SIZE
TOK_ROW = TOK_NEAR // FAR_SIZE
Q_ROWS = HEADS_HERE * TOK_NEAR

bf16 = jnp.bfloat16
f32 = jnp.float32


def rope_tables():
    half = HEAD_WIDTH // 2
    ladder = np.arange(half, dtype=np.float32) * np.float32(2.0 / HEAD_WIDTH)
    base = np.power(np.float32(rope_base), -ladder).astype(np.float32)
    wavelen = (np.float32(2.0 * math.pi) / base).astype(np.float32)
    smooth = ((np.float32(8192.0) / wavelen - 1) / 3).astype(np.float32)
    middle = ((1 - smooth) * base / 8 + smooth * base).astype(np.float32)
    freqs = np.where(wavelen < 2048, base, np.where(wavelen > 8192, base / 8, middle))
    pos = (CACHED_COUNT + np.arange(BLOCK_TOKENS)).astype(np.float32)
    angles = (pos[:, None] * freqs.astype(np.float32)[None, :]).astype(np.float32)
    cos = np.cos(angles.astype(np.float64)).astype(np.float32)
    sin = np.sin(angles.astype(np.float64)).astype(np.float32)
    return np.concatenate([cos, cos], 1), np.concatenate([-sin, sin], 1)


COS_TABLE, SIN_TABLE = rope_tables()


SCORE_SCALE = math.log2(math.e) / math.sqrt(HEAD_WIDTH)
LN2 = math.log(2.0)
PAD = 16


def exchange(x, axes):
    return lax.all_to_all(x, axes, 0, 0, tiled=True)


def spread(x, count, axes):
    return exchange(jnp.broadcast_to(x[None], (count,) + x.shape), axes)


def run(kernel, shapes, *args, scratch=(), scalars=()):
    spec = pl.BlockSpec(memory_space=pltpu.VMEM)
    smem = pl.BlockSpec(memory_space=pltpu.SMEM)
    return pl.pallas_call(
        kernel,
        out_shape=shapes,
        in_specs=[smem] * len(scalars) + [spec] * len(args),
        out_specs=jax.tree.map(lambda _: spec, shapes),
        scratch_shapes=scratch,
        compiler_params=pltpu.CompilerParams(vmem_limit_bytes=48 << 20),
    )(*scalars, *args)


def shape(*dims, dtype=bf16):
    return jax.ShapeDtypeStruct(dims, dtype)


def parts3(x):
    hi = x.astype(bf16)
    rest = x - hi.astype(f32)
    mid = rest.astype(bf16)
    low = (rest - mid.astype(f32)).astype(bf16)
    return hi.astype(f32), mid.astype(f32), low.astype(f32)


def pack_rows(rows):
    line = lax.broadcasted_iota(jnp.int32, (PAD, HEAD_WIDTH), 0)
    tile = jnp.zeros((PAD, HEAD_WIDTH), f32)
    for i, row in enumerate(rows):
        tile = jnp.where(line == i, jnp.broadcast_to(row, tile.shape), tile)
    return tile.astype(bf16)


def same(rows, cols, offset=0):
    a = lax.broadcasted_iota(jnp.int32, (rows, cols), 0)
    b = lax.broadcasted_iota(jnp.int32, (rows, cols), 1)
    return a + offset == b


def to_column(row, rows, offset=0):
    wide = jnp.broadcast_to(row, (rows, row.shape[1]))
    return jnp.sum(jnp.where(same(rows, row.shape[1], offset), wide, 0.0), axis=1, keepdims=True)


def to_row(column):
    n = column.shape[0]
    wide = jnp.broadcast_to(column, (n, n))
    return jnp.sum(jnp.where(same(n, n), wide, 0.0), axis=0, keepdims=True)


def project_kernel(tok_ref, gain_ref, w_ref, k_ref, v_ref, out_ref):
    scaled = (tok_ref[...].astype(f32) * gain_ref[...].astype(f32)).astype(bf16)
    pairs = [w_ref[:, 256 * i : 256 * (i + 1)] for i in range(HEADS_HERE // 2)]
    pairs.append(jnp.concatenate([k_ref[...], v_ref[...]], axis=1))
    for i, panel in enumerate(pairs):
        part = jnp.dot(scaled, panel, preferred_element_type=f32).astype(bf16)
        for j in range(2):
            head = part[:, HEAD_WIDTH * j : HEAD_WIDTH * (j + 1)]
            row = (2 * i + j) * TOK_NEAR
            for n in range(NEAR_SIZE):
                out_ref[n, row : row + TOK_NEAR, :] = head[n * TOK_NEAR : (n + 1) * TOK_NEAR]
    row = (HEADS_HERE + 2) * TOK_NEAR
    for n in range(NEAR_SIZE // 2):
        x = tok_ref[n * 128 : (n + 1) * 128, :]
        gram = lax.dot_general(x, x, (((1,), (1,)), ((), ())), preferred_element_type=f32)
        sums = jnp.sum(jnp.where(same(128, 128), gram, 0.0), axis=0, keepdims=True)
        tile = pack_rows(parts3(sums))
        out_ref[2 * n, row : row + PAD, :] = tile
        out_ref[2 * n + 1, row : row + PAD, :] = jnp.concatenate([tile[:, 64:], tile[:, :64]], axis=1)


def reduce_kernel(got_ref, out_ref):
    total = got_ref[0].astype(f32)
    for n in range(1, NEAR_SIZE):
        total = total + got_ref[n].astype(f32)
    low = total.astype(bf16)
    k_row, v_row, s_row = Q_ROWS, Q_ROWS + TOK_NEAR, Q_ROWS + 2 * TOK_NEAR
    sums = total[s_row : s_row + 1] + total[s_row + 1 : s_row + 2] + total[s_row + 2 : s_row + 3]
    tile = pack_rows(parts3(sums))
    for f in range(FAR_SIZE):
        out_ref[f, :Q_ROWS, :] = low[:Q_ROWS]
        out_ref[f, Q_ROWS : Q_ROWS + 16, :] = low[k_row + 16 * f : k_row + 16 * (f + 1)]
        out_ref[f, Q_ROWS + 16 : Q_ROWS + 32, :] = low[v_row + 16 * f : v_row + 16 * (f + 1)]
        out_ref[f, Q_ROWS + 32 : Q_ROWS + 48, :] = tile


def rope_kernel(far_ref, got_ref, cos_ref, sin_ref, cosn_ref, sinn_ref, q_ref, k_ref, v_ref):
    total = got_ref[0].astype(f32)
    for n in range(1, FAR_SIZE):
        total = total + got_ref[n].astype(f32)
    row = Q_ROWS + 2 * TOK_ROW
    sums = total[row : row + 1] + total[row + 1 : row + 2] + total[row + 2 : row + 3]
    inv = lax.rsqrt(sums / MODEL_WIDTH + epsilon)
    inv_q = to_column(inv, TOK_NEAR)
    inv_n = to_column(inv, TOK_ROW, far_ref[0] * TOK_ROW)
    cos, sin = cos_ref[...], sin_ref[...]
    for h in range(HEADS_HERE):
        u = total[h * TOK_NEAR : (h + 1) * TOK_NEAR] * inv_q
        u = (u * cos + pltpu.roll(u, HEAD_WIDTH // 2, 1) * sin).astype(bf16)
        for n in range(NEAR_SIZE):
            q_ref[n, h * TOK_NEAR : (h + 1) * TOK_NEAR, :] = u
    u = total[Q_ROWS : Q_ROWS + TOK_ROW] * inv_n
    k_ref[...] = (u * cosn_ref[...] + pltpu.roll(u, HEAD_WIDTH // 2, 1) * sinn_ref[...]).astype(bf16)
    v_ref[...] = (total[Q_ROWS + TOK_ROW : Q_ROWS + 2 * TOK_ROW] * inv_n).astype(bf16)


def attend_kernel(first_ref, q_ref, k_ref, v_ref, nk_ref, nv_ref, out_ref):
    contract = (((1,), (1,)), ((), ()))
    zeros = jnp.zeros((HEAD_WIDTH - TOK_ROW, HEAD_WIDTH), bf16)
    new_k = jnp.concatenate([nk_ref[...], zeros], axis=0)
    new_v = jnp.concatenate([nv_ref[...], zeros], axis=0)
    slot = lax.broadcasted_iota(jnp.int32, (Q_ROWS, HEAD_WIDTH), 1)
    line = lax.broadcasted_iota(jnp.int32, (Q_ROWS, HEAD_WIDTH), 0)
    new_token = jnp.where(slot < TOK_ROW, first_ref[0] + slot, BLOCK_TOKENS)

    def block(n, carry):
        q = q_ref[n]
        s = lax.dot_general(q, k_ref[...], contract, preferred_element_type=f32)
        fresh = lax.dot_general(q, new_k, contract, preferred_element_type=f32)
        token = n * TOK_NEAR + lax.rem(line, TOK_NEAR)
        fresh = jnp.where(new_token <= token, fresh, -jnp.inf)
        top = jnp.maximum(
            jnp.max(s, axis=1, keepdims=True), jnp.max(fresh, axis=1, keepdims=True)
        )
        base = top * SCORE_SCALE
        w = jnp.exp2(s * SCORE_SCALE - base)
        w_new = jnp.exp2(fresh * SCORE_SCALE - base)
        denom = jnp.sum(w, axis=1, keepdims=True) + jnp.sum(w_new, axis=1, keepdims=True)
        numer = jnp.dot(w.astype(bf16), v_ref[...], preferred_element_type=f32)
        numer = numer + jnp.dot(w_new.astype(bf16), new_v, preferred_element_type=f32)
        out_ref[n, :Q_ROWS, :] = (numer / denom).astype(bf16)
        lse = base * LN2 + jnp.log(denom)
        lo = parts3(to_row(lse[:HEAD_WIDTH]))
        hi = parts3(to_row(lse[HEAD_WIDTH:]))
        out_ref[n, Q_ROWS:, :] = pack_rows([x for pair in zip(lo, hi) for x in pair])
        return carry

    lax.fori_loop(0, NEAR_SIZE, block, 0)


def mix(got_ref, count):
    lse = []
    for n in range(count):
        t = got_ref[n, Q_ROWS:, :].astype(f32)
        lse.append(t[0:2] + t[2:4] + t[4:6])
    top = lse[0]
    for n in range(1, count):
        top = jnp.maximum(top, lse[n])
    share = [jnp.exp(x - top) for x in lse]
    total = sum(share[1:], share[0])
    halves = []
    for j in range(2):
        rows = slice(HEAD_WIDTH * j, HEAD_WIDTH * (j + 1))
        acc = jnp.zeros((HEAD_WIDTH, HEAD_WIDTH), f32)
        for n in range(count):
            ratio = to_column(share[n][j : j + 1] / total[j : j + 1], HEAD_WIDTH)
            acc = acc + got_ref[n, rows, :].astype(f32) * ratio
        halves.append(acc.astype(bf16))
    return halves, top + jnp.log(total)


def mix_near_kernel(got_ref, out_ref):
    halves, lse = mix(got_ref, NEAR_SIZE)
    parts = parts3(lse)
    tile = pack_rows([p[j : j + 1] for p in parts for j in range(2)])
    for f in range(FAR_SIZE):
        out_ref[f, :HEAD_WIDTH, :] = halves[0]
        out_ref[f, HEAD_WIDTH:Q_ROWS, :] = halves[1]
        out_ref[f, Q_ROWS:, :] = tile


def mix_far_kernel(got_ref, out_ref):
    halves, _ = mix(got_ref, FAR_SIZE)
    for n in range(NEAR_SIZE):
        out_ref[n, :HEAD_WIDTH, :] = halves[0]
        out_ref[n, HEAD_WIDTH:Q_ROWS, :] = halves[1]


def output_kernel(got_ref, w_ref, out_ref, ctx_ref):
    for n in range(NEAR_SIZE):
        for h in range(HEADS_HERE):
            block = got_ref[n, h * TOK_NEAR : (h + 1) * TOK_NEAR, :]
            ctx_ref[n * TOK_NEAR : (n + 1) * TOK_NEAR, h * HEAD_WIDTH : (h + 1) * HEAD_WIDTH] = block
    part = jnp.dot(ctx_ref[...], w_ref[...], preferred_element_type=f32).astype(bf16)
    rows = BLOCK_TOKENS // COLS
    for c in range(COLS):
        out_ref[c] = part[c * rows : (c + 1) * rows]


def body(tokens, norm_gain, w_query, key_weight, value_weight, w_out, cached_keys, cached_values):
    near = lax.axis_index("ylo") * 4 + lax.axis_index("zl")
    far = lax.axis_index("zh")
    group = lax.axis_index("col") // 2

    def panel(x):
        return lax.dynamic_slice_in_dim(x, group * HEAD_WIDTH, HEAD_WIDTH, 1)

    whole = spread(tokens, COLS, "col").reshape(BLOCK_TOKENS, -1)
    pay = run(
        project_kernel,
        shape(NEAR_SIZE, Q_ROWS + 2 * TOK_NEAR + PAD, HEAD_WIDTH),
        whole, norm_gain[None], w_query, panel(key_weight), panel(value_weight),
    )
    got = exchange(pay, NEAR)
    pay = run(reduce_kernel, shape(FAR_SIZE, Q_ROWS + 2 * TOK_ROW + PAD, HEAD_WIDTH), got)
    got = exchange(pay, "zh")

    start = near * TOK_NEAR
    first = start + far * TOK_ROW
    cos, sin = jnp.asarray(COS_TABLE), jnp.asarray(SIN_TABLE)
    pay, new_k, new_v = run(
        rope_kernel,
        (shape(NEAR_SIZE, Q_ROWS, HEAD_WIDTH), shape(TOK_ROW, HEAD_WIDTH), shape(TOK_ROW, HEAD_WIDTH)),
        got,
        lax.dynamic_slice_in_dim(cos, start, TOK_NEAR),
        lax.dynamic_slice_in_dim(sin, start, TOK_NEAR),
        lax.dynamic_slice_in_dim(cos, first, TOK_ROW),
        lax.dynamic_slice_in_dim(sin, first, TOK_ROW),
        scalars=(far.reshape(1).astype(jnp.int32),),
    )
    queries = exchange(pay, NEAR)
    pay = run(
        attend_kernel,
        shape(NEAR_SIZE, Q_ROWS + PAD, HEAD_WIDTH),
        queries, panel(cached_keys), panel(cached_values), new_k, new_v,
        scalars=(first.reshape(1).astype(jnp.int32),),
    )
    got = exchange(pay, NEAR)
    got = exchange(run(mix_near_kernel, shape(FAR_SIZE, Q_ROWS + PAD, HEAD_WIDTH), got), "zh")
    got = exchange(run(mix_far_kernel, shape(NEAR_SIZE, Q_ROWS, HEAD_WIDTH), got), NEAR)
    width = w_out.shape[1]
    pay = run(
        output_kernel,
        shape(COLS, BLOCK_TOKENS // COLS, width),
        got, w_out,
        scratch=[pltpu.VMEM((BLOCK_TOKENS, HEADS_HERE * HEAD_WIDTH), bf16)],
    )
    got = exchange(pay, "col")
    return jnp.sum(got.astype(f32), axis=0).astype(bf16)


def solution(mesh):
    fine = Mesh(mesh.devices.reshape(2, 4, 4, COLS), ("ylo", "zh", "zl", "col"))
    row = ("ylo", "zh", "zl")
    placed = (
        P("col", row),
        P(row),
        P(row, "col"),
        P(row, None),
        P(row, None),
        P("col", row),
        P(row, None),
        P(row, None),
    )
    return jax.shard_map(
        body, mesh=fine, in_specs=placed, out_specs=P("col", row), check_vma=False
    )
```

time: 202 us -> 183 us (0.906)
  matrix products: 18.8 us -> 0 us
  Pallas kernels: 0 us -> 12.8 us
  other arithmetic: 12.6 us -> 0.65 us
    dot_general x4 -> x0, matrix products: 18.8 us -> none  [the longest x1 8.72 us: body(): numer = jnp.dot(weights.astype(bf16), values, preferred_element_type=f32)]
    pallas_call x0 -> x7, Pallas kernels: none -> 12.8 us  [run(): pl.pallas_call(kernel, out_shape=shapes, in_specs=[smem] * len(scalars) +...]
    reduce_sum x12 -> x0, other arithmetic: 9.08 us -> none  [the longest x1 8.14 us: body(): denom = jnp.sum(weights, axis=1)]
  transfers between devices with their start and end apart: 3 -> 3, of which waited for: 3 -> 3; matrix products, arithmetic and copies ran while one was open for 3% -> 2% of each run, Pallas kernels for 0% -> 0%
where the time goes in v2:
time: 183 us; the launch traced here: 182 us
  blocking collectives  102 us (56%)
  waiting for transfers between devices  32.8 us (18%)
  starting transfers between devices  27.3 us (15%)
  Pallas kernels  12.8 us (7%)
  local copies, waits for them, and re-layouts  6.78 us (4%)
    all_to_all x5, blocking collectives, exchange(): return lax.all_to_all(x, axes, 0, 0, tiled=True)  102 us
    all_to_all x3, waiting for transfers between devices, exchange(): return lax.all_to_all(x, axes, 0, 0, tiled=True)  32.8 us
    all_to_all x3, starting transfers between devices, exchange(): return lax.all_to_all(x, axes, 0, 0, tiled=True)  27.3 us
    pallas_call x7, Pallas kernels, run(): pl.pallas_call(kernel, out_shape=shapes, in_specs=[smem] * len(scalars) +...  12.8 us
  transfers between devices with their start and end apart: 3, of which 3 were waited for; matrix products, arithmetic and copies ran while one was open for 2% of the time, Pallas kernels for 0%

profile of v2, /device:TPU:1, one launch (start us, length us, event | category | flops | bytes accessed | tf_op | source)
XLA Modules:
  0.0 182.1 jit_solution(3044566647772605699)
XLA Ops:
  0.0 1.5 broadcast_in_dim.4
  1.5 10.2 %all-to-all-start = ((bf16[16,32,256]{2,1,0:T(8,128)(2,1)}), bf16[16,32,256]{2,1,0:T(8,128)(2,1)S(1)}, u32[]{:S(2)}, u32[]{:S(2)}) async-start(bf16[16,32,256]{2,1,0:T(8,128)(2,1)} %broadcast_in_dim.4), calls=%async_computation | async-start | bytes 524288 | tf_op jit(solution)/shard_map/all_to_all | solution.py:58
  11.7 0.7 broadcast_in_dim.10.gain_ref
  12.3 0.9 constant_dynamic-slice_fusion.6
  13.2 7.2 %all-to-all-done = bf16[16,32,256]{2,1,0:T(8,128)(2,1)S(1)} async-done(((bf16[16,32,256]{2,1,0:T(8,128)(2,1)}), bf16[16,32,256]{2,1,0:T(8,128)(2,1)S(1)}, u32[]{:S(2)}, u32[]{:S(2)}) %all-to-all-start) | async-done | bytes 262176 | tf_op jit(solution)/shard_map/all_to_all | solution.py:58
  20.4 0.0 copy-start
  20.4 0.9 copy-done
  21.4 0.5 shard_map.100
  21.9 24.4 %all_to_all.40.got_ref = bf16[8,400,128]{2,1,0:T(8,128)(2,1)S(1)} all-to-all(bf16[8,400,128]{2,1,0:T(8,128)(2,1)S(1)} %shard_map.100), channel_id=1, replica_groups=mesh['ylo'=2,'zh'=4,'zl'=4,'col'=16] {'ylo','zl'}, dimensions={0} | all-to-all | bytes 1638400 | tf_op jit(solution)/shard_map/all_to_all | solution.py:58
  46.2 0.8 shard_map.101
  47.1 12.1 %all-to-all-start.2 = ((bf16[4,304,128]{2,1,0:T(8,128)(2,1)}), bf16[4,304,128]{2,1,0:T(8,128)(2,1)S(1)}, u32[]{:S(2)}, u32[]{:S(2)}) async-start(bf16[4,304,128]{2,1,0:T(8,128)(2,1)} %shard_map.101), calls=%async_computation.2 | async-start | bytes 622592 | tf_op jit(solution)/shard_map/all_to_all | solution.py:58
  59.2 0.7 constant_dynamic-slice_fusion.2
  59.9 0.8 constant_dynamic-slice_fusion.4
  60.7 16.5 %all-to-all-done.2.got_ref = bf16[4,304,128]{2,1,0:T(8,128)(2,1)S(1)} async-done(((bf16[4,304,128]{2,1,0:T(8,128)(2,1)}), bf16[4,304,128]{2,1,0:T(8,128)(2,1)S(1)}, u32[]{:S(2)}, u32[]{:S(2)}) %all-to-all-start.2) | async-done | bytes 311328 | tf_op jit(solution)/shard_map/all_to_all | solution.py:58
  77.1 1.0 shard_map.102
  78.1 5.0 %all-to-all-start.3 = ((bf16[8,256,128]{2,1,0:T(8,128)(2,1)}), bf16[8,256,128]{2,1,0:T(8,128)(2,1)S(1)}, u32[]{:S(2)}, u32[]{:S(2)}) async-start(bf16[8,256,128]{2,1,0:T(8,128)(2,1)} %get-tuple-element.8), calls=%async_computation.3 | async-start | bytes 1048576 | tf_op jit(solution)/shard_map/all_to_all | solution.py:58
  83.1 0.0 copy-start.1
  83.1 1.3 constant_dynamic-slice_fusion
  84.4 9.1 %all-to-all-done.3.q_ref = bf16[8,256,128]{2,1,0:T(8,128)(2,1)S(1)} async-done(((bf16[8,256,128]{2,1,0:T(8,128)(2,1)}), bf16[8,256,128]{2,1,0:T(8,128)(2,1)S(1)}, u32[]{:S(2)}, u32[]{:S(2)}) %all-to-all-start.3) | async-done | bytes 524320 | tf_op jit(solution)/shard_map/all_to_all | solution.py:58
  93.5 9.5 %shard_map.103 = bf16[8,272,128]{2,1,0:T(8,128)(2,1)S(1)} custom-call(s32[1]{0:T(128)} %bitcast.first_ref, bf16[8,256,128]{2,1,0:T(8,128)(2,1)S(1)} %all-to-all-done.3.q_ref, bf16[2048,128]{1,0:T(8,128)(2,1)S(1)} %get-tuple-element.12.k_ref, bf16[2048,128]{1,0:T(8,128)(2,1)S(1)} %get-tuple-element.11.v_ref, bf16[16,128]{1,0:T(8,128)(2,1)S(1)} %get-tuple-element.9.nk_ref, ...), custom_call_target="tpu_custom_call" | custom-call | tf_op jit(solution)/shard_map/pallas_call | solution.py:68
  103.0 18.4 %all_to_all.41.got_ref = bf16[8,272,128]{2,1,0:T(8,128)(2,1)S(1)} all-to-all(bf16[8,272,128]{2,1,0:T(8,128)(2,1)S(1)} %shard_map.103), channel_id=1, replica_groups=mesh['ylo'=2,'zh'=4,'zl'=4,'col'=16] {'ylo','zl'}, dimensions={0} | all-to-all | bytes 1114112 | tf_op jit(solution)/shard_map/all_to_all | solution.py:58
  121.4 0.4 shard_map.104
  121.8 25.7 %all_to_all.42.got_ref = bf16[4,272,128]{2,1,0:T(8,128)(2,1)S(1)} all-to-all(bf16[4,272,128]{2,1,0:T(8,128)(2,1)S(1)} %shard_map.104), channel_id=1, replica_groups=mesh['ylo'=2,'zh'=4,'zl'=4,'col'=16] {'zh'}, dimensions={0} | all-to-all | bytes 557056 | tf_op jit(solution)/shard_map/all_to_all | solution.py:58
  147.5 0.2 shard_map.105
  147.7 14.2 %all_to_all.43.got_ref = bf16[8,256,128]{2,1,0:T(8,128)(2,1)S(1)} all-to-all(bf16[8,256,128]{2,1,0:T(8,128)(2,1)S(1)} %shard_map.105), channel_id=1, replica_groups=mesh['ylo'=2,'zh'=4,'zl'=4,'col'=16] {'ylo','zl'}, dimensions={0} | all-to-all | bytes 1048576 | tf_op jit(solution)/shard_map/all_to_all | solution.py:58
  161.9 0.0 copy-done.1
  161.9 0.3 shard_map.106
  162.2 19.2 %all_to_all.44 = bf16[16,32,256]{2,1,0:T(8,128)(2,1)S(1)} all-to-all(bf16[16,32,256]{2,1,0:T(8,128)(2,1)S(1)} %shard_map.106), channel_id=1, replica_groups=mesh['ylo'=2,'zh'=4,'zl'=4,'col'=16] {'col'}, dimensions={0} | all-to-all | bytes 524288 | tf_op jit(solution)/shard_map/all_to_all | solution.py:58
  181.4 0.6 reduce_sum.12
Async XLA Ops:
  1.5 18.9 %all-to-all-start = ((bf16[16,32,256]{2,1,0:T(8,128)(2,1)}), bf16[16,32,256]{2,1,0:T(8,128)(2,1)S(1)}, u32[]{:S(2)}, u32[]{:S(2)}) async-start(bf16[16,32,256]{2,1,0:T(8,128)(2,1)} %broadcast_in_dim.4), calls=%async_computation | async-start | bytes 524288 | tf_op jit(solution)/shard_map/all_to_all | solution.py:58
  20.4 1.0 copy-start
  47.1 30.1 %all-to-all-start.2 = ((bf16[4,304,128]{2,1,0:T(8,128)(2,1)}), bf16[4,304,128]{2,1,0:T(8,128)(2,1)S(1)}, u32[]{:S(2)}, u32[]{:S(2)}) async-start(bf16[4,304,128]{2,1,0:T(8,128)(2,1)} %shard_map.101), calls=%async_computation.2 | async-start | bytes 622592 | tf_op jit(solution)/shard_map/all_to_all | solution.py:58
  78.1 15.4 %all-to-all-start.3 = ((bf16[8,256,128]{2,1,0:T(8,128)(2,1)}), bf16[8,256,128]{2,1,0:T(8,128)(2,1)S(1)}, u32[]{:S(2)}, u32[]{:S(2)}) async-start(bf16[8,256,128]{2,1,0:T(8,128)(2,1)} %get-tuple-element.8), calls=%async_computation.3 | async-start | bytes 1048576 | tf_op jit(solution)/shard_map/all_to_all | solution.py:58
  83.1 78.8 %copy-start.1 = (bf16[512,256]{1,0:T(8,128)(2,1)S(1)}, bf16[512,256]{1,0:T(8,128)(2,1)}, u32[]{:S(2)}) copy-start(bf16[512,256]{1,0:T(8,128)(2,1)} %w_ref.3) | copy-start | bytes 786436

commit v3 on v2

--- a/solution.py
+++ b/solution.py
@@ -18,11 +18,12 @@
 rope_base = 500000.0
 epsilon = 1e-05
 
-NEAR = ("ylo", "zl")
-NEAR_SIZE = 8
+NEAR_SIZE = 4
 FAR_SIZE = 4
 COLS = 16
-HEADS_HERE = QUERY_HEADS // COLS
+PAIR = 2
+HEADS_HERE = QUERY_HEADS // COLS // PAIR
+HEAD_COLS = HEADS_HERE * HEAD_WIDTH
 TOK_NEAR = BLOCK_TOKENS // NEAR_SIZE
 TOK_ROW = TOK_NEAR // FAR_SIZE
 Q_ROWS = HEADS_HERE * TOK_NEAR
@@ -52,6 +53,7 @@
 SCORE_SCALE = math.log2(math.e) / math.sqrt(HEAD_WIDTH)
 LN2 = math.log(2.0)
 PAD = 16
+PANEL = HEAD_PANEL = 256
 
 
 def exchange(x, axes):
@@ -112,25 +114,32 @@
     return jnp.sum(jnp.where(same(n, n), wide, 0.0), axis=0, keepdims=True)
 
 
-def project_kernel(tok_ref, gain_ref, w_ref, k_ref, v_ref, out_ref):
-    scaled = (tok_ref[...].astype(f32) * gain_ref[...].astype(f32)).astype(bf16)
-    pairs = [w_ref[:, 256 * i : 256 * (i + 1)] for i in range(HEADS_HERE // 2)]
-    pairs.append(jnp.concatenate([k_ref[...], v_ref[...]], axis=1))
-    for i, panel in enumerate(pairs):
-        part = jnp.dot(scaled, panel, preferred_element_type=f32).astype(bf16)
+def project_kernel(pair_ref, tok_ref, gain_ref, w_ref, k_ref, v_ref, far_ref, out_ref):
+    mine = pair_ref[0]
+    gains = [gain_ref[...], far_ref[HEAD_PANEL : HEAD_PANEL + 1, :PANEL]]
+    toks = [tok_ref[mine], tok_ref[1 - mine]]
+    scaled = [(t.astype(f32) * g.astype(f32)).astype(bf16) for t, g in zip(toks, gains)]
+    panels = [w_ref[:, pl.ds(pl.multiple_of(mine * HEAD_COLS, HEAD_COLS), HEAD_COLS)]]
+    panels.append(jnp.concatenate([k_ref[...], v_ref[...]], axis=1))
+    for i, panel in enumerate(panels):
+        other = far_ref[:HEAD_PANEL, HEAD_COLS * i : HEAD_COLS * (i + 1)]
+        part = jnp.dot(scaled[0], panel, preferred_element_type=f32)
+        part = (part + jnp.dot(scaled[1], other, preferred_element_type=f32)).astype(bf16)
         for j in range(2):
             head = part[:, HEAD_WIDTH * j : HEAD_WIDTH * (j + 1)]
             row = (2 * i + j) * TOK_NEAR
             for n in range(NEAR_SIZE):
                 out_ref[n, row : row + TOK_NEAR, :] = head[n * TOK_NEAR : (n + 1) * TOK_NEAR]
     row = (HEADS_HERE + 2) * TOK_NEAR
-    for n in range(NEAR_SIZE // 2):
-        x = tok_ref[n * 128 : (n + 1) * 128, :]
-        gram = lax.dot_general(x, x, (((1,), (1,)), ((), ())), preferred_element_type=f32)
-        sums = jnp.sum(jnp.where(same(128, 128), gram, 0.0), axis=0, keepdims=True)
-        tile = pack_rows(parts3(sums))
-        out_ref[2 * n, row : row + PAD, :] = tile
-        out_ref[2 * n + 1, row : row + PAD, :] = jnp.concatenate([tile[:, 64:], tile[:, :64]], axis=1)
+    contract = (((1,), (1,)), ((), ()))
+    for n in range(NEAR_SIZE):
+        sums = jnp.zeros((1, TOK_NEAR), f32)
+        for t in toks:
+            x = t[n * TOK_NEAR : (n + 1) * TOK_NEAR]
+            gram = lax.dot_general(x, x, contract, preferred_element_type=f32)
+            gram = jnp.where(same(TOK_NEAR, TOK_NEAR), gram, 0.0)
+            sums = sums + jnp.sum(gram, axis=0, keepdims=True)
+        out_ref[n, row : row + PAD, :] = pack_rows(parts3(sums))
 
 
 def reduce_kernel(got_ref, out_ref):
@@ -141,11 +150,12 @@
     k_row, v_row, s_row = Q_ROWS, Q_ROWS + TOK_NEAR, Q_ROWS + 2 * TOK_NEAR
     sums = total[s_row : s_row + 1] + total[s_row + 1 : s_row + 2] + total[s_row + 2 : s_row + 3]
     tile = pack_rows(parts3(sums))
+    own, end = TOK_ROW, 2 * TOK_ROW
     for f in range(FAR_SIZE):
         out_ref[f, :Q_ROWS, :] = low[:Q_ROWS]
-        out_ref[f, Q_ROWS : Q_ROWS + 16, :] = low[k_row + 16 * f : k_row + 16 * (f + 1)]
-        out_ref[f, Q_ROWS + 16 : Q_ROWS + 32, :] = low[v_row + 16 * f : v_row + 16 * (f + 1)]
-        out_ref[f, Q_ROWS + 32 : Q_ROWS + 48, :] = tile
+        out_ref[f, Q_ROWS : Q_ROWS + own, :] = low[k_row + own * f : k_row + own * (f + 1)]
+        out_ref[f, Q_ROWS + own : Q_ROWS + end, :] = low[v_row + own * f : v_row + own * (f + 1)]
+        out_ref[f, Q_ROWS + end : Q_ROWS + end + PAD, :] = tile
 
 
 def rope_kernel(far_ref, got_ref, cos_ref, sin_ref, cosn_ref, sinn_ref, q_ref, k_ref, v_ref):
@@ -168,7 +178,7 @@
     v_ref[...] = (total[Q_ROWS + TOK_ROW : Q_ROWS + 2 * TOK_ROW] * inv_n).astype(bf16)
 
 
-def attend_kernel(first_ref, q_ref, k_ref, v_ref, nk_ref, nv_ref, out_ref):
+def attend_kernel(first_ref, q_ref, kv_ref, other_ref, nk_ref, nv_ref, out_ref):
     contract = (((1,), (1,)), ((), ()))
     zeros = jnp.zeros((HEAD_WIDTH - TOK_ROW, HEAD_WIDTH), bf16)
     new_k = jnp.concatenate([nk_ref[...], zeros], axis=0)
@@ -179,19 +189,22 @@
 
     def block(n, carry):
         q = q_ref[n]
-        s = lax.dot_general(q, k_ref[...], contract, preferred_element_type=f32)
+        s = [
+            lax.dot_general(q, kv_ref[0], contract, preferred_element_type=f32),
+            lax.dot_general(q, other_ref[0], contract, preferred_element_type=f32),
+        ]
         fresh = lax.dot_general(q, new_k, contract, preferred_element_type=f32)
         token = n * TOK_NEAR + lax.rem(line, TOK_NEAR)
-        fresh = jnp.where(new_token <= token, fresh, -jnp.inf)
-        top = jnp.maximum(
-            jnp.max(s, axis=1, keepdims=True), jnp.max(fresh, axis=1, keepdims=True)
-        )
+        s.append(jnp.where(new_token <= token, fresh, -jnp.inf))
+        tops = [jnp.max(x, axis=1, keepdims=True) for x in s]
+        top = jnp.maximum(jnp.maximum(tops[0], tops[1]), tops[2])
         base = top * SCORE_SCALE
-        w = jnp.exp2(s * SCORE_SCALE - base)
-        w_new = jnp.exp2(fresh * SCORE_SCALE - base)
-        denom = jnp.sum(w, axis=1, keepdims=True) + jnp.sum(w_new, axis=1, keepdims=True)
-        numer = jnp.dot(w.astype(bf16), v_ref[...], preferred_element_type=f32)
-        numer = numer + jnp.dot(w_new.astype(bf16), new_v, preferred_element_type=f32)
+        denom = jnp.zeros_like(base)
+        numer = jnp.zeros((Q_ROWS, HEAD_WIDTH), f32)
+        for x, v in zip(s, (kv_ref[1], other_ref[1], new_v)):
+            w = jnp.exp2(x * SCORE_SCALE - base)
+            denom = denom + jnp.sum(w, axis=1, keepdims=True)
+            numer = numer + jnp.dot(w.astype(bf16), v, preferred_element_type=f32)
         out_ref[n, :Q_ROWS, :] = (numer / denom).astype(bf16)
         lse = base * LN2 + jnp.log(denom)
         lo = parts3(to_row(lse[:HEAD_WIDTH]))
@@ -240,32 +253,51 @@
         out_ref[n, HEAD_WIDTH:Q_ROWS, :] = halves[1]
 
 
-def output_kernel(got_ref, w_ref, out_ref, ctx_ref):
+def output_kernel(pair_ref, got_ref, w_ref, other_ref, out_ref, ctx_ref):
+    mine = pair_ref[0]
     for n in range(NEAR_SIZE):
         for h in range(HEADS_HERE):
             block = got_ref[n, h * TOK_NEAR : (h + 1) * TOK_NEAR, :]
             ctx_ref[n * TOK_NEAR : (n + 1) * TOK_NEAR, h * HEAD_WIDTH : (h + 1) * HEAD_WIDTH] = block
-    part = jnp.dot(ctx_ref[...], w_ref[...], preferred_element_type=f32).astype(bf16)
+    own = w_ref[pl.ds(pl.multiple_of(mine * HEAD_COLS, HEAD_COLS), HEAD_COLS), :]
     rows = BLOCK_TOKENS // COLS
-    for c in range(COLS):
-        out_ref[c] = part[c * rows : (c + 1) * rows]
+    for side, panel in ((mine, own), (1 - mine, other_ref[...])):
+        part = jnp.dot(ctx_ref[...], panel, preferred_element_type=f32).astype(bf16)
+        for c in range(COLS):
+            out_ref[side * COLS + c] = part[c * rows : (c + 1) * rows]
+
+
+def trade(x):
+    return lax.ppermute(x, "ylo", [(0, 1), (1, 0)])
 
 
 def body(tokens, norm_gain, w_query, key_weight, value_weight, w_out, cached_keys, cached_values):
-    near = lax.axis_index("ylo") * 4 + lax.axis_index("zl")
+    mine = lax.axis_index("ylo")
+    near = lax.axis_index("zl")
     far = lax.axis_index("zh")
     group = lax.axis_index("col") // 2
+    pair = mine.reshape(1).astype(jnp.int32)
 
     def panel(x):
         return lax.dynamic_slice_in_dim(x, group * HEAD_WIDTH, HEAD_WIDTH, 1)
 
-    whole = spread(tokens, COLS, "col").reshape(BLOCK_TOKENS, -1)
+    k_panel, v_panel = panel(key_weight), panel(value_weight)
+    w_far = lax.dynamic_slice_in_dim(w_query, (1 - mine) * HEAD_COLS, HEAD_COLS, 1)
+    w_far = jnp.concatenate([w_far, k_panel, v_panel], axis=1)
+    gain_row = jnp.pad(norm_gain[None], ((0, PAD - 1), (0, w_far.shape[1] - norm_gain.shape[0])))
+    w_far = trade(jnp.concatenate([w_far, gain_row], axis=0))
+    whole = spread(tokens, PAIR * COLS, ("ylo", "col")).reshape(PAIR, BLOCK_TOKENS, -1)
+    kv_own = jnp.stack([panel(cached_keys), panel(cached_values)])
+    kv_far = trade(kv_own)
+    o_far = trade(lax.dynamic_slice_in_dim(w_out, (1 - mine) * HEAD_COLS, HEAD_COLS, 0))
+
     pay = run(
         project_kernel,
         shape(NEAR_SIZE, Q_ROWS + 2 * TOK_NEAR + PAD, HEAD_WIDTH),
-        whole, norm_gain[None], w_query, panel(key_weight), panel(value_weight),
-    )
-    got = exchange(pay, NEAR)
+        whole, norm_gain[None], w_query, k_panel, v_panel, w_far,
+        scalars=(pair,),
+    )
+    got = exchange(pay, "zl")
     pay = run(reduce_kernel, shape(FAR_SIZE, Q_ROWS + 2 * TOK_ROW + PAD, HEAD_WIDTH), got)
     got = exchange(pay, "zh")
 
@@ -282,24 +314,24 @@
         lax.dynamic_slice_in_dim(sin, first, TOK_ROW),
         scalars=(far.reshape(1).astype(jnp.int32),),
     )
-    queries = exchange(pay, NEAR)
+    queries = exchange(pay, "zl")
     pay = run(
         attend_kernel,
         shape(NEAR_SIZE, Q_ROWS + PAD, HEAD_WIDTH),
-        queries, panel(cached_keys), panel(cached_values), new_k, new_v,
+        queries, kv_own, kv_far, new_k, new_v,
         scalars=(first.reshape(1).astype(jnp.int32),),
     )
-    got = exchange(pay, NEAR)
+    got = exchange(pay, "zl")
     got = exchange(run(mix_near_kernel, shape(FAR_SIZE, Q_ROWS + PAD, HEAD_WIDTH), got), "zh")
-    got = exchange(run(mix_far_kernel, shape(NEAR_SIZE, Q_ROWS, HEAD_WIDTH), got), NEAR)
-    width = w_out.shape[1]
+    got = exchange(run(mix_far_kernel, shape(NEAR_SIZE, Q_ROWS, HEAD_WIDTH), got), "zl")
     pay = run(
         output_kernel,
-        shape(COLS, BLOCK_TOKENS // COLS, width),
-        got, w_out,
-        scratch=[pltpu.VMEM((BLOCK_TOKENS, HEADS_HERE * HEAD_WIDTH), bf16)],
-    )
-    got = exchange(pay, "col")
+        shape(PAIR * COLS, BLOCK_TOKENS // COLS, w_out.shape[1]),
+        got, w_out, o_far,
+        scratch=[pltpu.VMEM((BLOCK_TOKENS, HEAD_COLS), bf16)],
+        scalars=(pair,),
+    )
+    got = exchange(pay, ("ylo", "col"))
     return jnp.sum(got.astype(f32), axis=0).astype(bf16)
 
 

time: 183 us -> 170 us (0.929)
  blocking collectives: 102 us -> 74.8 us
  starting transfers between devices: 27.3 us -> 39 us
    all_to_all x5 -> x4, blocking collectives: 102 us -> 74.8 us  [exchange(): return lax.all_to_all(x, axes, 0, 0, tiled=True)]
    ppermute x0 -> x3, waiting for transfers between devices: none -> 14.5 us  [trade(): return lax.ppermute(x, 'ylo', [(0, 1), (1, 0)])]
    all_to_all x3 -> x4, waiting for transfers between devices: 32.8 us -> 18.9 us  [exchange(): return lax.all_to_all(x, axes, 0, 0, tiled=True)]
    ppermute x0 -> x3, starting transfers between devices: none -> 7.24 us  [trade(): return lax.ppermute(x, 'ylo', [(0, 1), (1, 0)])]
    all_to_all x3 -> x4, starting transfers between devices: 27.3 us -> 31.8 us  [exchange(): return lax.all_to_all(x, axes, 0, 0, tiled=True)]
  transfers between devices with their start and end apart: 3 -> 7, of which waited for: 3 -> 5; matrix products, arithmetic and copies ran while one was open for 2% -> 3% of each run, Pallas kernels for 0% -> 1%
where the time goes in v3:
time: 170 us; the launch traced here: 169 us
  blocking collectives  74.8 us (44%)
  starting transfers between devices  39 us (23%)
  waiting for transfers between devices  33.4 us (20%)
  Pallas kernels  12.8 us (8%)
  local copies, waits for them, and re-layouts  7.91 us (5%)
    all_to_all x4, blocking collectives, exchange(): return lax.all_to_all(x, axes, 0, 0, tiled=True)  74.8 us
    all_to_all x4, starting transfers between devices, exchange(): return lax.all_to_all(x, axes, 0, 0, tiled=True)  31.8 us
    all_to_all x4, waiting for transfers between devices, exchange(): return lax.all_to_all(x, axes, 0, 0, tiled=True)  18.9 us
    ppermute x3, waiting for transfers between devices, trade(): return lax.ppermute(x, 'ylo', [(0, 1), (1, 0)])  14.5 us
    pallas_call x7, Pallas kernels, run(): pl.pallas_call(kernel, out_shape=shapes, in_specs=[smem] * len(scalars) +...  12.8 us
    ppermute x3, starting transfers between devices, trade(): return lax.ppermute(x, 'ylo', [(0, 1), (1, 0)])  7.24 us
  transfers between devices with their start and end apart: 7, of which 5 were waited for; matrix products, arithmetic and copies ran while one was open for 3% of the time, Pallas kernels for 1%

profile of v3, /device:TPU:1, one launch (start us, length us, event | category | flops | bytes accessed | tf_op | source)
XLA Modules:
  0.0 168.9 jit_solution(3731423679185108986)
XLA Ops:
  0.0 1.6 broadcast_in_dim.4
  1.6 10.4 %all-to-all-start = ((bf16[32,32,256]{2,1,0:T(8,128)(2,1)}), bf16[32,32,256]{2,1,0:T(8,128)(2,1)S(1)}, u32[]{:S(2)}, u32[]{:S(2)}) async-start(bf16[32,32,256]{2,1,0:T(8,128)(2,1)} %broadcast_in_dim.4), calls=%async_computation | async-start | bytes 1048576 | tf_op jit(solution)/shard_map/all_to_all | solution.py:60
  12.0 0.7 broadcast_in_dim.5.gain_ref
  12.7 0.9 constant_dynamic-slice_fusion.5
  13.6 0.9 constant_dynamic-slice_fusion.6
  14.5 3.4 %collective-permute-start = (bf16[272,512]{1,0:T(8,128)(2,1)S(1)}, bf16[272,512]{1,0:T(8,128)(2,1)S(1)}, u32[]{:S(2)}, u32[]{:S(2)}) collective-permute-start(bf16[272,512]{1,0:T(8,128)(2,1)S(1)} %fusion.1), channel_id=1, source_target_pairs={{0,256},{256,0},{1,257},{257,1},{2,258},{258,2},{3,259},{259,3},{4... | collective-permute-start | bytes 835592 | tf_op jit(solution)/shard_map/ppermute | solution.py:271
  17.9 9.5 %collective-permute-done.far_ref = bf16[272,512]{1,0:T(8,128)(2,1)S(1)} collective-permute-done((bf16[272,512]{1,0:T(8,128)(2,1)S(1)}, bf16[272,512]{1,0:T(8,128)(2,1)S(1)}, u32[]{:S(2)}, u32[]{:S(2)}) %collective-permute-start) | collective-permute-done | bytes 278560 | tf_op jit(solution)/shard_map/ppermute | solution.py:271
  27.4 0.0 all-to-all-done
  27.4 0.0 copy-start
  27.4 0.9 copy-done
  28.4 0.6 shard_map.100
  29.0 17.9 %all_to_all.40.got_ref = bf16[4,528,128]{2,1,0:T(8,128)(2,1)S(1)} all-to-all(bf16[4,528,128]{2,1,0:T(8,128)(2,1)S(1)} %shard_map.100), channel_id=1, replica_groups=mesh['ylo'=2,'zh'=4,'zl'=4,'col'=16] {'zl'}, dimensions={0} | all-to-all | bytes 1081344 | tf_op jit(solution)/shard_map/all_to_all | solution.py:60
  46.9 0.8 shard_map.101
  47.7 12.1 %all-to-all-start.2 = ((bf16[4,336,128]{2,1,0:T(8,128)(2,1)}), bf16[4,336,128]{2,1,0:T(8,128)(2,1)S(1)}, u32[]{:S(2)}, u32[]{:S(2)}) async-start(bf16[4,336,128]{2,1,0:T(8,128)(2,1)} %shard_map.101), calls=%async_computation.2 | async-start | bytes 688128 | tf_op jit(solution)/shard_map/all_to_all | solution.py:60
  59.8 1.3 dynamic-slice_bitcast_fusion
  61.1 0.0 copy-start.1
  61.1 0.1 pad_maximum_fusion.kv_ref
  61.2 1.9 %collective-permute-start.1 = (bf16[2,2048,128]{2,1,0:T(8,128)(2,1)S(1)}, bf16[2,2048,128]{2,1,0:T(8,128)(2,1)S(1)}, u32[]{:S(2)}, u32[]{:S(2)}) collective-permute-start(bf16[2,2048,128]{2,1,0:T(8,128)(2,1)S(1)} %pad_maximum_fusion.kv_ref), channel_id=1, source_target_pairs={{0,256},{256,0},{1,257},{257,1},{2,258},{258,2},{3,259},{259,3},{4... | collective-permute-start | bytes 3145736 | tf_op jit(solution)/shard_map/ppermute | solution.py:271
  63.1 0.7 constant_dynamic-slice_fusion.1
  63.9 0.9 constant_dynamic-slice_fusion.3
  64.8 14.4 %all-to-all-done.2.got_ref = bf16[4,336,128]{2,1,0:T(8,128)(2,1)S(1)} async-done(((bf16[4,336,128]{2,1,0:T(8,128)(2,1)}), bf16[4,336,128]{2,1,0:T(8,128)(2,1)S(1)}, u32[]{:S(2)}, u32[]{:S(2)}) %all-to-all-start.2) | async-done | bytes 344096 | tf_op jit(solution)/shard_map/all_to_all | solution.py:60
  79.2 0.9 shard_map.102
  80.1 4.7 %all-to-all-start.3 = ((bf16[4,256,128]{2,1,0:T(8,128)(2,1)}), bf16[4,256,128]{2,1,0:T(8,128)(2,1)S(1)}, u32[]{:S(2)}, u32[]{:S(2)}) async-start(bf16[4,256,128]{2,1,0:T(8,128)(2,1)} %get-tuple-element.8), calls=%async_computation.3 | async-start | bytes 524288 | tf_op jit(solution)/shard_map/all_to_all | solution.py:60
  84.8 1.2 collective-permute-done.1.other_ref
  86.0 4.4 %all-to-all-done.3.q_ref = bf16[4,256,128]{2,1,0:T(8,128)(2,1)S(1)} async-done(((bf16[4,256,128]{2,1,0:T(8,128)(2,1)}), bf16[4,256,128]{2,1,0:T(8,128)(2,1)S(1)}, u32[]{:S(2)}, u32[]{:S(2)}) %all-to-all-start.3) | async-done | bytes 262176 | tf_op jit(solution)/shard_map/all_to_all | solution.py:60
  90.5 9.0 %shard_map.103 = bf16[4,272,128]{2,1,0:T(8,128)(2,1)S(1)} custom-call(s32[1]{0:T(128)} %bitcast.1.first_ref, bf16[4,256,128]{2,1,0:T(8,128)(2,1)S(1)} %all-to-all-done.3.q_ref, bf16[2,2048,128]{2,1,0:T(8,128)(2,1)S(1)} %pad_maximum_fusion.kv_ref, bf16[2,2048,128]{2,1,0:T(8,128)(2,1)S(1)} %collective-permute-done.1.other_ref, ...), custom_call_target="tpu_custom_call" | custom-call | tf_op jit(solution)/shard_map/pallas_call | solution.py:70
  99.5 9.5 %all_to_all.41.got_ref = bf16[4,272,128]{2,1,0:T(8,128)(2,1)S(1)} all-to-all(bf16[4,272,128]{2,1,0:T(8,128)(2,1)S(1)} %shard_map.103), channel_id=1, replica_groups=mesh['ylo'=2,'zh'=4,'zl'=4,'col'=16] {'zl'}, dimensions={0} | all-to-all | bytes 557056 | tf_op jit(solution)/shard_map/all_to_all | solution.py:60
  109.0 0.2 shard_map.104
  109.2 23.1 %all_to_all.42.got_ref = bf16[4,272,128]{2,1,0:T(8,128)(2,1)S(1)} all-to-all(bf16[4,272,128]{2,1,0:T(8,128)(2,1)S(1)} %shard_map.104), channel_id=1, replica_groups=mesh['ylo'=2,'zh'=4,'zl'=4,'col'=16] {'zh'}, dimensions={0} | all-to-all | bytes 557056 | tf_op jit(solution)/shard_map/all_to_all | solution.py:60
  132.4 0.9 shard_map.105
  133.3 4.5 %all-to-all-start.6 = ((bf16[4,256,128]{2,1,0:T(8,128)(2,1)}), bf16[4,256,128]{2,1,0:T(8,128)(2,1)S(1)}, u32[]{:S(2)}, u32[]{:S(2)}) async-start(bf16[4,256,128]{2,1,0:T(8,128)(2,1)} %shard_map.105), calls=%async_computation.6 | async-start | bytes 524288 | tf_op jit(solution)/shard_map/all_to_all | solution.py:60
  137.9 0.0 copy-done.1
  137.9 1.9 %collective-permute-start.2 = (bf16[256,256]{1,0:T(8,128)(2,1)S(1)}, bf16[256,256]{1,0:T(8,128)(2,1)S(1)}, u32[]{:S(2)}, u32[]{:S(2)}) collective-permute-start(bf16[256,256]{1,0:T(8,128)(2,1)S(1)} %constant_dynamic-slice_fusion), channel_id=1, source_target_pairs={{0,256},{256,0},{1,257},{257,1},{2,258},{258,2},{3,259},{259,3},{4... | collective-permute-start | bytes 393224 | tf_op jit(solution)/shard_map/ppermute | solution.py:271
  139.8 3.8 %collective-permute-done.2.other_ref = bf16[256,256]{1,0:T(8,128)(2,1)S(1)} collective-permute-done((bf16[256,256]{1,0:T(8,128)(2,1)S(1)}, bf16[256,256]{1,0:T(8,128)(2,1)S(1)}, u32[]{:S(2)}, u32[]{:S(2)}) %collective-permute-start.2) | collective-permute-done | bytes 131104 | tf_op jit(solution)/shard_map/ppermute | solution.py:271
  143.6 0.0 all-to-all-done.6.got_ref
  143.6 0.3 shard_map.106
  143.9 24.3 %all_to_all.43 = bf16[32,32,256]{2,1,0:T(8,128)(2,1)S(1)} all-to-all(bf16[32,32,256]{2,1,0:T(8,128)(2,1)S(1)} %shard_map.106), channel_id=1, replica_groups=mesh['ylo'=2,'zh'=4,'zl'=4,'col'=16] {'ylo','col'}, dimensions={0} | all-to-all | bytes 1048576 | tf_op jit(solution)/shard_map/all_to_all | solution.py:60
  168.2 0.7 reduce_sum.12
  (2 shorter events, 0.0 us)
Async XLA Ops:
  1.6 25.9 %all-to-all-start = ((bf16[32,32,256]{2,1,0:T(8,128)(2,1)}), bf16[32,32,256]{2,1,0:T(8,128)(2,1)S(1)}, u32[]{:S(2)}, u32[]{:S(2)}) async-start(bf16[32,32,256]{2,1,0:T(8,128)(2,1)} %broadcast_in_dim.4), calls=%async_computation | async-start | bytes 1048576 | tf_op jit(solution)/shard_map/all_to_all | solution.py:60
  14.5 12.9 %collective-permute-start = (bf16[272,512]{1,0:T(8,128)(2,1)S(1)}, bf16[272,512]{1,0:T(8,128)(2,1)S(1)}, u32[]{:S(2)}, u32[]{:S(2)}) collective-permute-start(bf16[272,512]{1,0:T(8,128)(2,1)S(1)} %fusion.1), channel_id=1, source_target_pairs={{0,256},{256,0},{1,257},{257,1},{2,258},{258,2},{3,259},{259,3},{4... | collective-permute-start | bytes 835592 | tf_op jit(solution)/shard_map/ppermute | solution.py:271
  27.4 1.0 copy-start
  47.7 31.5 %all-to-all-start.2 = ((bf16[4,336,128]{2,1,0:T(8,128)(2,1)}), bf16[4,336,128]{2,1,0:T(8,128)(2,1)S(1)}, u32[]{:S(2)}, u32[]{:S(2)}) async-start(bf16[4,336,128]{2,1,0:T(8,128)(2,1)} %shard_map.101), calls=%async_computation.2 | async-start | bytes 688128 | tf_op jit(solution)/shard_map/all_to_all | solution.py:60
  61.1 76.8 %copy-start.1 = (bf16[512,256]{1,0:T(8,128)(2,1)S(1)}, bf16[512,256]{1,0:T(8,128)(2,1)}, u32[]{:S(2)}) copy-start(bf16[512,256]{1,0:T(8,128)(2,1)} %w_ref.3) | copy-start | bytes 786436
  61.2 24.9 %collective-permute-start.1 = (bf16[2,2048,128]{2,1,0:T(8,128)(2,1)S(1)}, bf16[2,2048,128]{2,1,0:T(8,128)(2,1)S(1)}, u32[]{:S(2)}, u32[]{:S(2)}) collective-permute-start(bf16[2,2048,128]{2,1,0:T(8,128)(2,1)S(1)} %pad_maximum_fusion.kv_ref), channel_id=1, source_target_pairs={{0,256},{256,0},{1,257},{257,1},{2,258},{258,2},{3,259},{259,3},{4... | collective-permute-start | bytes 3145736 | tf_op jit(solution)/shard_map/ppermute | solution.py:271
  80.1 10.4 %all-to-all-start.3 = ((bf16[4,256,128]{2,1,0:T(8,128)(2,1)}), bf16[4,256,128]{2,1,0:T(8,128)(2,1)S(1)}, u32[]{:S(2)}, u32[]{:S(2)}) async-start(bf16[4,256,128]{2,1,0:T(8,128)(2,1)} %get-tuple-element.8), calls=%async_computation.3 | async-start | bytes 524288 | tf_op jit(solution)/shard_map/all_to_all | solution.py:60
  133.3 10.3 %all-to-all-start.6 = ((bf16[4,256,128]{2,1,0:T(8,128)(2,1)}), bf16[4,256,128]{2,1,0:T(8,128)(2,1)S(1)}, u32[]{:S(2)}, u32[]{:S(2)}) async-start(bf16[4,256,128]{2,1,0:T(8,128)(2,1)} %shard_map.105), calls=%async_computation.6 | async-start | bytes 524288 | tf_op jit(solution)/shard_map/all_to_all | solution.py:60
  137.9 5.7 %collective-permute-start.2 = (bf16[256,256]{1,0:T(8,128)(2,1)S(1)}, bf16[256,256]{1,0:T(8,128)(2,1)S(1)}, u32[]{:S(2)}, u32[]{:S(2)}) collective-permute-start(bf16[256,256]{1,0:T(8,128)(2,1)S(1)} %constant_dynamic-slice_fusion), channel_id=1, source_target_pairs={{0,256},{256,0},{1,257},{257,1},{2,258},{258,2},{3,259},{259,3},{4... | collective-permute-start | bytes 393224 | tf_op jit(solution)/shard_map/ppermute | solution.py:271

commit v4 on v3

--- a/solution.py
+++ b/solution.py
@@ -22,6 +22,8 @@
 FAR_SIZE = 4
 COLS = 16
 PAIR = 2
+CHIPS = 16
+PLANE = ("ylo", "yhi", "x")
 HEADS_HERE = QUERY_HEADS // COLS // PAIR
 HEAD_COLS = HEADS_HERE * HEAD_WIDTH
 TOK_NEAR = BLOCK_TOKENS // NEAR_SIZE
@@ -53,7 +55,7 @@
 SCORE_SCALE = math.log2(math.e) / math.sqrt(HEAD_WIDTH)
 LN2 = math.log(2.0)
 PAD = 16
-PANEL = HEAD_PANEL = 256
+PANEL = 256
 
 
 def exchange(x, axes):
@@ -114,23 +116,26 @@
     return jnp.sum(jnp.where(same(n, n), wide, 0.0), axis=0, keepdims=True)
 
 
-def project_kernel(pair_ref, tok_ref, gain_ref, w_ref, k_ref, v_ref, far_ref, out_ref):
+def project_kernel(pair_ref, tok_ref, gain_ref, w_ref, kv_ref, far_ref, out_ref):
     mine = pair_ref[0]
-    gains = [gain_ref[...], far_ref[HEAD_PANEL : HEAD_PANEL + 1, :PANEL]]
-    toks = [tok_ref[mine], tok_ref[1 - mine]]
+    gains = [gain_ref[...], far_ref[PANEL : PANEL + 1, :PANEL]]
+    toks = []
+    for side in (mine, 1 - mine):
+        blocks = [tok_ref[core, side, j] for j in range(CHIPS // PAIR) for core in range(2)]
+        toks.append(jnp.concatenate(blocks, axis=0))
     scaled = [(t.astype(f32) * g.astype(f32)).astype(bf16) for t, g in zip(toks, gains)]
-    panels = [w_ref[:, pl.ds(pl.multiple_of(mine * HEAD_COLS, HEAD_COLS), HEAD_COLS)]]
-    panels.append(jnp.concatenate([k_ref[...], v_ref[...]], axis=1))
+    panels = [w_ref[:, pl.ds(pl.multiple_of(mine * HEAD_COLS, HEAD_COLS), HEAD_COLS)], kv_ref[...]]
     for i, panel in enumerate(panels):
-        other = far_ref[:HEAD_PANEL, HEAD_COLS * i : HEAD_COLS * (i + 1)]
+        width = panel.shape[1]
+        other = far_ref[:PANEL, HEAD_COLS * i : HEAD_COLS * i + width]
         part = jnp.dot(scaled[0], panel, preferred_element_type=f32)
         part = (part + jnp.dot(scaled[1], other, preferred_element_type=f32)).astype(bf16)
-        for j in range(2):
+        for j in range(width // HEAD_WIDTH):
             head = part[:, HEAD_WIDTH * j : HEAD_WIDTH * (j + 1)]
             row = (2 * i + j) * TOK_NEAR
             for n in range(NEAR_SIZE):
                 out_ref[n, row : row + TOK_NEAR, :] = head[n * TOK_NEAR : (n + 1) * TOK_NEAR]
-    row = (HEADS_HERE + 2) * TOK_NEAR
+    row = Q_ROWS + TOK_NEAR
     contract = (((1,), (1,)), ((), ()))
     for n in range(NEAR_SIZE):
         sums = jnp.zeros((1, TOK_NEAR), f32)
@@ -147,26 +152,26 @@
     for n in range(1, NEAR_SIZE):
         total = total + got_ref[n].astype(f32)
     low = total.astype(bf16)
-    k_row, v_row, s_row = Q_ROWS, Q_ROWS + TOK_NEAR, Q_ROWS + 2 * TOK_NEAR
+    s_row = Q_ROWS + TOK_NEAR
     sums = total[s_row : s_row + 1] + total[s_row + 1 : s_row + 2] + total[s_row + 2 : s_row + 3]
     tile = pack_rows(parts3(sums))
-    own, end = TOK_ROW, 2 * TOK_ROW
+    end = Q_ROWS + TOK_ROW
     for f in range(FAR_SIZE):
+        row = Q_ROWS + TOK_ROW * f
         out_ref[f, :Q_ROWS, :] = low[:Q_ROWS]
-        out_ref[f, Q_ROWS : Q_ROWS + own, :] = low[k_row + own * f : k_row + own * (f + 1)]
-        out_ref[f, Q_ROWS + own : Q_ROWS + end, :] = low[v_row + own * f : v_row + own * (f + 1)]
-        out_ref[f, Q_ROWS + end : Q_ROWS + end + PAD, :] = tile
-
-
-def rope_kernel(far_ref, got_ref, cos_ref, sin_ref, cosn_ref, sinn_ref, q_ref, k_ref, v_ref):
+        out_ref[f, Q_ROWS:end, :] = low[row : row + TOK_ROW]
+        out_ref[f, end : end + PAD, :] = tile
+
+
+def rope_kernel(place_ref, got_ref, cos_ref, sin_ref, cosn_ref, sinn_ref, q_ref, new_ref):
     total = got_ref[0].astype(f32)
     for n in range(1, FAR_SIZE):
         total = total + got_ref[n].astype(f32)
-    row = Q_ROWS + 2 * TOK_ROW
+    row = Q_ROWS + TOK_ROW
     sums = total[row : row + 1] + total[row + 1 : row + 2] + total[row + 2 : row + 3]
     inv = lax.rsqrt(sums / MODEL_WIDTH + epsilon)
     inv_q = to_column(inv, TOK_NEAR)
-    inv_n = to_column(inv, TOK_ROW, far_ref[0] * TOK_ROW)
+    inv_n = to_column(inv, TOK_ROW, place_ref[0] * TOK_ROW)
     cos, sin = cos_ref[...], sin_ref[...]
     for h in range(HEADS_HERE):
         u = total[h * TOK_NEAR : (h + 1) * TOK_NEAR] * inv_q
@@ -174,18 +179,20 @@
         for n in range(NEAR_SIZE):
             q_ref[n, h * TOK_NEAR : (h + 1) * TOK_NEAR, :] = u
     u = total[Q_ROWS : Q_ROWS + TOK_ROW] * inv_n
-    k_ref[...] = (u * cosn_ref[...] + pltpu.roll(u, HEAD_WIDTH // 2, 1) * sinn_ref[...]).astype(bf16)
-    v_ref[...] = (total[Q_ROWS + TOK_ROW : Q_ROWS + 2 * TOK_ROW] * inv_n).astype(bf16)
-
-
-def attend_kernel(first_ref, q_ref, kv_ref, other_ref, nk_ref, nv_ref, out_ref):
+    turned = u * cosn_ref[...] + pltpu.roll(u, HEAD_WIDTH // 2, 1) * sinn_ref[...]
+    new_ref[...] = jnp.where(place_ref[1] == 0, turned, u).astype(bf16)
+
+
+def attend_kernel(place_ref, q_ref, kv_ref, other_ref, own_ref, swap_ref, out_ref):
     contract = (((1,), (1,)), ((), ()))
     zeros = jnp.zeros((HEAD_WIDTH - TOK_ROW, HEAD_WIDTH), bf16)
-    new_k = jnp.concatenate([nk_ref[...], zeros], axis=0)
-    new_v = jnp.concatenate([nv_ref[...], zeros], axis=0)
+    even = place_ref[1] == 0
+    own, swap = own_ref[...].astype(f32), swap_ref[...].astype(f32)
+    new_k = jnp.concatenate([jnp.where(even, own, swap).astype(bf16), zeros], axis=0)
+    new_v = jnp.concatenate([jnp.where(even, swap, own).astype(bf16), zeros], axis=0)
     slot = lax.broadcasted_iota(jnp.int32, (Q_ROWS, HEAD_WIDTH), 1)
     line = lax.broadcasted_iota(jnp.int32, (Q_ROWS, HEAD_WIDTH), 0)
-    new_token = jnp.where(slot < TOK_ROW, first_ref[0] + slot, BLOCK_TOKENS)
+    new_token = jnp.where(slot < TOK_ROW, place_ref[0] + slot, BLOCK_TOKENS)
 
     def block(n, carry):
         q = q_ref[n]
@@ -248,106 +255,127 @@
 
 def mix_far_kernel(got_ref, out_ref):
     halves, _ = mix(got_ref, FAR_SIZE)
+    rows = BLOCK_TOKENS // COLS
     for n in range(NEAR_SIZE):
-        out_ref[n, :HEAD_WIDTH, :] = halves[0]
-        out_ref[n, HEAD_WIDTH:Q_ROWS, :] = halves[1]
-
-
-def output_kernel(pair_ref, got_ref, w_ref, other_ref, out_ref, ctx_ref):
-    mine = pair_ref[0]
+        for core in range(2):
+            for h in range(HEADS_HERE):
+                for sub in range(2):
+                    at = (2 * sub + core) * rows
+                    to = (2 * h + sub) * rows
+                    out_ref[2 * n + core, to : to + rows, :] = halves[h][at : at + rows]
+
+
+def output_kernel(place_ref, got_ref, own_ref, swap_ref, out_ref, ctx_ref):
+    mine, core = place_ref[0], place_ref[1]
+    rows = BLOCK_TOKENS // COLS
     for n in range(NEAR_SIZE):
         for h in range(HEADS_HERE):
-            block = got_ref[n, h * TOK_NEAR : (h + 1) * TOK_NEAR, :]
-            ctx_ref[n * TOK_NEAR : (n + 1) * TOK_NEAR, h * HEAD_WIDTH : (h + 1) * HEAD_WIDTH] = block
-    own = w_ref[pl.ds(pl.multiple_of(mine * HEAD_COLS, HEAD_COLS), HEAD_COLS), :]
-    rows = BLOCK_TOKENS // COLS
-    for side, panel in ((mine, own), (1 - mine, other_ref[...])):
-        part = jnp.dot(ctx_ref[...], panel, preferred_element_type=f32).astype(bf16)
-        for c in range(COLS):
-            out_ref[side * COLS + c] = part[c * rows : (c + 1) * rows]
-
-
-def trade(x):
-    return lax.ppermute(x, "ylo", [(0, 1), (1, 0)])
+            to = slice(2 * n * rows, 2 * (n + 1) * rows)
+            at = slice(2 * h * rows, 2 * (h + 1) * rows)
+            lanes = slice(h * HEAD_WIDTH, (h + 1) * HEAD_WIDTH)
+            ctx_ref[0, to, lanes] = got_ref[2 * n + core, at, :]
+            ctx_ref[1, to, lanes] = got_ref[2 * n + 1 - core, at, :]
+    for i, side in enumerate((mine, 1 - mine)):
+        part = jnp.dot(ctx_ref[0], own_ref[i], preferred_element_type=f32)
+        part = part + jnp.dot(ctx_ref[1], swap_ref[i], preferred_element_type=f32)
+        part = part.astype(bf16)
+        for c in range(CHIPS // PAIR):
+            out_ref[side * (CHIPS // PAIR) + c] = part[c * rows : (c + 1) * rows]
+
+
+def trade(x, axis):
+    return lax.ppermute(x, axis, [(0, 1), (1, 0)])
 
 
 def body(tokens, norm_gain, w_query, key_weight, value_weight, w_out, cached_keys, cached_values):
     mine = lax.axis_index("ylo")
     near = lax.axis_index("zl")
     far = lax.axis_index("zh")
-    group = lax.axis_index("col") // 2
-    pair = mine.reshape(1).astype(jnp.int32)
+    core = lax.axis_index("core")
+    group = lax.axis_index("yhi") * 4 + lax.axis_index("x")
 
     def panel(x):
         return lax.dynamic_slice_in_dim(x, group * HEAD_WIDTH, HEAD_WIDTH, 1)
 
-    k_panel, v_panel = panel(key_weight), panel(value_weight)
+    def place(*xs):
+        return (jnp.stack(xs).astype(jnp.int32),)
+
+    kv_panel = jnp.where(core == 0, panel(key_weight), panel(value_weight))
     w_far = lax.dynamic_slice_in_dim(w_query, (1 - mine) * HEAD_COLS, HEAD_COLS, 1)
-    w_far = jnp.concatenate([w_far, k_panel, v_panel], axis=1)
+    w_far = jnp.concatenate([w_far, kv_panel], axis=1)
     gain_row = jnp.pad(norm_gain[None], ((0, PAD - 1), (0, w_far.shape[1] - norm_gain.shape[0])))
-    w_far = trade(jnp.concatenate([w_far, gain_row], axis=0))
-    whole = spread(tokens, PAIR * COLS, ("ylo", "col")).reshape(PAIR, BLOCK_TOKENS, -1)
+    w_far = trade(jnp.concatenate([w_far, gain_row], axis=0), "ylo")
+    whole = lax.all_gather(spread(tokens, CHIPS, PLANE), "core", axis=0)
+    whole = whole.reshape((2, PAIR, CHIPS // PAIR) + tokens.shape)
     kv_own = jnp.stack([panel(cached_keys), panel(cached_values)])
-    kv_far = trade(kv_own)
-    o_far = trade(lax.dynamic_slice_in_dim(w_out, (1 - mine) * HEAD_COLS, HEAD_COLS, 0))
-
+    kv_far = trade(kv_own, "ylo")
     pay = run(
         project_kernel,
-        shape(NEAR_SIZE, Q_ROWS + 2 * TOK_NEAR + PAD, HEAD_WIDTH),
-        whole, norm_gain[None], w_query, k_panel, v_panel, w_far,
-        scalars=(pair,),
-    )
+        shape(NEAR_SIZE, Q_ROWS + TOK_NEAR + PAD, HEAD_WIDTH),
+        whole, norm_gain[None], w_query, kv_panel, w_far,
+        scalars=place(mine),
+    )
+    pay, w_out = lax.optimization_barrier((pay, w_out))
+    o_own = lax.dynamic_slice_in_dim(w_out, mine * HEAD_COLS, HEAD_COLS, 0)
+    o_far = trade(lax.dynamic_slice_in_dim(w_out, (1 - mine) * HEAD_COLS, HEAD_COLS, 0), "ylo")
     got = exchange(pay, "zl")
-    pay = run(reduce_kernel, shape(FAR_SIZE, Q_ROWS + 2 * TOK_ROW + PAD, HEAD_WIDTH), got)
+    pay = run(reduce_kernel, shape(FAR_SIZE, Q_ROWS + TOK_ROW + PAD, HEAD_WIDTH), got)
+    pay, o_far = lax.optimization_barrier((pay, o_far))
+    o_own = jnp.stack([o_own, o_far])
     got = exchange(pay, "zh")
 
     start = near * TOK_NEAR
     first = start + far * TOK_ROW
     cos, sin = jnp.asarray(COS_TABLE), jnp.asarray(SIN_TABLE)
-    pay, new_k, new_v = run(
+    pay, new_own = run(
         rope_kernel,
-        (shape(NEAR_SIZE, Q_ROWS, HEAD_WIDTH), shape(TOK_ROW, HEAD_WIDTH), shape(TOK_ROW, HEAD_WIDTH)),
+        (shape(NEAR_SIZE, Q_ROWS, HEAD_WIDTH), shape(TOK_ROW, HEAD_WIDTH)),
         got,
         lax.dynamic_slice_in_dim(cos, start, TOK_NEAR),
         lax.dynamic_slice_in_dim(sin, start, TOK_NEAR),
         lax.dynamic_slice_in_dim(cos, first, TOK_ROW),
         lax.dynamic_slice_in_dim(sin, first, TOK_ROW),
-        scalars=(far.reshape(1).astype(jnp.int32),),
-    )
+        scalars=place(far, core),
+    )
+    new_swap = trade(new_own, "core")
+    o_swap = trade(o_own, "core")
     queries = exchange(pay, "zl")
     pay = run(
         attend_kernel,
         shape(NEAR_SIZE, Q_ROWS + PAD, HEAD_WIDTH),
-        queries, kv_own, kv_far, new_k, new_v,
-        scalars=(first.reshape(1).astype(jnp.int32),),
-    )
+        queries, kv_own, kv_far, new_own, new_swap,
+        scalars=place(first, core),
+    )
+    pay, o_swap = lax.optimization_barrier((pay, o_swap))
     got = exchange(pay, "zl")
     got = exchange(run(mix_near_kernel, shape(FAR_SIZE, Q_ROWS + PAD, HEAD_WIDTH), got), "zh")
-    got = exchange(run(mix_far_kernel, shape(NEAR_SIZE, Q_ROWS, HEAD_WIDTH), got), "zl")
+    got = run(mix_far_kernel, shape(2 * NEAR_SIZE, Q_ROWS // 2, HEAD_WIDTH), got)
+    got = exchange(got, ("zl", "core"))
     pay = run(
         output_kernel,
-        shape(PAIR * COLS, BLOCK_TOKENS // COLS, w_out.shape[1]),
-        got, w_out, o_far,
-        scratch=[pltpu.VMEM((BLOCK_TOKENS, HEAD_COLS), bf16)],
-        scalars=(pair,),
-    )
-    got = exchange(pay, ("ylo", "col"))
+        shape(CHIPS, BLOCK_TOKENS // COLS, w_out.shape[1]),
+        got, o_own, o_swap,
+        scratch=[pltpu.VMEM((2, BLOCK_TOKENS // 2, HEAD_COLS), bf16)],
+        scalars=place(mine, core),
+    )
+    got = exchange(pay, PLANE)
     return jnp.sum(got.astype(f32), axis=0).astype(bf16)
 
 
 def solution(mesh):
-    fine = Mesh(mesh.devices.reshape(2, 4, 4, COLS), ("ylo", "zh", "zl", "col"))
+    fine = Mesh(mesh.devices.reshape(2, 4, 4, 2, 4, 2), ("ylo", "zh", "zl", "yhi", "x", "core"))
     row = ("ylo", "zh", "zl")
+    col = ("yhi", "x", "core")
     placed = (
-        P("col", row),
+        P(col, row),
         P(row),
-        P(row, "col"),
+        P(row, col),
         P(row, None),
         P(row, None),
-        P("col", row),
+        P(col, row),
         P(row, None),
         P(row, None),
     )
     return jax.shard_map(
-        body, mesh=fine, in_specs=placed, out_specs=P("col", row), check_vma=False
-    )
+        body, mesh=fine, in_specs=placed, out_specs=P(col, row), check_vma=False
+    )

time: 170 us -> 160 us (0.941)
  blocking collectives: 74.8 us -> 50.2 us
  starting transfers between devices: 39 us -> 51.5 us
  Pallas kernels: 12.8 us -> 15.1 us
    all_to_all x4 -> x3, blocking collectives: 74.8 us -> 44.6 us  [exchange(): return lax.all_to_all(x, axes, 0, 0, tiled=True)]
    all_to_all x4 -> x5, waiting for transfers between devices: 18.9 us -> 32.4 us  [exchange(): return lax.all_to_all(x, axes, 0, 0, tiled=True)]
    ppermute x3 -> x5, waiting for transfers between devices: 14.5 us -> 1.07 us  [trade(): return lax.ppermute(x, axis, [(0, 1), (1, 0)])]
    ppermute x3 -> x5, starting transfers between devices: 7.24 us -> 15.1 us  [trade(): return lax.ppermute(x, axis, [(0, 1), (1, 0)])]
    all_gather x0 -> x1, blocking collectives: none -> 5.58 us  [body(): whole = lax.all_gather(spread(tokens, CHIPS, PLANE), 'core', axis=0)]
    all_to_all x4 -> x5, starting transfers between devices: 31.8 us -> 36.5 us  [exchange(): return lax.all_to_all(x, axes, 0, 0, tiled=True)]
    pallas_call x7, Pallas kernels: 12.8 us -> 15.1 us  [run(): pl.pallas_call(kernel, out_shape=shapes, in_specs=[smem] * len(scalars) +...]
  transfers between devices with their start and end apart: 7 -> 10, of which waited for: 5 -> 5; matrix products, arithmetic and copies ran while one was open for 3% -> 4% of each run, Pallas kernels for 1% -> 7%
where the time goes in v4:
time: 160 us; the launch traced here: 159 us
  starting transfers between devices  51.5 us (32%)
  blocking collectives  50.2 us (31%)
  waiting for transfers between devices  33.4 us (21%)
  Pallas kernels  15.1 us (9%)
  local copies, waits for them, and re-layouts  6.93 us (4%)
  other arithmetic  1.93 us (1%)
    all_to_all x3, blocking collectives, exchange(): return lax.all_to_all(x, axes, 0, 0, tiled=True)  44.6 us
    all_to_all x5, starting transfers between devices, exchange(): return lax.all_to_all(x, axes, 0, 0, tiled=True)  36.5 us
    all_to_all x5, waiting for transfers between devices, exchange(): return lax.all_to_all(x, axes, 0, 0, tiled=True)  32.4 us
    pallas_call x7, Pallas kernels, run(): pl.pallas_call(kernel, out_shape=shapes, in_specs=[smem] * len(scalars) +...  15.1 us
    ppermute x5, starting transfers between devices, trade(): return lax.ppermute(x, axis, [(0, 1), (1, 0)])  15.1 us
    all_gather x1, blocking collectives, body(): whole = lax.all_gather(spread(tokens, CHIPS, PLANE), 'core', axis=0)  5.58 us
  transfers between devices with their start and end apart: 10, of which 5 were waited for; matrix products, arithmetic and copies ran while one was open for 4% of the time, Pallas kernels for 7%

profile of v4, /device:TPU:1, one launch (start us, length us, event | category | flops | bytes accessed | tf_op | source)
XLA Modules:
  0.0 159.3 jit_solution(16232985873012728405)
XLA Ops:
  0.0 0.0 copy-start.1
  0.0 1.5 broadcast_in_dim.4
  1.5 7.6 %all-to-all-start = ((bf16[16,32,256]{2,1,0:T(8,128)(2,1)}), bf16[16,32,256]{2,1,0:T(8,128)(2,1)S(1)}, u32[]{:S(2)}, u32[]{:S(2)}) async-start(bf16[16,32,256]{2,1,0:T(8,128)(2,1)} %broadcast_in_dim.4), calls=%async_computation | async-start | bytes 524288 | tf_op jit(solution)/shard_map/all_to_all | solution.py:62
  9.1 0.9 constant_dynamic-slice_fusion.5
  10.0 0.9 dynamic-slice_select_fusion.kv_ref
  10.9 0.7 broadcast_in_dim.5.gain_ref
  11.6 3.3 %collective-permute-start = (bf16[272,384]{1,0:T(8,128)(2,1)S(1)}, bf16[272,384]{1,0:T(8,128)(2,1)S(1)}, u32[]{:S(2)}, u32[]{:S(2)}) collective-permute-start(bf16[272,384]{1,0:T(8,128)(2,1)S(1)} %fusion.1), channel_id=1, source_target_pairs={{0,256},{256,0},{1,257},{257,1},{2,258},{258,2},{3,259},{259,3},{4... | collective-permute-start | bytes 626696 | tf_op jit(solution)/shard_map/ppermute | solution.py:287
  14.9 1.9 %all-to-all-done = bf16[16,32,256]{2,1,0:T(8,128)(2,1)S(1)} async-done(((bf16[16,32,256]{2,1,0:T(8,128)(2,1)}), bf16[16,32,256]{2,1,0:T(8,128)(2,1)S(1)}, u32[]{:S(2)}, u32[]{:S(2)}) %all-to-all-start) | async-done | bytes 262176 | tf_op jit(solution)/shard_map/all_to_all | solution.py:62
  16.8 5.6 %all-gather = bf16[32,32,256]{2,1,0:T(8,128)(2,1)S(1)} all-gather(bf16[16,32,256]{2,1,0:T(8,128)(2,1)S(1)} %all-to-all-done), channel_id=2, replica_groups=mesh['ylo'=2,'zh'=4,'zl'=4,'yhi'=2,'x'=4,'core'=2] {'core'}, dimensions={0}, use_global_device_ids=true | all-gather | bytes 786432 | tf_op jit(solution)/shard_map/all_gather | solution.py:308
  22.3 0.0 collective-permute-done.far_ref
  22.3 0.0 copy-start
  22.4 0.9 copy-done
  23.3 1.4 shard_map.100
  24.7 3.8 %all-to-all-start.1 = ((bf16[4,400,128]{2,1,0:T(8,128)(2,1)}), bf16[4,400,128]{2,1,0:T(8,128)(2,1)S(1)}, u32[]{:S(2)}, u32[]{:S(2)}) async-start(bf16[4,400,128]{2,1,0:T(8,128)(2,1)} %shard_map.100), calls=%async_computation.1 | async-start | bytes 819200 | tf_op jit(solution)/shard_map/all_to_all | solution.py:62
  28.4 0.0 copy-done.1
  28.5 2.1 %collective-permute-start.1 = (bf16[256,256]{1,0:T(8,128)(2,1)S(1)}, bf16[256,256]{1,0:T(8,128)(2,1)S(1)}, u32[]{:S(2)}, u32[]{:S(2)}) collective-permute-start(bf16[256,256]{1,0:T(8,128)(2,1)S(1)} %get-tuple-element.22), channel_id=1, source_target_pairs={{0,256},{256,0},{1,257},{257,1},{2,258},{258,2},{3,259},{259,3},{4... | collective-permute-start | bytes 393224 | tf_op jit(solution)/shard_map/ppermute | solution.py:287
  30.5 9.4 %all-to-all-done.1.got_ref = bf16[4,400,128]{2,1,0:T(8,128)(2,1)S(1)} async-done(((bf16[4,400,128]{2,1,0:T(8,128)(2,1)}), bf16[4,400,128]{2,1,0:T(8,128)(2,1)S(1)}, u32[]{:S(2)}, u32[]{:S(2)}) %all-to-all-start.1) | async-done | bytes 409632 | tf_op jit(solution)/shard_map/all_to_all | solution.py:62
  40.0 0.8 shard_map.101
  40.7 0.0 collective-permute-done.1
  40.7 12.6 %all-to-all-start.2 = ((bf16[4,304,128]{2,1,0:T(8,128)(2,1)}), bf16[4,304,128]{2,1,0:T(8,128)(2,1)S(1)}, u32[]{:S(2)}, u32[]{:S(2)}) async-start(bf16[4,304,128]{2,1,0:T(8,128)(2,1)} %shard_map.101), calls=%async_computation.2 | async-start | bytes 622592 | tf_op jit(solution)/shard_map/all_to_all | solution.py:62
  53.4 1.3 dynamic-slice_bitcast_fusion
  54.6 0.1 pad_maximum_fusion.kv_ref
  54.8 1.9 %collective-permute-start.2 = (bf16[2,2048,128]{2,1,0:T(8,128)(2,1)S(1)}, bf16[2,2048,128]{2,1,0:T(8,128)(2,1)S(1)}, u32[]{:S(2)}, u32[]{:S(2)}) collective-permute-start(bf16[2,2048,128]{2,1,0:T(8,128)(2,1)S(1)} %pad_maximum_fusion.kv_ref), channel_id=1, source_target_pairs={{0,256},{256,0},{1,257},{257,1},{2,258},{258,2},{3,259},{259,3},{4... | collective-permute-start | bytes 3145736 | tf_op jit(solution)/shard_map/ppermute | solution.py:287
  56.7 0.1 pad_add_fusion.2.place_ref
  56.8 0.7 constant_dynamic-slice_fusion
  57.5 0.9 constant_dynamic-slice_fusion.2
  58.4 12.4 %all-to-all-done.2.got_ref = bf16[4,304,128]{2,1,0:T(8,128)(2,1)S(1)} async-done(((bf16[4,304,128]{2,1,0:T(8,128)(2,1)}), bf16[4,304,128]{2,1,0:T(8,128)(2,1)S(1)}, u32[]{:S(2)}, u32[]{:S(2)}) %all-to-all-start.2) | async-done | bytes 311328 | tf_op jit(solution)/shard_map/all_to_all | solution.py:62
  70.8 1.4 shard_map.102
  72.2 3.4 %all-to-all-start.3 = ((bf16[4,256,128]{2,1,0:T(8,128)(2,1)}), bf16[4,256,128]{2,1,0:T(8,128)(2,1)S(1)}, u32[]{:S(2)}, u32[]{:S(2)}) async-start(bf16[4,256,128]{2,1,0:T(8,128)(2,1)} %get-tuple-element.16), calls=%async_computation.3 | async-start | bytes 524288 | tf_op jit(solution)/shard_map/all_to_all | solution.py:62
  75.7 5.9 %collective-permute-start.4 = (bf16[2,256,256]{2,1,0:T(8,128)(2,1)S(1)}, bf16[2,256,256]{2,1,0:T(8,128)(2,1)S(1)}, u32[]{:S(2)}, u32[]{:S(2)}) collective-permute-start(bf16[2,256,256]{2,1,0:T(8,128)(2,1)S(1)} %pad_maximum_fusion.1.own_ref), channel_id=1, source_target_pairs={{0,1},{1,0},{2,3},{3,2},{4,5},{5,4},{6,7},{7,6},{8,9},{9,8},{10,11... | collective-permute-start | bytes 786440 | tf_op jit(solution)/shard_map/ppermute | solution.py:287
  81.6 1.9 %collective-permute-start.3 = (bf16[32,128]{1,0:T(8,128)(2,1)S(1)}, bf16[32,128]{1,0:T(8,128)(2,1)S(1)}, u32[]{:S(2)}, u32[]{:S(2)}) collective-permute-start(bf16[32,128]{1,0:T(8,128)(2,1)S(1)} %get-tuple-element.17.own_ref), channel_id=1, source_target_pairs={{0,1},{1,0},{2,3},{3,2},{4,5},{5,4},{6,7},{7,6},{8,9},{9,8},{10,11... | collective-permute-start | bytes 24584 | tf_op jit(solution)/shard_map/ppermute | solution.py:287
  83.5 0.1 pad_add_fusion.1.place_ref
  83.6 0.0 collective-permute-done.2.other_ref
  83.6 1.1 collective-permute-done.3.swap_ref
  84.7 0.0 all-to-all-done.3.q_ref
  84.7 9.5 %shard_map.103 = bf16[4,272,128]{2,1,0:T(8,128)(2,1)S(1)} custom-call(s32[2]{0:T(128)S(1)} %pad_add_fusion.1.place_ref, bf16[4,256,128]{2,1,0:T(8,128)(2,1)S(1)} %all-to-all-done.3.q_ref, bf16[2,2048,128]{2,1,0:T(8,128)(2,1)S(1)} %pad_maximum_fusion.kv_ref, bf16[2,2048,128]{2,1,0:T(8,128)(2,1)S(1)} %collective-permute-done.2.other_ref, ...), custom_call_target="tpu_custom_call" | custom-call | tf_op jit(solution)/shard_map/pallas_call | solution.py:72
  94.2 0.0 collective-permute-done.4.swap_ref
  94.2 13.0 %all_to_all.40.got_ref = bf16[4,272,128]{2,1,0:T(8,128)(2,1)S(1)} all-to-all(bf16[4,272,128]{2,1,0:T(8,128)(2,1)S(1)} %shard_map.103), channel_id=1, replica_groups=mesh['ylo'=2,'zh'=4,'zl'=4,'yhi'=2,'x'=4,'core'=2] {'zl'}, dimensions={0} | all-to-all | bytes 557056 | tf_op jit(solution)/shard_map/all_to_all | solution.py:62
  107.2 0.2 shard_map.104
  107.5 21.4 %all_to_all.41.got_ref = bf16[4,272,128]{2,1,0:T(8,128)(2,1)S(1)} all-to-all(bf16[4,272,128]{2,1,0:T(8,128)(2,1)S(1)} %shard_map.104), channel_id=1, replica_groups=mesh['ylo'=2,'zh'=4,'zl'=4,'yhi'=2,'x'=4,'core'=2] {'zh'}, dimensions={0} | all-to-all | bytes 557056 | tf_op jit(solution)/shard_map/all_to_all | solution.py:62
  128.9 0.9 shard_map.105
  129.8 9.1 %all-to-all-start.6 = ((bf16[8,128,128]{2,1,0:T(8,128)(2,1)}), bf16[8,128,128]{2,1,0:T(8,128)(2,1)S(1)}, u32[]{:S(2)}, u32[]{:S(2)}) async-start(bf16[8,128,128]{2,1,0:T(8,128)(2,1)} %shard_map.105), calls=%async_computation.6 | async-start | bytes 524288 | tf_op jit(solution)/shard_map/all_to_all | solution.py:62
  138.9 0.1 pad_add_fusion.place_ref
  138.9 8.6 %all-to-all-done.6.got_ref = bf16[8,128,128]{2,1,0:T(8,128)(2,1)S(1)} async-done(((bf16[8,128,128]{2,1,0:T(8,128)(2,1)}), bf16[8,128,128]{2,1,0:T(8,128)(2,1)S(1)}, u32[]{:S(2)}, u32[]{:S(2)}) %all-to-all-start.6) | async-done | bytes 262176 | tf_op jit(solution)/shard_map/all_to_all | solution.py:62
  147.6 0.8 shard_map.106
  148.4 10.2 %all_to_all.42 = bf16[16,32,256]{2,1,0:T(8,128)(2,1)S(1)} all-to-all(bf16[16,32,256]{2,1,0:T(8,128)(2,1)S(1)} %shard_map.106), channel_id=1, replica_groups=mesh['ylo'=2,'zh'=4,'zl'=4,'yhi'=2,'x'=4,'core'=2] {'ylo','yhi','x'}, dimensions={0} | all-to-all | bytes 524288 | tf_op jit(solution)/shard_map/all_to_all | solution.py:62
  158.6 0.6 reduce_sum.12
  (3 shorter events, 0.1 us)
Async XLA Ops:
  0.0 28.4 %copy-start.1 = (bf16[512,256]{1,0:T(8,128)(2,1)S(1)}, bf16[512,256]{1,0:T(8,128)(2,1)}, u32[]{:S(2)}) copy-start(bf16[512,256]{1,0:T(8,128)(2,1)} %param.15) | copy-start | bytes 786436
  1.5 15.3 %all-to-all-start = ((bf16[16,32,256]{2,1,0:T(8,128)(2,1)}), bf16[16,32,256]{2,1,0:T(8,128)(2,1)S(1)}, u32[]{:S(2)}, u32[]{:S(2)}) async-start(bf16[16,32,256]{2,1,0:T(8,128)(2,1)} %broadcast_in_dim.4), calls=%async_computation | async-start | bytes 524288 | tf_op jit(solution)/shard_map/all_to_all | solution.py:62
  11.6 10.7 %collective-permute-start = (bf16[272,384]{1,0:T(8,128)(2,1)S(1)}, bf16[272,384]{1,0:T(8,128)(2,1)S(1)}, u32[]{:S(2)}, u32[]{:S(2)}) collective-permute-start(bf16[272,384]{1,0:T(8,128)(2,1)S(1)} %fusion.1), channel_id=1, source_target_pairs={{0,256},{256,0},{1,257},{257,1},{2,258},{258,2},{3,259},{259,3},{4... | collective-permute-start | bytes 626696 | tf_op jit(solution)/shard_map/ppermute | solution.py:287
  22.3 1.0 copy-start
  24.7 15.3 %all-to-all-start.1 = ((bf16[4,400,128]{2,1,0:T(8,128)(2,1)}), bf16[4,400,128]{2,1,0:T(8,128)(2,1)S(1)}, u32[]{:S(2)}, u32[]{:S(2)}) async-start(bf16[4,400,128]{2,1,0:T(8,128)(2,1)} %shard_map.100), calls=%async_computation.1 | async-start | bytes 819200 | tf_op jit(solution)/shard_map/all_to_all | solution.py:62
  28.5 12.3 %collective-permute-start.1 = (bf16[256,256]{1,0:T(8,128)(2,1)S(1)}, bf16[256,256]{1,0:T(8,128)(2,1)S(1)}, u32[]{:S(2)}, u32[]{:S(2)}) collective-permute-start(bf16[256,256]{1,0:T(8,128)(2,1)S(1)} %get-tuple-element.22), channel_id=1, source_target_pairs={{0,256},{256,0},{1,257},{257,1},{2,258},{258,2},{3,259},{259,3},{4... | collective-permute-start | bytes 393224 | tf_op jit(solution)/shard_map/ppermute | solution.py:287
  40.7 30.0 %all-to-all-start.2 = ((bf16[4,304,128]{2,1,0:T(8,128)(2,1)}), bf16[4,304,128]{2,1,0:T(8,128)(2,1)S(1)}, u32[]{:S(2)}, u32[]{:S(2)}) async-start(bf16[4,304,128]{2,1,0:T(8,128)(2,1)} %shard_map.101), calls=%async_computation.2 | async-start | bytes 622592 | tf_op jit(solution)/shard_map/all_to_all | solution.py:62
  54.8 28.8 %collective-permute-start.2 = (bf16[2,2048,128]{2,1,0:T(8,128)(2,1)S(1)}, bf16[2,2048,128]{2,1,0:T(8,128)(2,1)S(1)}, u32[]{:S(2)}, u32[]{:S(2)}) collective-permute-start(bf16[2,2048,128]{2,1,0:T(8,128)(2,1)S(1)} %pad_maximum_fusion.kv_ref), channel_id=1, source_target_pairs={{0,256},{256,0},{1,257},{257,1},{2,258},{258,2},{3,259},{259,3},{4... | collective-permute-start | bytes 3145736 | tf_op jit(solution)/shard_map/ppermute | solution.py:287
  72.2 12.5 %all-to-all-start.3 = ((bf16[4,256,128]{2,1,0:T(8,128)(2,1)}), bf16[4,256,128]{2,1,0:T(8,128)(2,1)S(1)}, u32[]{:S(2)}, u32[]{:S(2)}) async-start(bf16[4,256,128]{2,1,0:T(8,128)(2,1)} %get-tuple-element.16), calls=%async_computation.3 | async-start | bytes 524288 | tf_op jit(solution)/shard_map/all_to_all | solution.py:62
  75.7 18.6 %collective-permute-start.4 = (bf16[2,256,256]{2,1,0:T(8,128)(2,1)S(1)}, bf16[2,256,256]{2,1,0:T(8,128)(2,1)S(1)}, u32[]{:S(2)}, u32[]{:S(2)}) collective-permute-start(bf16[2,256,256]{2,1,0:T(8,128)(2,1)S(1)} %pad_maximum_fusion.1.own_ref), channel_id=1, source_target_pairs={{0,1},{1,0},{2,3},{3,2},{4,5},{5,4},{6,7},{7,6},{8,9},{9,8},{10,11... | collective-permute-start | bytes 786440 | tf_op jit(solution)/shard_map/ppermute | solution.py:287
  81.6 3.1 %collective-permute-start.3 = (bf16[32,128]{1,0:T(8,128)(2,1)S(1)}, bf16[32,128]{1,0:T(8,128)(2,1)S(1)}, u32[]{:S(2)}, u32[]{:S(2)}) collective-permute-start(bf16[32,128]{1,0:T(8,128)(2,1)S(1)} %get-tuple-element.17.own_ref), channel_id=1, source_target_pairs={{0,1},{1,0},{2,3},{3,2},{4,5},{5,4},{6,7},{7,6},{8,9},{9,8},{10,11... | collective-permute-start | bytes 24584 | tf_op jit(solution)/shard_map/ppermute | solution.py:287
  129.8 17.8 %all-to-all-start.6 = ((bf16[8,128,128]{2,1,0:T(8,128)(2,1)}), bf16[8,128,128]{2,1,0:T(8,128)(2,1)S(1)}, u32[]{:S(2)}, u32[]{:S(2)}) async-start(bf16[8,128,128]{2,1,0:T(8,128)(2,1)} %shard_map.105), calls=%async_computation.6 | async-start | bytes 524288 | tf_op jit(solution)/shard_map/all_to_all | solution.py:62

commit v5 on v4

--- a/solution.py
+++ b/solution.py
@@ -124,7 +124,7 @@
         blocks = [tok_ref[core, side, j] for j in range(CHIPS // PAIR) for core in range(2)]
         toks.append(jnp.concatenate(blocks, axis=0))
     scaled = [(t.astype(f32) * g.astype(f32)).astype(bf16) for t, g in zip(toks, gains)]
-    panels = [w_ref[:, pl.ds(pl.multiple_of(mine * HEAD_COLS, HEAD_COLS), HEAD_COLS)], kv_ref[...]]
+    panels = [w_ref[...], kv_ref[...]]
     for i, panel in enumerate(panels):
         width = panel.shape[1]
         other = far_ref[:PANEL, HEAD_COLS * i : HEAD_COLS * i + width]
@@ -186,7 +186,8 @@
 def attend_kernel(place_ref, q_ref, kv_ref, other_ref, own_ref, swap_ref, out_ref):
     contract = (((1,), (1,)), ((), ()))
     zeros = jnp.zeros((HEAD_WIDTH - TOK_ROW, HEAD_WIDTH), bf16)
-    even = place_ref[1] == 0
+    core = place_ref[1]
+    even = core == 0
     own, swap = own_ref[...].astype(f32), swap_ref[...].astype(f32)
     new_k = jnp.concatenate([jnp.where(even, own, swap).astype(bf16), zeros], axis=0)
     new_v = jnp.concatenate([jnp.where(even, swap, own).astype(bf16), zeros], axis=0)
@@ -198,7 +199,7 @@
         q = q_ref[n]
         s = [
             lax.dot_general(q, kv_ref[0], contract, preferred_element_type=f32),
-            lax.dot_general(q, other_ref[0], contract, preferred_element_type=f32),
+            lax.dot_general(q, other_ref[core], contract, preferred_element_type=f32),
         ]
         fresh = lax.dot_general(q, new_k, contract, preferred_element_type=f32)
         token = n * TOK_NEAR + lax.rem(line, TOK_NEAR)
@@ -208,7 +209,7 @@
         base = top * SCORE_SCALE
         denom = jnp.zeros_like(base)
         numer = jnp.zeros((Q_ROWS, HEAD_WIDTH), f32)
-        for x, v in zip(s, (kv_ref[1], other_ref[1], new_v)):
+        for x, v in zip(s, (kv_ref[1], other_ref[1 - core], new_v)):
             w = jnp.exp2(x * SCORE_SCALE - base)
             denom = denom + jnp.sum(w, axis=1, keepdims=True)
             numer = numer + jnp.dot(w.astype(bf16), v, preferred_element_type=f32)
@@ -304,25 +305,30 @@
     w_far = lax.dynamic_slice_in_dim(w_query, (1 - mine) * HEAD_COLS, HEAD_COLS, 1)
     w_far = jnp.concatenate([w_far, kv_panel], axis=1)
     gain_row = jnp.pad(norm_gain[None], ((0, PAD - 1), (0, w_far.shape[1] - norm_gain.shape[0])))
-    w_far = trade(jnp.concatenate([w_far, gain_row], axis=0), "ylo")
+    w_far = jnp.concatenate([w_far, gain_row], axis=0)
+    w_own = lax.dynamic_slice_in_dim(w_query, mine * HEAD_COLS, HEAD_COLS, 1)
+    tokens, w_far, w_own = lax.optimization_barrier((tokens, w_far, w_own))
+    w_far = trade(w_far, "ylo")
     whole = lax.all_gather(spread(tokens, CHIPS, PLANE), "core", axis=0)
     whole = whole.reshape((2, PAIR, CHIPS // PAIR) + tokens.shape)
-    kv_own = jnp.stack([panel(cached_keys), panel(cached_values)])
-    kv_far = trade(kv_own, "ylo")
     pay = run(
         project_kernel,
         shape(NEAR_SIZE, Q_ROWS + TOK_NEAR + PAD, HEAD_WIDTH),
-        whole, norm_gain[None], w_query, kv_panel, w_far,
+        whole, norm_gain[None], w_own, kv_panel, w_far,
         scalars=place(mine),
     )
-    pay, w_out = lax.optimization_barrier((pay, w_out))
+    pay, group = lax.optimization_barrier((pay, group))
+    kv_far = trade(jnp.where(core == 0, panel(cached_keys), panel(cached_values)), "ylo")
+    got = exchange(pay, "zl")
+    pay = run(reduce_kernel, shape(FAR_SIZE, Q_ROWS + TOK_ROW + PAD, HEAD_WIDTH), got)
+    pay, kv_far, w_out, group = lax.optimization_barrier((pay, kv_far, w_out, group))
+    kv_far = jnp.stack([kv_far, trade(kv_far, "core")])
+    kv_own = jnp.stack([panel(cached_keys), panel(cached_values)])
     o_own = lax.dynamic_slice_in_dim(w_out, mine * HEAD_COLS, HEAD_COLS, 0)
     o_far = trade(lax.dynamic_slice_in_dim(w_out, (1 - mine) * HEAD_COLS, HEAD_COLS, 0), "ylo")
-    got = exchange(pay, "zl")
-    pay = run(reduce_kernel, shape(FAR_SIZE, Q_ROWS + TOK_ROW + PAD, HEAD_WIDTH), got)
-    pay, o_far = lax.optimization_barrier((pay, o_far))
     o_own = jnp.stack([o_own, o_far])
     got = exchange(pay, "zh")
+    got, kv_own, kv_far, o_own = lax.optimization_barrier((got, kv_own, kv_far, o_own))
 
     start = near * TOK_NEAR
     first = start + far * TOK_ROW

time: 160 us -> 167 us (1.044)
  starting transfers between devices: 51.5 us -> 60.1 us
  waiting for transfers between devices: 33.4 us -> 29.5 us
  other arithmetic: 1.93 us -> 4.42 us
    all_to_all x5, waiting for transfers between devices: 32.4 us -> 21.1 us  [exchange(): return lax.all_to_all(x, axes, 0, 0, tiled=True)]
    all_to_all x5, starting transfers between devices: 36.5 us -> 44.1 us  [exchange(): return lax.all_to_all(x, axes, 0, 0, tiled=True)]
    ppermute x5 -> x6, waiting for transfers between devices: 1.07 us -> 8.37 us  [trade(): return lax.ppermute(x, axis, [(0, 1), (1, 0)])]
    ppermute x5 -> x6, starting transfers between devices: 15.1 us -> 16 us  [trade(): return lax.ppermute(x, axis, [(0, 1), (1, 0)])]
  transfers between devices with their start and end apart: 10 -> 11, of which waited for: 5 -> 7; matrix products, arithmetic and copies ran while one was open for 4% -> 3% of each run, Pallas kernels for 7% -> 6%
where the time goes in v5:
time: 167 us; the launch traced here: 166 us
  starting transfers between devices  60.1 us (36%)
  blocking collectives  50.8 us (30%)
  waiting for transfers between devices  29.5 us (18%)
  Pallas kernels  15.2 us (9%)
  local copies, waits for them, and re-layouts  6.08 us (4%)
  other arithmetic  4.42 us (3%)
    all_to_all x3, blocking collectives, exchange(): return lax.all_to_all(x, axes, 0, 0, tiled=True)  45.1 us
    all_to_all x5, starting transfers between devices, exchange(): return lax.all_to_all(x, axes, 0, 0, tiled=True)  44.1 us
    all_to_all x5, waiting for transfers between devices, exchange(): return lax.all_to_all(x, axes, 0, 0, tiled=True)  21.1 us
    ppermute x6, starting transfers between devices, trade(): return lax.ppermute(x, axis, [(0, 1), (1, 0)])  16 us
    pallas_call x7, Pallas kernels, run(): pl.pallas_call(kernel, out_shape=shapes, in_specs=[smem] * len(scalars) +...  15.2 us
    ppermute x6, waiting for transfers between devices, trade(): return lax.ppermute(x, axis, [(0, 1), (1, 0)])  8.37 us
    all_gather x1, blocking collectives, body(): whole = lax.all_gather(spread(tokens, CHIPS, PLANE), 'core', axis=0)  5.73 us
  transfers between devices with their start and end apart: 11, of which 7 were waited for; matrix products, arithmetic and copies ran while one was open for 3% of the time, Pallas kernels for 6%

profile of v5, /device:TPU:1, one launch (start us, length us, event | category | flops | bytes accessed | tf_op | source)
XLA Modules:
  0.0 166.3 jit_solution(10004598883670266881)
XLA Ops:
  0.0 0.7 broadcast_in_dim.4.gain_ref
  0.7 1.0 constant_dynamic-slice_fusion.5
  1.7 0.9 dynamic-slice_select_fusion.1.kv_ref
  2.6 1.4 broadcast_in_dim.5
  4.1 7.6 %all-to-all-start = ((bf16[16,32,256]{2,1,0:T(8,128)(2,1)}), bf16[16,32,256]{2,1,0:T(8,128)(2,1)S(1)}, u32[]{:S(2)}, u32[]{:S(2)}) async-start(bf16[16,32,256]{2,1,0:T(8,128)(2,1)} %broadcast_in_dim.5), calls=%async_computation | async-start | bytes 524288 | tf_op jit(solution)/shard_map/all_to_all | solution.py:62
  11.7 3.3 %collective-permute-start = (bf16[272,384]{1,0:T(8,128)(2,1)S(1)}, bf16[272,384]{1,0:T(8,128)(2,1)S(1)}, u32[]{:S(2)}, u32[]{:S(2)}) collective-permute-start(bf16[272,384]{1,0:T(8,128)(2,1)S(1)} %fusion.1), channel_id=1, source_target_pairs={{0,256},{256,0},{1,257},{257,1},{2,258},{258,2},{3,259},{259,3},{4... | collective-permute-start | bytes 626696 | tf_op jit(solution)/shard_map/ppermute | solution.py:288
  14.9 4.3 %all-to-all-done = bf16[16,32,256]{2,1,0:T(8,128)(2,1)S(1)} async-done(((bf16[16,32,256]{2,1,0:T(8,128)(2,1)}), bf16[16,32,256]{2,1,0:T(8,128)(2,1)S(1)}, u32[]{:S(2)}, u32[]{:S(2)}) %all-to-all-start) | async-done | bytes 262176 | tf_op jit(solution)/shard_map/all_to_all | solution.py:62
  19.2 5.7 %all-gather = bf16[32,32,256]{2,1,0:T(8,128)(2,1)S(1)} all-gather(bf16[16,32,256]{2,1,0:T(8,128)(2,1)S(1)} %all-to-all-done), channel_id=2, replica_groups=mesh['ylo'=2,'zh'=4,'zl'=4,'yhi'=2,'x'=4,'core'=2] {'core'}, dimensions={0}, use_global_device_ids=true | all-gather | bytes 786432 | tf_op jit(solution)/shard_map/all_gather | solution.py:312
  24.9 0.0 collective-permute-done.far_ref
  24.9 1.3 shard_map.100
  26.3 3.8 %all-to-all-start.1 = ((bf16[4,400,128]{2,1,0:T(8,128)(2,1)}), bf16[4,400,128]{2,1,0:T(8,128)(2,1)S(1)}, u32[]{:S(2)}, u32[]{:S(2)}) async-start(bf16[4,400,128]{2,1,0:T(8,128)(2,1)} %shard_map.100), calls=%async_computation.1 | async-start | bytes 819200 | tf_op jit(solution)/shard_map/all_to_all | solution.py:62
  30.1 1.4 dynamic-slice_select_fusion
  31.5 2.0 %collective-permute-start.1 = (bf16[2048,128]{1,0:T(8,128)(2,1)S(1)}, bf16[2048,128]{1,0:T(8,128)(2,1)S(1)}, u32[]{:S(2)}, u32[]{:S(2)}) collective-permute-start(bf16[2048,128]{1,0:T(8,128)(2,1)S(1)} %dynamic-slice_select_fusion), channel_id=1, source_target_pairs={{0,256},{256,0},{1,257},{257,1},{2,258},{258,2},{3,259},{259,3},{4... | collective-permute-start | bytes 1572872 | tf_op jit(solution)/shard_map/ppermute | solution.py:288
  33.5 0.1 pad_add_fusion.2.place_ref
  33.6 0.7 constant_dynamic-slice_fusion
  34.3 0.9 constant_dynamic-slice_fusion.2
  35.2 6.5 %all-to-all-done.1.got_ref = bf16[4,400,128]{2,1,0:T(8,128)(2,1)S(1)} async-done(((bf16[4,400,128]{2,1,0:T(8,128)(2,1)}), bf16[4,400,128]{2,1,0:T(8,128)(2,1)S(1)}, u32[]{:S(2)}, u32[]{:S(2)}) %all-to-all-start.1) | async-done | bytes 409632 | tf_op jit(solution)/shard_map/all_to_all | solution.py:62
  41.7 0.8 shard_map.101
  42.5 3.7 %collective-permute-done.1 = bf16[2048,128]{1,0:T(8,128)(2,1)S(1)} collective-permute-done((bf16[2048,128]{1,0:T(8,128)(2,1)S(1)}, bf16[2048,128]{1,0:T(8,128)(2,1)S(1)}, u32[]{:S(2)}, u32[]{:S(2)}) %collective-permute-start.1) | collective-permute-done | bytes 524320 | tf_op jit(solution)/shard_map/ppermute | solution.py:288
  46.2 13.0 %all-to-all-start.2 = ((bf16[4,304,128]{2,1,0:T(8,128)(2,1)}), bf16[4,304,128]{2,1,0:T(8,128)(2,1)S(1)}, u32[]{:S(2)}, u32[]{:S(2)}) async-start(bf16[4,304,128]{2,1,0:T(8,128)(2,1)} %shard_map.101), calls=%async_computation.2 | async-start | bytes 622592 | tf_op jit(solution)/shard_map/all_to_all | solution.py:62
  59.2 3.4 %collective-permute-start.2 = (bf16[2048,128]{1,0:T(8,128)(2,1)S(1)}, bf16[2048,128]{1,0:T(8,128)(2,1)}, u32[]{:S(2)}, u32[]{:S(2)}) collective-permute-start(bf16[2048,128]{1,0:T(8,128)(2,1)S(1)} %collective-permute-done.1), channel_id=1, source_target_pairs={{0,1},{1,0},{2,3},{3,2},{4,5},{5,4},{6,7},{7,6},{8,9},{9,8},{10,11... | collective-permute-start | bytes 1572872 | tf_op jit(solution)/shard_map/ppermute | solution.py:288
  62.6 0.0 copy-done
  62.6 2.0 %collective-permute-start.3 = (bf16[256,256]{1,0:T(8,128)(2,1)S(1)}, bf16[256,256]{1,0:T(8,128)(2,1)S(1)}, u32[]{:S(2)}, u32[]{:S(2)}) collective-permute-start(bf16[256,256]{1,0:T(8,128)(2,1)S(1)} %get-tuple-element.40), channel_id=1, source_target_pairs={{0,256},{256,0},{1,257},{257,1},{2,258},{258,2},{3,259},{259,3},{4... | collective-permute-start | bytes 393224 | tf_op jit(solution)/shard_map/ppermute | solution.py:288
  64.6 1.3 dynamic-slice_bitcast_fusion
  65.9 0.1 pad_maximum_fusion.kv_ref
  66.0 3.6 %collective-permute-done.3 = bf16[256,256]{1,0:T(8,128)(2,1)S(1)} collective-permute-done((bf16[256,256]{1,0:T(8,128)(2,1)S(1)}, bf16[256,256]{1,0:T(8,128)(2,1)S(1)}, u32[]{:S(2)}, u32[]{:S(2)}) %collective-permute-start.3) | collective-permute-done | bytes 131104 | tf_op jit(solution)/shard_map/ppermute | solution.py:288
  69.6 0.0 collective-permute-done.2
  69.6 1.1 pad_maximum_fusion.1.other_ref
  70.8 1.7 %all-to-all-done.2.got_ref = bf16[4,304,128]{2,1,0:T(8,128)(2,1)S(1)} async-done(((bf16[4,304,128]{2,1,0:T(8,128)(2,1)}), bf16[4,304,128]{2,1,0:T(8,128)(2,1)S(1)}, u32[]{:S(2)}, u32[]{:S(2)}) %all-to-all-start.2) | async-done | bytes 311328 | tf_op jit(solution)/shard_map/all_to_all | solution.py:62
  72.5 1.4 shard_map.102
  74.0 11.6 %all-to-all-start.3 = ((bf16[4,256,128]{2,1,0:T(8,128)(2,1)}), bf16[4,256,128]{2,1,0:T(8,128)(2,1)S(1)}, u32[]{:S(2)}, u32[]{:S(2)}) async-start(bf16[4,256,128]{2,1,0:T(8,128)(2,1)} %get-tuple-element.32), calls=%async_computation.3 | async-start | bytes 524288 | tf_op jit(solution)/shard_map/all_to_all | solution.py:62
  85.6 3.4 %collective-permute-start.5 = (bf16[2,256,256]{2,1,0:T(8,128)(2,1)S(1)}, bf16[2,256,256]{2,1,0:T(8,128)(2,1)S(1)}, u32[]{:S(2)}, u32[]{:S(2)}) collective-permute-start(bf16[2,256,256]{2,1,0:T(8,128)(2,1)S(1)} %pad_maximum_fusion.2.own_ref), channel_id=1, source_target_pairs={{0,1},{1,0},{2,3},{3,2},{4,5},{5,4},{6,7},{7,6},{8,9},{9,8},{10,11... | collective-permute-start | bytes 786440 | tf_op jit(solution)/shard_map/ppermute | solution.py:288
  88.9 1.9 %collective-permute-start.4 = (bf16[32,128]{1,0:T(8,128)(2,1)S(1)}, bf16[32,128]{1,0:T(8,128)(2,1)S(1)}, u32[]{:S(2)}, u32[]{:S(2)}) collective-permute-start(bf16[32,128]{1,0:T(8,128)(2,1)S(1)} %get-tuple-element.35.own_ref), channel_id=1, source_target_pairs={{0,1},{1,0},{2,3},{3,2},{4,5},{5,4},{6,7},{7,6},{8,9},{9,8},{10,11... | collective-permute-start | bytes 24584 | tf_op jit(solution)/shard_map/ppermute | solution.py:288
  90.9 0.1 pad_add_fusion.1.place_ref
  90.9 1.1 collective-permute-done.4.swap_ref
  92.0 0.0 all-to-all-done.3.q_ref
  92.0 9.6 %shard_map.103 = bf16[4,272,128]{2,1,0:T(8,128)(2,1)S(1)} custom-call(s32[2]{0:T(128)S(1)} %pad_add_fusion.1.place_ref, bf16[4,256,128]{2,1,0:T(8,128)(2,1)S(1)} %all-to-all-done.3.q_ref, bf16[2,2048,128]{2,1,0:T(8,128)(2,1)S(1)} %pad_maximum_fusion.kv_ref, bf16[2,2048,128]{2,1,0:T(8,128)(2,1)S(1)} %pad_maximum_fusion.1.other_ref, ...), custom_call_target="tpu_custom_call" | custom-call | tf_op jit(solution)/shard_map/pallas_call | solution.py:72
  101.6 0.0 collective-permute-done.5.swap_ref
  101.7 11.9 %all_to_all.40.got_ref = bf16[4,272,128]{2,1,0:T(8,128)(2,1)S(1)} all-to-all(bf16[4,272,128]{2,1,0:T(8,128)(2,1)S(1)} %shard_map.103), channel_id=1, replica_groups=mesh['ylo'=2,'zh'=4,'zl'=4,'yhi'=2,'x'=4,'core'=2] {'zl'}, dimensions={0} | all-to-all | bytes 557056 | tf_op jit(solution)/shard_map/all_to_all | solution.py:62
  113.5 0.2 shard_map.104
  113.8 22.2 %all_to_all.41.got_ref = bf16[4,272,128]{2,1,0:T(8,128)(2,1)S(1)} all-to-all(bf16[4,272,128]{2,1,0:T(8,128)(2,1)S(1)} %shard_map.104), channel_id=1, replica_groups=mesh['ylo'=2,'zh'=4,'zl'=4,'yhi'=2,'x'=4,'core'=2] {'zh'}, dimensions={0} | all-to-all | bytes 557056 | tf_op jit(solution)/shard_map/all_to_all | solution.py:62
  135.9 0.9 shard_map.105
  136.9 8.2 %all-to-all-start.6 = ((bf16[8,128,128]{2,1,0:T(8,128)(2,1)}), bf16[8,128,128]{2,1,0:T(8,128)(2,1)S(1)}, u32[]{:S(2)}, u32[]{:S(2)}) async-start(bf16[8,128,128]{2,1,0:T(8,128)(2,1)} %shard_map.105), calls=%async_computation.6 | async-start | bytes 524288 | tf_op jit(solution)/shard_map/all_to_all | solution.py:62
  145.0 0.1 pad_add_fusion.place_ref
  145.1 8.7 %all-to-all-done.6.got_ref = bf16[8,128,128]{2,1,0:T(8,128)(2,1)S(1)} async-done(((bf16[8,128,128]{2,1,0:T(8,128)(2,1)}), bf16[8,128,128]{2,1,0:T(8,128)(2,1)S(1)}, u32[]{:S(2)}, u32[]{:S(2)}) %all-to-all-start.6) | async-done | bytes 262176 | tf_op jit(solution)/shard_map/all_to_all | solution.py:62
  153.8 0.9 shard_map.106
  154.6 11.1 %all_to_all.42 = bf16[16,32,256]{2,1,0:T(8,128)(2,1)S(1)} all-to-all(bf16[16,32,256]{2,1,0:T(8,128)(2,1)S(1)} %shard_map.106), channel_id=1, replica_groups=mesh['ylo'=2,'zh'=4,'zl'=4,'yhi'=2,'x'=4,'core'=2] {'ylo','yhi','x'}, dimensions={0} | all-to-all | bytes 524288 | tf_op jit(solution)/shard_map/all_to_all | solution.py:62
  165.7 0.6 reduce_sum.12
  (4 shorter events, 0.1 us)
Async XLA Ops:
  0.0 62.6 %copy-start = (bf16[512,256]{1,0:T(8,128)(2,1)S(1)}, bf16[512,256]{1,0:T(8,128)(2,1)}, u32[]{:S(2)}) copy-start(bf16[512,256]{1,0:T(8,128)(2,1)} %param.15) | copy-start | bytes 786436
  4.1 15.1 %all-to-all-start = ((bf16[16,32,256]{2,1,0:T(8,128)(2,1)}), bf16[16,32,256]{2,1,0:T(8,128)(2,1)S(1)}, u32[]{:S(2)}, u32[]{:S(2)}) async-start(bf16[16,32,256]{2,1,0:T(8,128)(2,1)} %broadcast_in_dim.5), calls=%async_computation | async-start | bytes 524288 | tf_op jit(solution)/shard_map/all_to_all | solution.py:62
  11.7 13.3 %collective-permute-start = (bf16[272,384]{1,0:T(8,128)(2,1)S(1)}, bf16[272,384]{1,0:T(8,128)(2,1)S(1)}, u32[]{:S(2)}, u32[]{:S(2)}) collective-permute-start(bf16[272,384]{1,0:T(8,128)(2,1)S(1)} %fusion.1), channel_id=1, source_target_pairs={{0,256},{256,0},{1,257},{257,1},{2,258},{258,2},{3,259},{259,3},{4... | collective-permute-start | bytes 626696 | tf_op jit(solution)/shard_map/ppermute | solution.py:288
  26.3 15.4 %all-to-all-start.1 = ((bf16[4,400,128]{2,1,0:T(8,128)(2,1)}), bf16[4,400,128]{2,1,0:T(8,128)(2,1)S(1)}, u32[]{:S(2)}, u32[]{:S(2)}) async-start(bf16[4,400,128]{2,1,0:T(8,128)(2,1)} %shard_map.100), calls=%async_computation.1 | async-start | bytes 819200 | tf_op jit(solution)/shard_map/all_to_all | solution.py:62
  31.5 14.7 %collective-permute-start.1 = (bf16[2048,128]{1,0:T(8,128)(2,1)S(1)}, bf16[2048,128]{1,0:T(8,128)(2,1)S(1)}, u32[]{:S(2)}, u32[]{:S(2)}) collective-permute-start(bf16[2048,128]{1,0:T(8,128)(2,1)S(1)} %dynamic-slice_select_fusion), channel_id=1, source_target_pairs={{0,256},{256,0},{1,257},{257,1},{2,258},{258,2},{3,259},{259,3},{4... | collective-permute-start | bytes 1572872 | tf_op jit(solution)/shard_map/ppermute | solution.py:288
  46.2 26.3 %all-to-all-start.2 = ((bf16[4,304,128]{2,1,0:T(8,128)(2,1)}), bf16[4,304,128]{2,1,0:T(8,128)(2,1)S(1)}, u32[]{:S(2)}, u32[]{:S(2)}) async-start(bf16[4,304,128]{2,1,0:T(8,128)(2,1)} %shard_map.101), calls=%async_computation.2 | async-start | bytes 622592 | tf_op jit(solution)/shard_map/all_to_all | solution.py:62
  59.2 10.5 %collective-permute-start.2 = (bf16[2048,128]{1,0:T(8,128)(2,1)S(1)}, bf16[2048,128]{1,0:T(8,128)(2,1)}, u32[]{:S(2)}, u32[]{:S(2)}) collective-permute-start(bf16[2048,128]{1,0:T(8,128)(2,1)S(1)} %collective-permute-done.1), channel_id=1, source_target_pairs={{0,1},{1,0},{2,3},{3,2},{4,5},{5,4},{6,7},{7,6},{8,9},{9,8},{10,11... | collective-permute-start | bytes 1572872 | tf_op jit(solution)/shard_map/ppermute | solution.py:288
  62.6 7.0 %collective-permute-start.3 = (bf16[256,256]{1,0:T(8,128)(2,1)S(1)}, bf16[256,256]{1,0:T(8,128)(2,1)S(1)}, u32[]{:S(2)}, u32[]{:S(2)}) collective-permute-start(bf16[256,256]{1,0:T(8,128)(2,1)S(1)} %get-tuple-element.40), channel_id=1, source_target_pairs={{0,256},{256,0},{1,257},{257,1},{2,258},{258,2},{3,259},{259,3},{4... | collective-permute-start | bytes 393224 | tf_op jit(solution)/shard_map/ppermute | solution.py:288
  74.0 18.0 %all-to-all-start.3 = ((bf16[4,256,128]{2,1,0:T(8,128)(2,1)}), bf16[4,256,128]{2,1,0:T(8,128)(2,1)S(1)}, u32[]{:S(2)}, u32[]{:S(2)}) async-start(bf16[4,256,128]{2,1,0:T(8,128)(2,1)} %get-tuple-element.32), calls=%async_computation.3 | async-start | bytes 524288 | tf_op jit(solution)/shard_map/all_to_all | solution.py:62
  85.6 16.1 %collective-permute-start.5 = (bf16[2,256,256]{2,1,0:T(8,128)(2,1)S(1)}, bf16[2,256,256]{2,1,0:T(8,128)(2,1)S(1)}, u32[]{:S(2)}, u32[]{:S(2)}) collective-permute-start(bf16[2,256,256]{2,1,0:T(8,128)(2,1)S(1)} %pad_maximum_fusion.2.own_ref), channel_id=1, source_target_pairs={{0,1},{1,0},{2,3},{3,2},{4,5},{5,4},{6,7},{7,6},{8,9},{9,8},{10,11... | collective-permute-start | bytes 786440 | tf_op jit(solution)/shard_map/ppermute | solution.py:288
  88.9 3.1 %collective-permute-start.4 = (bf16[32,128]{1,0:T(8,128)(2,1)S(1)}, bf16[32,128]{1,0:T(8,128)(2,1)S(1)}, u32[]{:S(2)}, u32[]{:S(2)}) collective-permute-start(bf16[32,128]{1,0:T(8,128)(2,1)S(1)} %get-tuple-element.35.own_ref), channel_id=1, source_target_pairs={{0,1},{1,0},{2,3},{3,2},{4,5},{5,4},{6,7},{7,6},{8,9},{9,8},{10,11... | collective-permute-start | bytes 24584 | tf_op jit(solution)/shard_map/ppermute | solution.py:288
  136.9 16.9 %all-to-all-start.6 = ((bf16[8,128,128]{2,1,0:T(8,128)(2,1)}), bf16[8,128,128]{2,1,0:T(8,128)(2,1)S(1)}, u32[]{:S(2)}, u32[]{:S(2)}) async-start(bf16[8,128,128]{2,1,0:T(8,128)(2,1)} %shard_map.105), calls=%async_computation.6 | async-start | bytes 524288 | tf_op jit(solution)/shard_map/all_to_all | solution.py:62

commit v6 on v4

--- a/solution.py
+++ b/solution.py
@@ -62,10 +62,6 @@
     return lax.all_to_all(x, axes, 0, 0, tiled=True)
 
 
-def spread(x, count, axes):
-    return exchange(jnp.broadcast_to(x[None], (count,) + x.shape), axes)
-
-
 def run(kernel, shapes, *args, scratch=(), scalars=()):
     spec = pl.BlockSpec(memory_space=pltpu.VMEM)
     smem = pl.BlockSpec(memory_space=pltpu.SMEM)
@@ -116,6 +112,11 @@
     return jnp.sum(jnp.where(same(n, n), wide, 0.0), axis=0, keepdims=True)
 
 
+def copies_kernel(x_ref, out_ref):
+    for i in range(CHIPS):
+        out_ref[i] = x_ref[...]
+
+
 def project_kernel(pair_ref, tok_ref, gain_ref, w_ref, kv_ref, far_ref, out_ref):
     mine = pair_ref[0]
     gains = [gain_ref[...], far_ref[PANEL : PANEL + 1, :PANEL]]
@@ -124,7 +125,7 @@
         blocks = [tok_ref[core, side, j] for j in range(CHIPS // PAIR) for core in range(2)]
         toks.append(jnp.concatenate(blocks, axis=0))
     scaled = [(t.astype(f32) * g.astype(f32)).astype(bf16) for t, g in zip(toks, gains)]
-    panels = [w_ref[:, pl.ds(pl.multiple_of(mine * HEAD_COLS, HEAD_COLS), HEAD_COLS)], kv_ref[...]]
+    panels = [w_ref[...], kv_ref[...]]
     for i, panel in enumerate(panels):
         width = panel.shape[1]
         other = far_ref[:PANEL, HEAD_COLS * i : HEAD_COLS * i + width]
@@ -190,36 +191,36 @@
     own, swap = own_ref[...].astype(f32), swap_ref[...].astype(f32)
     new_k = jnp.concatenate([jnp.where(even, own, swap).astype(bf16), zeros], axis=0)
     new_v = jnp.concatenate([jnp.where(even, swap, own).astype(bf16), zeros], axis=0)
-    slot = lax.broadcasted_iota(jnp.int32, (Q_ROWS, HEAD_WIDTH), 1)
-    line = lax.broadcasted_iota(jnp.int32, (Q_ROWS, HEAD_WIDTH), 0)
+    rows = 2 * Q_ROWS
+    slot = lax.broadcasted_iota(jnp.int32, (rows, HEAD_WIDTH), 1)
+    line = lax.broadcasted_iota(jnp.int32, (rows, HEAD_WIDTH), 0)
     new_token = jnp.where(slot < TOK_ROW, place_ref[0] + slot, BLOCK_TOKENS)
-
-    def block(n, carry):
-        q = q_ref[n]
-        s = [
-            lax.dot_general(q, kv_ref[0], contract, preferred_element_type=f32),
-            lax.dot_general(q, other_ref[0], contract, preferred_element_type=f32),
-        ]
-        fresh = lax.dot_general(q, new_k, contract, preferred_element_type=f32)
-        token = n * TOK_NEAR + lax.rem(line, TOK_NEAR)
-        s.append(jnp.where(new_token <= token, fresh, -jnp.inf))
-        tops = [jnp.max(x, axis=1, keepdims=True) for x in s]
-        top = jnp.maximum(jnp.maximum(tops[0], tops[1]), tops[2])
-        base = top * SCORE_SCALE
-        denom = jnp.zeros_like(base)
-        numer = jnp.zeros((Q_ROWS, HEAD_WIDTH), f32)
-        for x, v in zip(s, (kv_ref[1], other_ref[1], new_v)):
-            w = jnp.exp2(x * SCORE_SCALE - base)
-            denom = denom + jnp.sum(w, axis=1, keepdims=True)
-            numer = numer + jnp.dot(w.astype(bf16), v, preferred_element_type=f32)
-        out_ref[n, :Q_ROWS, :] = (numer / denom).astype(bf16)
-        lse = base * LN2 + jnp.log(denom)
-        lo = parts3(to_row(lse[:HEAD_WIDTH]))
-        hi = parts3(to_row(lse[HEAD_WIDTH:]))
-        out_ref[n, Q_ROWS:, :] = pack_rows([x for pair in zip(lo, hi) for x in pair])
-        return carry
-
-    lax.fori_loop(0, NEAR_SIZE, block, 0)
+    at = jnp.where(line < Q_ROWS, 0, TOK_NEAR) + lax.rem(line, TOK_NEAR)
+    for n in range(0, NEAR_SIZE, 2):
+        q = jnp.concatenate([q_ref[n], q_ref[n + 1]], axis=0)
+        top = denom = numer = None
+        for k, v in ((kv_ref[0], kv_ref[1]), (other_ref[0], other_ref[1]), (new_k, new_v)):
+            s = lax.dot_general(q, k, contract, preferred_element_type=f32)
+            if k is new_k:
+                s = jnp.where(new_token <= n * TOK_NEAR + at, s, -jnp.inf)
+            here = jnp.max(s, axis=1, keepdims=True)
+            most = here if top is None else jnp.maximum(top, here)
+            w = jnp.exp2(s * SCORE_SCALE - most * SCORE_SCALE)
+            total = jnp.sum(w, axis=1, keepdims=True)
+            part = jnp.dot(w.astype(bf16), v, preferred_element_type=f32)
+            if top is not None:
+                fade = jnp.exp2((top - most) * SCORE_SCALE)
+                total = denom * fade + total
+                part = numer * fade + part
+            top, denom, numer = most, total, part
+        out = (numer / denom).astype(bf16)
+        lse = top * (SCORE_SCALE * LN2) + jnp.log(denom)
+        for i in range(2):
+            out_ref[n + i, :Q_ROWS, :] = out[i * Q_ROWS : (i + 1) * Q_ROWS]
+            row = i * Q_ROWS
+            lo = parts3(to_row(lse[row : row + HEAD_WIDTH]))
+            hi = parts3(to_row(lse[row + HEAD_WIDTH : row + Q_ROWS]))
+            out_ref[n + i, Q_ROWS:, :] = pack_rows([x for pair in zip(lo, hi) for x in pair])
 
 
 def mix(got_ref, count):
@@ -247,10 +248,9 @@
     halves, lse = mix(got_ref, NEAR_SIZE)
     parts = parts3(lse)
     tile = pack_rows([p[j : j + 1] for p in parts for j in range(2)])
-    for f in range(FAR_SIZE):
-        out_ref[f, :HEAD_WIDTH, :] = halves[0]
-        out_ref[f, HEAD_WIDTH:Q_ROWS, :] = halves[1]
-        out_ref[f, Q_ROWS:, :] = tile
+    out_ref[:HEAD_WIDTH, :] = halves[0]
+    out_ref[HEAD_WIDTH:Q_ROWS, :] = halves[1]
+    out_ref[Q_ROWS:, :] = tile
 
 
 def mix_far_kernel(got_ref, out_ref):
@@ -301,18 +301,19 @@
         return (jnp.stack(xs).astype(jnp.int32),)
 
     kv_panel = jnp.where(core == 0, panel(key_weight), panel(value_weight))
+    w_own = lax.dynamic_slice_in_dim(w_query, mine * HEAD_COLS, HEAD_COLS, 1)
     w_far = lax.dynamic_slice_in_dim(w_query, (1 - mine) * HEAD_COLS, HEAD_COLS, 1)
     w_far = jnp.concatenate([w_far, kv_panel], axis=1)
     gain_row = jnp.pad(norm_gain[None], ((0, PAD - 1), (0, w_far.shape[1] - norm_gain.shape[0])))
     w_far = trade(jnp.concatenate([w_far, gain_row], axis=0), "ylo")
-    whole = lax.all_gather(spread(tokens, CHIPS, PLANE), "core", axis=0)
+    whole = lax.all_gather(exchange(run(copies_kernel, shape(CHIPS, *tokens.shape), tokens), PLANE), "core", axis=0)
     whole = whole.reshape((2, PAIR, CHIPS // PAIR) + tokens.shape)
     kv_own = jnp.stack([panel(cached_keys), panel(cached_values)])
     kv_far = trade(kv_own, "ylo")
     pay = run(
         project_kernel,
         shape(NEAR_SIZE, Q_ROWS + TOK_NEAR + PAD, HEAD_WIDTH),
-        whole, norm_gain[None], w_query, kv_panel, w_far,
+        whole, norm_gain[None], w_own, kv_panel, w_far,
         scalars=place(mine),
     )
     pay, w_out = lax.optimization_barrier((pay, w_out))
@@ -348,7 +349,7 @@
     )
     pay, o_swap = lax.optimization_barrier((pay, o_swap))
     got = exchange(pay, "zl")
-    got = exchange(run(mix_near_kernel, shape(FAR_SIZE, Q_ROWS + PAD, HEAD_WIDTH), got), "zh")
+    got = lax.all_gather(run(mix_near_kernel, shape(Q_ROWS + PAD, HEAD_WIDTH), got), "zh", axis=0)
     got = run(mix_far_kernel, shape(2 * NEAR_SIZE, Q_ROWS // 2, HEAD_WIDTH), got)
     got = exchange(got, ("zl", "core"))
     pay = run(

time: 160 us -> 154 us (0.963)
  Pallas kernels: 15.1 us -> 13.1 us
  starting transfers between devices: 51.5 us -> 49.6 us
  local copies, waits for them, and re-layouts: 6.93 us -> 5.3 us
    all_to_all x3 -> x2, blocking collectives: 44.6 us -> 26 us  [exchange(): return lax.all_to_all(x, axes, 0, 0, tiled=True)]
    all_gather x1 -> x2, blocking collectives: 5.58 us -> 23.7 us  [the longest x1 18.1 us: body(): lax.all_gather(run(mix_near_kernel, shape(Q_ROWS + PAD, HEAD_WIDTH), got)...]
    pallas_call x7 -> x8, Pallas kernels: 15.1 us -> 13.1 us  [run(): pl.pallas_call(kernel, out_shape=shapes, in_specs=[smem] * len(scalars) +...]
    all_to_all x5, starting transfers between devices: 36.5 us -> 34.5 us  [exchange(): return lax.all_to_all(x, axes, 0, 0, tiled=True)]
  transfers between devices with their start and end apart: 10 -> 10, of which waited for: 5 -> 5; matrix products, arithmetic and copies ran while one was open for 4% -> 4% of each run, Pallas kernels for 7% -> 6%
where the time goes in v6:
time: 154 us; the launch traced here: 153 us
  blocking collectives  49.7 us (32%)
  starting transfers between devices  49.6 us (32%)
  waiting for transfers between devices  33.4 us (22%)
  Pallas kernels  13.1 us (9%)
  local copies, waits for them, and re-layouts  5.3 us (3%)
  other arithmetic  1.93 us (1%)
    all_to_all x5, starting transfers between devices, exchange(): return lax.all_to_all(x, axes, 0, 0, tiled=True)  34.5 us
    all_to_all x5, waiting for transfers between devices, exchange(): return lax.all_to_all(x, axes, 0, 0, tiled=True)  32.3 us
    all_to_all x2, blocking collectives, exchange(): return lax.all_to_all(x, axes, 0, 0, tiled=True)  26 us
    all_gather x1, blocking collectives, body(): lax.all_gather(run(mix_near_kernel, shape(Q_ROWS + PAD, HEAD_WIDTH), got)...  18.1 us
    ppermute x5, starting transfers between devices, trade(): return lax.ppermute(x, axis, [(0, 1), (1, 0)])  15.1 us
    pallas_call x8, Pallas kernels, run(): pl.pallas_call(kernel, out_shape=shapes, in_specs=[smem] * len(scalars) +...  13.1 us
    all_gather x1, blocking collectives, body(): lax.all_gather(exchange(run(copies_kernel, shape(CHIPS, *tokens.shape), t...  5.58 us
  transfers between devices with their start and end apart: 10, of which 5 were waited for; matrix products, arithmetic and copies ran while one was open for 4% of the time, Pallas kernels for 6%

profile of v6, /device:TPU:1, one launch (start us, length us, event | category | flops | bytes accessed | tf_op | source)
XLA Modules:
  0.0 153.2 jit_solution(13665729250344913202)
XLA Ops:
  0.0 0.0 copy-start
  0.0 0.7 copy-done
  0.7 0.0 copy-start.1
  0.7 0.7 shard_map.100
  1.4 7.6 %all-to-all-start = ((bf16[16,32,256]{2,1,0:T(8,128)(2,1)}), bf16[16,32,256]{2,1,0:T(8,128)(2,1)S(1)}, u32[]{:S(2)}, u32[]{:S(2)}) async-start(bf16[16,32,256]{2,1,0:T(8,128)(2,1)} %shard_map.100), calls=%async_computation | async-start | bytes 524288 | tf_op jit(solution)/shard_map/all_to_all | solution.py:62
  9.1 1.0 constant_dynamic-slice_fusion.5
  10.0 0.9 dynamic-slice_select_fusion.kv_ref
  11.0 0.7 broadcast_in_dim.4.gain_ref
  11.6 3.3 %collective-permute-start = (bf16[272,384]{1,0:T(8,128)(2,1)S(1)}, bf16[272,384]{1,0:T(8,128)(2,1)S(1)}, u32[]{:S(2)}, u32[]{:S(2)}) collective-permute-start(bf16[272,384]{1,0:T(8,128)(2,1)S(1)} %fusion.1), channel_id=1, source_target_pairs={{0,256},{256,0},{1,257},{257,1},{2,258},{258,2},{3,259},{259,3},{4... | collective-permute-start | bytes 626696 | tf_op jit(solution)/shard_map/ppermute | solution.py:287
  14.9 1.8 %all-to-all-done = bf16[16,32,256]{2,1,0:T(8,128)(2,1)S(1)} async-done(((bf16[16,32,256]{2,1,0:T(8,128)(2,1)}), bf16[16,32,256]{2,1,0:T(8,128)(2,1)S(1)}, u32[]{:S(2)}, u32[]{:S(2)}) %all-to-all-start) | async-done | bytes 262176 | tf_op jit(solution)/shard_map/all_to_all | solution.py:62
  16.7 5.6 %all-gather = bf16[32,32,256]{2,1,0:T(8,128)(2,1)S(1)} all-gather(bf16[16,32,256]{2,1,0:T(8,128)(2,1)S(1)} %all-to-all-done), channel_id=2, replica_groups=mesh['ylo'=2,'zh'=4,'zl'=4,'yhi'=2,'x'=4,'core'=2] {'core'}, dimensions={0}, use_global_device_ids=true | all-gather | bytes 786432 | tf_op jit(solution)/shard_map/all_gather | solution.py:309
  22.3 0.0 collective-permute-done.far_ref
  22.3 1.3 shard_map.101
  23.7 3.8 %all-to-all-start.1 = ((bf16[4,400,128]{2,1,0:T(8,128)(2,1)}), bf16[4,400,128]{2,1,0:T(8,128)(2,1)S(1)}, u32[]{:S(2)}, u32[]{:S(2)}) async-start(bf16[4,400,128]{2,1,0:T(8,128)(2,1)} %shard_map.101), calls=%async_computation.1 | async-start | bytes 819200 | tf_op jit(solution)/shard_map/all_to_all | solution.py:62
  27.4 0.0 copy-done.1
  27.5 2.1 %collective-permute-start.1 = (bf16[256,256]{1,0:T(8,128)(2,1)S(1)}, bf16[256,256]{1,0:T(8,128)(2,1)S(1)}, u32[]{:S(2)}, u32[]{:S(2)}) collective-permute-start(bf16[256,256]{1,0:T(8,128)(2,1)S(1)} %get-tuple-element.22), channel_id=1, source_target_pairs={{0,256},{256,0},{1,257},{257,1},{2,258},{258,2},{3,259},{259,3},{4... | collective-permute-start | bytes 393224 | tf_op jit(solution)/shard_map/ppermute | solution.py:287
  29.5 9.4 %all-to-all-done.1.got_ref = bf16[4,400,128]{2,1,0:T(8,128)(2,1)S(1)} async-done(((bf16[4,400,128]{2,1,0:T(8,128)(2,1)}), bf16[4,400,128]{2,1,0:T(8,128)(2,1)S(1)}, u32[]{:S(2)}, u32[]{:S(2)}) %all-to-all-start.1) | async-done | bytes 409632 | tf_op jit(solution)/shard_map/all_to_all | solution.py:62
  39.0 0.8 shard_map.102
  39.7 0.0 collective-permute-done.1
  39.7 12.6 %all-to-all-start.2 = ((bf16[4,304,128]{2,1,0:T(8,128)(2,1)}), bf16[4,304,128]{2,1,0:T(8,128)(2,1)S(1)}, u32[]{:S(2)}, u32[]{:S(2)}) async-start(bf16[4,304,128]{2,1,0:T(8,128)(2,1)} %shard_map.102), calls=%async_computation.2 | async-start | bytes 622592 | tf_op jit(solution)/shard_map/all_to_all | solution.py:62
  52.4 1.3 dynamic-slice_bitcast_fusion
  53.7 0.1 pad_maximum_fusion.kv_ref
  53.8 1.9 %collective-permute-start.2 = (bf16[2,2048,128]{2,1,0:T(8,128)(2,1)S(1)}, bf16[2,2048,128]{2,1,0:T(8,128)(2,1)S(1)}, u32[]{:S(2)}, u32[]{:S(2)}) collective-permute-start(bf16[2,2048,128]{2,1,0:T(8,128)(2,1)S(1)} %pad_maximum_fusion.kv_ref), channel_id=1, source_target_pairs={{0,256},{256,0},{1,257},{257,1},{2,258},{258,2},{3,259},{259,3},{4... | collective-permute-start | bytes 3145736 | tf_op jit(solution)/shard_map/ppermute | solution.py:287
  55.7 0.1 pad_add_fusion.2.place_ref
  55.8 0.7 constant_dynamic-slice_fusion
  56.5 0.9 constant_dynamic-slice_fusion.2
  57.4 12.4 %all-to-all-done.2.got_ref = bf16[4,304,128]{2,1,0:T(8,128)(2,1)S(1)} async-done(((bf16[4,304,128]{2,1,0:T(8,128)(2,1)}), bf16[4,304,128]{2,1,0:T(8,128)(2,1)S(1)}, u32[]{:S(2)}, u32[]{:S(2)}) %all-to-all-start.2) | async-done | bytes 311328 | tf_op jit(solution)/shard_map/all_to_all | solution.py:62
  69.8 1.4 shard_map.103
  71.2 3.4 %all-to-all-start.3 = ((bf16[4,256,128]{2,1,0:T(8,128)(2,1)}), bf16[4,256,128]{2,1,0:T(8,128)(2,1)S(1)}, u32[]{:S(2)}, u32[]{:S(2)}) async-start(bf16[4,256,128]{2,1,0:T(8,128)(2,1)} %get-tuple-element.16), calls=%async_computation.3 | async-start | bytes 524288 | tf_op jit(solution)/shard_map/all_to_all | solution.py:62
  74.7 5.9 %collective-permute-start.4 = (bf16[2,256,256]{2,1,0:T(8,128)(2,1)S(1)}, bf16[2,256,256]{2,1,0:T(8,128)(2,1)S(1)}, u32[]{:S(2)}, u32[]{:S(2)}) collective-permute-start(bf16[2,256,256]{2,1,0:T(8,128)(2,1)S(1)} %pad_maximum_fusion.1.own_ref), channel_id=1, source_target_pairs={{0,1},{1,0},{2,3},{3,2},{4,5},{5,4},{6,7},{7,6},{8,9},{9,8},{10,11... | collective-permute-start | bytes 786440 | tf_op jit(solution)/shard_map/ppermute | solution.py:287
  80.6 1.9 %collective-permute-start.3 = (bf16[32,128]{1,0:T(8,128)(2,1)S(1)}, bf16[32,128]{1,0:T(8,128)(2,1)S(1)}, u32[]{:S(2)}, u32[]{:S(2)}) collective-permute-start(bf16[32,128]{1,0:T(8,128)(2,1)S(1)} %get-tuple-element.17.own_ref), channel_id=1, source_target_pairs={{0,1},{1,0},{2,3},{3,2},{4,5},{5,4},{6,7},{7,6},{8,9},{9,8},{10,11... | collective-permute-start | bytes 24584 | tf_op jit(solution)/shard_map/ppermute | solution.py:287
  82.5 0.1 pad_add_fusion.1.place_ref
  82.6 0.0 collective-permute-done.2.other_ref
  82.6 1.1 collective-permute-done.3.swap_ref
  83.7 0.0 all-to-all-done.3.q_ref
  83.7 6.8 %shard_map.104 = bf16[4,272,128]{2,1,0:T(8,128)(2,1)S(1)} custom-call(s32[2]{0:T(128)S(1)} %pad_add_fusion.1.place_ref, bf16[4,256,128]{2,1,0:T(8,128)(2,1)S(1)} %all-to-all-done.3.q_ref, bf16[2,2048,128]{2,1,0:T(8,128)(2,1)S(1)} %pad_maximum_fusion.kv_ref, bf16[2,2048,128]{2,1,0:T(8,128)(2,1)S(1)} %collective-permute-done.2.other_ref, ...), custom_call_target="tpu_custom_call" | custom-call | tf_op jit(solution)/shard_map/pallas_call | solution.py:68
  90.5 0.0 collective-permute-done.4.swap_ref
  90.5 13.0 %all_to_all.35.got_ref = bf16[4,272,128]{2,1,0:T(8,128)(2,1)S(1)} all-to-all(bf16[4,272,128]{2,1,0:T(8,128)(2,1)S(1)} %shard_map.104), channel_id=1, replica_groups=mesh['ylo'=2,'zh'=4,'zl'=4,'yhi'=2,'x'=4,'core'=2] {'zl'}, dimensions={0} | all-to-all | bytes 557056 | tf_op jit(solution)/shard_map/all_to_all | solution.py:62
  103.5 0.2 shard_map.105
  103.8 18.1 %all-gather.1 = bf16[1088,128]{1,0:T(8,128)(2,1)S(1)} all-gather(bf16[272,128]{1,0:T(8,128)(2,1)S(1)} %shard_map.105), channel_id=3, replica_groups=mesh['ylo'=2,'zh'=4,'zl'=4,'yhi'=2,'x'=4,'core'=2] {'zh'}, dimensions={0}, use_global_device_ids=true | all-gather | bytes 348160 | tf_op jit(solution)/shard_map/all_gather | solution.py:352
  121.9 0.9 shard_map.106
  122.9 7.1 %all-to-all-start.5 = ((bf16[8,128,128]{2,1,0:T(8,128)(2,1)}), bf16[8,128,128]{2,1,0:T(8,128)(2,1)S(1)}, u32[]{:S(2)}, u32[]{:S(2)}) async-start(bf16[8,128,128]{2,1,0:T(8,128)(2,1)} %shard_map.106), calls=%async_computation.5 | async-start | bytes 524288 | tf_op jit(solution)/shard_map/all_to_all | solution.py:62
  130.0 0.1 pad_add_fusion.place_ref
  130.1 8.7 %all-to-all-done.5.got_ref = bf16[8,128,128]{2,1,0:T(8,128)(2,1)S(1)} async-done(((bf16[8,128,128]{2,1,0:T(8,128)(2,1)}), bf16[8,128,128]{2,1,0:T(8,128)(2,1)S(1)}, u32[]{:S(2)}, u32[]{:S(2)}) %all-to-all-start.5) | async-done | bytes 262176 | tf_op jit(solution)/shard_map/all_to_all | solution.py:62
  138.7 0.8 shard_map.107
  139.6 13.0 %all_to_all.36 = bf16[16,32,256]{2,1,0:T(8,128)(2,1)S(1)} all-to-all(bf16[16,32,256]{2,1,0:T(8,128)(2,1)S(1)} %shard_map.107), channel_id=1, replica_groups=mesh['ylo'=2,'zh'=4,'zl'=4,'yhi'=2,'x'=4,'core'=2] {'ylo','yhi','x'}, dimensions={0} | all-to-all | bytes 524288 | tf_op jit(solution)/shard_map/all_to_all | solution.py:62
  152.5 0.6 reduce_sum.12
  (3 shorter events, 0.1 us)
Async XLA Ops:
  0.0 0.7 copy-start
  0.7 26.7 %copy-start.1 = (bf16[512,256]{1,0:T(8,128)(2,1)S(1)}, bf16[512,256]{1,0:T(8,128)(2,1)}, u32[]{:S(2)}) copy-start(bf16[512,256]{1,0:T(8,128)(2,1)} %param.15) | copy-start | bytes 786436
  1.4 15.3 %all-to-all-start = ((bf16[16,32,256]{2,1,0:T(8,128)(2,1)}), bf16[16,32,256]{2,1,0:T(8,128)(2,1)S(1)}, u32[]{:S(2)}, u32[]{:S(2)}) async-start(bf16[16,32,256]{2,1,0:T(8,128)(2,1)} %shard_map.100), calls=%async_computation | async-start | bytes 524288 | tf_op jit(solution)/shard_map/all_to_all | solution.py:62
  11.6 10.7 %collective-permute-start = (bf16[272,384]{1,0:T(8,128)(2,1)S(1)}, bf16[272,384]{1,0:T(8,128)(2,1)S(1)}, u32[]{:S(2)}, u32[]{:S(2)}) collective-permute-start(bf16[272,384]{1,0:T(8,128)(2,1)S(1)} %fusion.1), channel_id=1, source_target_pairs={{0,256},{256,0},{1,257},{257,1},{2,258},{258,2},{3,259},{259,3},{4... | collective-permute-start | bytes 626696 | tf_op jit(solution)/shard_map/ppermute | solution.py:287
  23.7 15.3 %all-to-all-start.1 = ((bf16[4,400,128]{2,1,0:T(8,128)(2,1)}), bf16[4,400,128]{2,1,0:T(8,128)(2,1)S(1)}, u32[]{:S(2)}, u32[]{:S(2)}) async-start(bf16[4,400,128]{2,1,0:T(8,128)(2,1)} %shard_map.101), calls=%async_computation.1 | async-start | bytes 819200 | tf_op jit(solution)/shard_map/all_to_all | solution.py:62
  27.5 12.3 %collective-permute-start.1 = (bf16[256,256]{1,0:T(8,128)(2,1)S(1)}, bf16[256,256]{1,0:T(8,128)(2,1)S(1)}, u32[]{:S(2)}, u32[]{:S(2)}) collective-permute-start(bf16[256,256]{1,0:T(8,128)(2,1)S(1)} %get-tuple-element.22), channel_id=1, source_target_pairs={{0,256},{256,0},{1,257},{257,1},{2,258},{258,2},{3,259},{259,3},{4... | collective-permute-start | bytes 393224 | tf_op jit(solution)/shard_map/ppermute | solution.py:287
  39.7 30.0 %all-to-all-start.2 = ((bf16[4,304,128]{2,1,0:T(8,128)(2,1)}), bf16[4,304,128]{2,1,0:T(8,128)(2,1)S(1)}, u32[]{:S(2)}, u32[]{:S(2)}) async-start(bf16[4,304,128]{2,1,0:T(8,128)(2,1)} %shard_map.102), calls=%async_computation.2 | async-start | bytes 622592 | tf_op jit(solution)/shard_map/all_to_all | solution.py:62
  53.8 28.9 %collective-permute-start.2 = (bf16[2,2048,128]{2,1,0:T(8,128)(2,1)S(1)}, bf16[2,2048,128]{2,1,0:T(8,128)(2,1)S(1)}, u32[]{:S(2)}, u32[]{:S(2)}) collective-permute-start(bf16[2,2048,128]{2,1,0:T(8,128)(2,1)S(1)} %pad_maximum_fusion.kv_ref), channel_id=1, source_target_pairs={{0,256},{256,0},{1,257},{257,1},{2,258},{258,2},{3,259},{259,3},{4... | collective-permute-start | bytes 3145736 | tf_op jit(solution)/shard_map/ppermute | solution.py:287
  71.2 12.5 %all-to-all-start.3 = ((bf16[4,256,128]{2,1,0:T(8,128)(2,1)}), bf16[4,256,128]{2,1,0:T(8,128)(2,1)S(1)}, u32[]{:S(2)}, u32[]{:S(2)}) async-start(bf16[4,256,128]{2,1,0:T(8,128)(2,1)} %get-tuple-element.16), calls=%async_computation.3 | async-start | bytes 524288 | tf_op jit(solution)/shard_map/all_to_all | solution.py:62
  74.7 15.8 %collective-permute-start.4 = (bf16[2,256,256]{2,1,0:T(8,128)(2,1)S(1)}, bf16[2,256,256]{2,1,0:T(8,128)(2,1)S(1)}, u32[]{:S(2)}, u32[]{:S(2)}) collective-permute-start(bf16[2,256,256]{2,1,0:T(8,128)(2,1)S(1)} %pad_maximum_fusion.1.own_ref), channel_id=1, source_target_pairs={{0,1},{1,0},{2,3},{3,2},{4,5},{5,4},{6,7},{7,6},{8,9},{9,8},{10,11... | collective-permute-start | bytes 786440 | tf_op jit(solution)/shard_map/ppermute | solution.py:287
  80.6 3.1 %collective-permute-start.3 = (bf16[32,128]{1,0:T(8,128)(2,1)S(1)}, bf16[32,128]{1,0:T(8,128)(2,1)S(1)}, u32[]{:S(2)}, u32[]{:S(2)}) collective-permute-start(bf16[32,128]{1,0:T(8,128)(2,1)S(1)} %get-tuple-element.17.own_ref), channel_id=1, source_target_pairs={{0,1},{1,0},{2,3},{3,2},{4,5},{5,4},{6,7},{7,6},{8,9},{9,8},{10,11... | collective-permute-start | bytes 24584 | tf_op jit(solution)/shard_map/ppermute | solution.py:287
  122.9 15.9 %all-to-all-start.5 = ((bf16[8,128,128]{2,1,0:T(8,128)(2,1)}), bf16[8,128,128]{2,1,0:T(8,128)(2,1)S(1)}, u32[]{:S(2)}, u32[]{:S(2)}) async-start(bf16[8,128,128]{2,1,0:T(8,128)(2,1)} %shard_map.106), calls=%async_computation.5 | async-start | bytes 524288 | tf_op jit(solution)/shard_map/all_to_all | solution.py:62

commit v7 on v6

--- a/solution.py
+++ b/solution.py
@@ -155,31 +155,29 @@
     low = total.astype(bf16)
     s_row = Q_ROWS + TOK_NEAR
     sums = total[s_row : s_row + 1] + total[s_row + 1 : s_row + 2] + total[s_row + 2 : s_row + 3]
-    tile = pack_rows(parts3(sums))
-    end = Q_ROWS + TOK_ROW
-    for f in range(FAR_SIZE):
-        row = Q_ROWS + TOK_ROW * f
-        out_ref[f, :Q_ROWS, :] = low[:Q_ROWS]
-        out_ref[f, Q_ROWS:end, :] = low[row : row + TOK_ROW]
-        out_ref[f, end : end + PAD, :] = tile
+    out_ref[:s_row, :] = low[:s_row]
+    out_ref[s_row:, :] = pack_rows(parts3(sums))
 
 
 def rope_kernel(place_ref, got_ref, cos_ref, sin_ref, cosn_ref, sinn_ref, q_ref, new_ref):
-    total = got_ref[0].astype(f32)
-    for n in range(1, FAR_SIZE):
-        total = total + got_ref[n].astype(f32)
-    row = Q_ROWS + TOK_ROW
-    sums = total[row : row + 1] + total[row + 1 : row + 2] + total[row + 2 : row + 3]
+    def gather(rows):
+        total = got_ref[0, rows, :].astype(f32)
+        for n in range(1, FAR_SIZE):
+            total = total + got_ref[n, rows, :].astype(f32)
+        return total
+
+    tile = gather(slice(Q_ROWS + TOK_NEAR, Q_ROWS + TOK_NEAR + PAD))
+    sums = tile[0:1] + tile[1:2] + tile[2:3]
     inv = lax.rsqrt(sums / MODEL_WIDTH + epsilon)
     inv_q = to_column(inv, TOK_NEAR)
     inv_n = to_column(inv, TOK_ROW, place_ref[0] * TOK_ROW)
     cos, sin = cos_ref[...], sin_ref[...]
     for h in range(HEADS_HERE):
-        u = total[h * TOK_NEAR : (h + 1) * TOK_NEAR] * inv_q
+        u = gather(slice(h * TOK_NEAR, (h + 1) * TOK_NEAR)) * inv_q
         u = (u * cos + pltpu.roll(u, HEAD_WIDTH // 2, 1) * sin).astype(bf16)
         for n in range(NEAR_SIZE):
             q_ref[n, h * TOK_NEAR : (h + 1) * TOK_NEAR, :] = u
-    u = total[Q_ROWS : Q_ROWS + TOK_ROW] * inv_n
+    u = gather(pl.ds(pl.multiple_of(Q_ROWS + place_ref[0] * TOK_ROW, TOK_ROW), TOK_ROW)) * inv_n
     turned = u * cosn_ref[...] + pltpu.roll(u, HEAD_WIDTH // 2, 1) * sinn_ref[...]
     new_ref[...] = jnp.where(place_ref[1] == 0, turned, u).astype(bf16)
 
@@ -308,22 +306,21 @@
     w_far = trade(jnp.concatenate([w_far, gain_row], axis=0), "ylo")
     whole = lax.all_gather(exchange(run(copies_kernel, shape(CHIPS, *tokens.shape), tokens), PLANE), "core", axis=0)
     whole = whole.reshape((2, PAIR, CHIPS // PAIR) + tokens.shape)
-    kv_own = jnp.stack([panel(cached_keys), panel(cached_values)])
-    kv_far = trade(kv_own, "ylo")
     pay = run(
         project_kernel,
         shape(NEAR_SIZE, Q_ROWS + TOK_NEAR + PAD, HEAD_WIDTH),
         whole, norm_gain[None], w_own, kv_panel, w_far,
         scalars=place(mine),
     )
-    pay, w_out = lax.optimization_barrier((pay, w_out))
+    pay, group = lax.optimization_barrier((pay, group))
+    kv_own = jnp.stack([panel(cached_keys), panel(cached_values)])
+    kv_far = trade(kv_own, "ylo")
+    got = exchange(pay, "zl")
+    pay = run(reduce_kernel, shape(Q_ROWS + TOK_NEAR + PAD, HEAD_WIDTH), got)
+    got = lax.all_gather(pay, "zh", axis=0)
+    got, w_out = lax.optimization_barrier((got, w_out))
     o_own = lax.dynamic_slice_in_dim(w_out, mine * HEAD_COLS, HEAD_COLS, 0)
     o_far = trade(lax.dynamic_slice_in_dim(w_out, (1 - mine) * HEAD_COLS, HEAD_COLS, 0), "ylo")
-    got = exchange(pay, "zl")
-    pay = run(reduce_kernel, shape(FAR_SIZE, Q_ROWS + TOK_ROW + PAD, HEAD_WIDTH), got)
-    pay, o_far = lax.optimization_barrier((pay, o_far))
-    o_own = jnp.stack([o_own, o_far])
-    got = exchange(pay, "zh")
 
     start = near * TOK_NEAR
     first = start + far * TOK_ROW
@@ -339,7 +336,6 @@
         scalars=place(far, core),
     )
     new_swap = trade(new_own, "core")
-    o_swap = trade(o_own, "core")
     queries = exchange(pay, "zl")
     pay = run(
         attend_kernel,
@@ -347,10 +343,13 @@
         queries, kv_own, kv_far, new_own, new_swap,
         scalars=place(first, core),
     )
-    pay, o_swap = lax.optimization_barrier((pay, o_swap))
+    pay, o_own, o_far = lax.optimization_barrier((pay, o_own, o_far))
     got = exchange(pay, "zl")
     got = lax.all_gather(run(mix_near_kernel, shape(Q_ROWS + PAD, HEAD_WIDTH), got), "zh", axis=0)
     got = run(mix_far_kernel, shape(2 * NEAR_SIZE, Q_ROWS // 2, HEAD_WIDTH), got)
+    got, o_own, o_far = lax.optimization_barrier((got, o_own, o_far))
+    o_own = jnp.stack([o_own, o_far])
+    o_swap = trade(o_own, "core")
     got = exchange(got, ("zl", "core"))
     pay = run(
         output_kernel,

time: 154 us -> 151 us (0.981)
  blocking collectives: 49.7 us -> 73 us
  waiting for transfers between devices: 33.4 us -> 15.5 us
  starting transfers between devices: 49.6 us -> 42.1 us
    all_gather x0 -> x1, blocking collectives: none -> 24.9 us  [body(): got = lax.all_gather(pay, 'zh', axis=0)]
    all_to_all x5 -> x4, waiting for transfers between devices: 32.3 us -> 13.5 us  [exchange(): return lax.all_to_all(x, axes, 0, 0, tiled=True)]
    all_to_all x5 -> x4, starting transfers between devices: 34.5 us -> 24.8 us  [exchange(): return lax.all_to_all(x, axes, 0, 0, tiled=True)]
    ppermute x5, starting transfers between devices: 15.1 us -> 17.2 us  [trade(): return lax.ppermute(x, axis, [(0, 1), (1, 0)])]
  transfers between devices with their start and end apart: 10 -> 9, of which waited for: 5 -> 5; matrix products, arithmetic and copies ran while one was open for 4% -> 4% of each run, Pallas kernels for 6% -> 6%
where the time goes in v7:
time: 151 us; the launch traced here: 150 us
  blocking collectives  73 us (48%)
  starting transfers between devices  42.1 us (28%)
  waiting for transfers between devices  15.5 us (10%)
  Pallas kernels  12.4 us (8%)
  local copies, waits for them, and re-layouts  5.31 us (4%)
  other arithmetic  1.93 us (1%)
    all_to_all x2, blocking collectives, exchange(): return lax.all_to_all(x, axes, 0, 0, tiled=True)  26 us
    all_gather x1, blocking collectives, body(): got = lax.all_gather(pay, 'zh', axis=0)  24.9 us
    all_to_all x4, starting transfers between devices, exchange(): return lax.all_to_all(x, axes, 0, 0, tiled=True)  24.8 us
    ppermute x5, starting transfers between devices, trade(): return lax.ppermute(x, axis, [(0, 1), (1, 0)])  17.2 us
    all_gather x1, blocking collectives, body(): lax.all_gather(run(mix_near_kernel, shape(Q_ROWS + PAD, HEAD_WIDTH), got)...  16.6 us
    all_to_all x4, waiting for transfers between devices, exchange(): return lax.all_to_all(x, axes, 0, 0, tiled=True)  13.5 us
    pallas_call x8, Pallas kernels, run(): pl.pallas_call(kernel, out_shape=shapes, in_specs=[smem] * len(scalars) +...  12.4 us
    all_gather x1, blocking collectives, body(): lax.all_gather(exchange(run(copies_kernel, shape(CHIPS, *tokens.shape), t...  5.58 us
  transfers between devices with their start and end apart: 9, of which 5 were waited for; matrix products, arithmetic and copies ran while one was open for 4% of the time, Pallas kernels for 6%

profile of v7, /device:TPU:1, one launch (start us, length us, event | category | flops | bytes accessed | tf_op | source)
XLA Modules:
  0.0 150.4 jit_solution(15868387423583356916)
XLA Ops:
  0.0 0.0 copy-start
  0.0 0.7 copy-done
  0.7 0.7 shard_map.100
  1.4 7.6 %all-to-all-start = ((bf16[16,32,256]{2,1,0:T(8,128)(2,1)}), bf16[16,32,256]{2,1,0:T(8,128)(2,1)S(1)}, u32[]{:S(2)}, u32[]{:S(2)}) async-start(bf16[16,32,256]{2,1,0:T(8,128)(2,1)} %shard_map.100), calls=%async_computation | async-start | bytes 524288 | tf_op jit(solution)/shard_map/all_to_all | solution.py:62
  9.1 1.0 constant_dynamic-slice_fusion.6
  10.1 0.9 dynamic-slice_select_fusion.kv_ref
  11.0 0.7 broadcast_in_dim.4.gain_ref
  11.6 3.3 %collective-permute-start = (bf16[272,384]{1,0:T(8,128)(2,1)S(1)}, bf16[272,384]{1,0:T(8,128)(2,1)S(1)}, u32[]{:S(2)}, u32[]{:S(2)}) collective-permute-start(bf16[272,384]{1,0:T(8,128)(2,1)S(1)} %fusion.1), channel_id=1, source_target_pairs={{0,256},{256,0},{1,257},{257,1},{2,258},{258,2},{3,259},{259,3},{4... | collective-permute-start | bytes 626696 | tf_op jit(solution)/shard_map/ppermute | solution.py:285
  14.9 1.8 %all-to-all-done = bf16[16,32,256]{2,1,0:T(8,128)(2,1)S(1)} async-done(((bf16[16,32,256]{2,1,0:T(8,128)(2,1)}), bf16[16,32,256]{2,1,0:T(8,128)(2,1)S(1)}, u32[]{:S(2)}, u32[]{:S(2)}) %all-to-all-start) | async-done | bytes 262176 | tf_op jit(solution)/shard_map/all_to_all | solution.py:62
  16.7 5.6 %all-gather = bf16[32,32,256]{2,1,0:T(8,128)(2,1)S(1)} all-gather(bf16[16,32,256]{2,1,0:T(8,128)(2,1)S(1)} %all-to-all-done), channel_id=2, replica_groups=mesh['ylo'=2,'zh'=4,'zl'=4,'yhi'=2,'x'=4,'core'=2] {'core'}, dimensions={0}, use_global_device_ids=true | all-gather | bytes 786432 | tf_op jit(solution)/shard_map/all_gather | solution.py:307
  22.3 0.0 collective-permute-done.far_ref
  22.3 0.0 copy-start.1
  22.3 1.3 shard_map.101
  23.7 3.8 %all-to-all-start.1 = ((bf16[4,400,128]{2,1,0:T(8,128)(2,1)}), bf16[4,400,128]{2,1,0:T(8,128)(2,1)S(1)}, u32[]{:S(2)}, u32[]{:S(2)}) async-start(bf16[4,400,128]{2,1,0:T(8,128)(2,1)} %shard_map.101), calls=%async_computation.1 | async-start | bytes 819200 | tf_op jit(solution)/shard_map/all_to_all | solution.py:62
  27.4 0.7 constant_dynamic-slice_fusion.2
  28.2 0.9 constant_dynamic-slice_fusion.4
  29.1 1.3 dynamic-slice_bitcast_fusion
  30.4 0.1 pad_maximum_fusion.kv_ref
  30.5 2.1 %collective-permute-start.1 = (bf16[2,2048,128]{2,1,0:T(8,128)(2,1)S(1)}, bf16[2,2048,128]{2,1,0:T(8,128)(2,1)S(1)}, u32[]{:S(2)}, u32[]{:S(2)}) collective-permute-start(bf16[2,2048,128]{2,1,0:T(8,128)(2,1)S(1)} %pad_maximum_fusion.kv_ref), channel_id=1, source_target_pairs={{0,256},{256,0},{1,257},{257,1},{2,258},{258,2},{3,259},{259,3},{4... | collective-permute-start | bytes 3145736 | tf_op jit(solution)/shard_map/ppermute | solution.py:285
  32.5 0.1 pad_add_fusion.2.place_ref
  32.6 6.4 %all-to-all-done.1.got_ref = bf16[4,400,128]{2,1,0:T(8,128)(2,1)S(1)} async-done(((bf16[4,400,128]{2,1,0:T(8,128)(2,1)}), bf16[4,400,128]{2,1,0:T(8,128)(2,1)S(1)}, u32[]{:S(2)}, u32[]{:S(2)}) %all-to-all-start.1) | async-done | bytes 409632 | tf_op jit(solution)/shard_map/all_to_all | solution.py:62
  39.0 0.1 shard_map.102
  39.0 24.9 %all-gather.1 = bf16[1600,128]{1,0:T(8,128)(2,1)S(1)} all-gather(bf16[400,128]{1,0:T(8,128)(2,1)S(1)} %shard_map.102), channel_id=3, replica_groups=mesh['ylo'=2,'zh'=4,'zl'=4,'yhi'=2,'x'=4,'core'=2] {'zh'}, dimensions={0}, use_global_device_ids=true | all-gather | bytes 512000 | tf_op jit(solution)/shard_map/all_gather | solution.py:320
  63.9 1.4 shard_map.103
  65.4 3.4 %all-to-all-start.2 = ((bf16[4,256,128]{2,1,0:T(8,128)(2,1)}), bf16[4,256,128]{2,1,0:T(8,128)(2,1)S(1)}, u32[]{:S(2)}, u32[]{:S(2)}) async-start(bf16[4,256,128]{2,1,0:T(8,128)(2,1)} %get-tuple-element.19), calls=%async_computation.2 | async-start | bytes 524288 | tf_op jit(solution)/shard_map/all_to_all | solution.py:62
  68.8 0.0 copy-done.1
  68.8 2.4 %collective-permute-start.3 = (bf16[256,256]{1,0:T(8,128)(2,1)S(1)}, bf16[256,256]{1,0:T(8,128)(2,1)S(1)}, u32[]{:S(2)}, u32[]{:S(2)}) collective-permute-start(bf16[256,256]{1,0:T(8,128)(2,1)S(1)} %get-tuple-element.29), channel_id=1, source_target_pairs={{0,256},{256,0},{1,257},{257,1},{2,258},{258,2},{3,259},{259,3},{4... | collective-permute-start | bytes 393224 | tf_op jit(solution)/shard_map/ppermute | solution.py:285
  71.2 7.5 %collective-permute-start.2 = (bf16[32,128]{1,0:T(8,128)(2,1)S(1)}, bf16[32,128]{1,0:T(8,128)(2,1)S(1)}, u32[]{:S(2)}, u32[]{:S(2)}) collective-permute-start(bf16[32,128]{1,0:T(8,128)(2,1)S(1)} %get-tuple-element.21.own_ref), channel_id=1, source_target_pairs={{0,1},{1,0},{2,3},{3,2},{4,5},{5,4},{6,7},{7,6},{8,9},{9,8},{10,11... | collective-permute-start | bytes 24584 | tf_op jit(solution)/shard_map/ppermute | solution.py:285
  78.7 0.1 pad_add_fusion.1.place_ref
  78.8 0.0 collective-permute-done.1.other_ref
  78.8 0.7 collective-permute-done.2.swap_ref
  79.5 0.0 all-to-all-done.2.q_ref
  79.6 6.8 %shard_map.104 = bf16[4,272,128]{2,1,0:T(8,128)(2,1)S(1)} custom-call(s32[2]{0:T(128)S(1)} %pad_add_fusion.1.place_ref, bf16[4,256,128]{2,1,0:T(8,128)(2,1)S(1)} %all-to-all-done.2.q_ref, bf16[2,2048,128]{2,1,0:T(8,128)(2,1)S(1)} %pad_maximum_fusion.kv_ref, bf16[2,2048,128]{2,1,0:T(8,128)(2,1)S(1)} %collective-permute-done.1.other_ref, ...), custom_call_target="tpu_custom_call" | custom-call | tf_op jit(solution)/shard_map/pallas_call | solution.py:68
  86.4 0.0 collective-permute-done.3
  86.4 12.3 %all_to_all.30.got_ref = bf16[4,272,128]{2,1,0:T(8,128)(2,1)S(1)} all-to-all(bf16[4,272,128]{2,1,0:T(8,128)(2,1)S(1)} %shard_map.104), channel_id=1, replica_groups=mesh['ylo'=2,'zh'=4,'zl'=4,'yhi'=2,'x'=4,'core'=2] {'zl'}, dimensions={0} | all-to-all | bytes 557056 | tf_op jit(solution)/shard_map/all_to_all | solution.py:62
  98.7 0.2 shard_map.105
  98.9 16.6 %all-gather.2 = bf16[1088,128]{1,0:T(8,128)(2,1)S(1)} all-gather(bf16[272,128]{1,0:T(8,128)(2,1)S(1)} %shard_map.105), channel_id=4, replica_groups=mesh['ylo'=2,'zh'=4,'zl'=4,'yhi'=2,'x'=4,'core'=2] {'zh'}, dimensions={0}, use_global_device_ids=true | all-gather | bytes 348160 | tf_op jit(solution)/shard_map/all_gather | solution.py:348
  115.5 1.0 shard_map.106
  116.5 10.1 %all-to-all-start.4 = ((bf16[8,128,128]{2,1,0:T(8,128)(2,1)}), bf16[8,128,128]{2,1,0:T(8,128)(2,1)S(1)}, u32[]{:S(2)}, u32[]{:S(2)}) async-start(bf16[8,128,128]{2,1,0:T(8,128)(2,1)} %shard_map.106), calls=%async_computation.4 | async-start | bytes 524288 | tf_op jit(solution)/shard_map/all_to_all | solution.py:62
  126.5 2.0 %collective-permute-start.4 = (bf16[2,256,256]{2,1,0:T(8,128)(2,1)S(1)}, bf16[2,256,256]{2,1,0:T(8,128)(2,1)S(1)}, u32[]{:S(2)}, u32[]{:S(2)}) collective-permute-start(bf16[2,256,256]{2,1,0:T(8,128)(2,1)S(1)} %pad_maximum_fusion.1.own_ref), channel_id=1, source_target_pairs={{0,1},{1,0},{2,3},{3,2},{4,5},{5,4},{6,7},{7,6},{8,9},{9,8},{10,11... | collective-permute-start | bytes 786440 | tf_op jit(solution)/shard_map/ppermute | solution.py:285
  128.6 0.1 pad_add_fusion.place_ref
  128.6 1.3 collective-permute-done.4.swap_ref
  130.0 5.3 %all-to-all-done.4.got_ref = bf16[8,128,128]{2,1,0:T(8,128)(2,1)S(1)} async-done(((bf16[8,128,128]{2,1,0:T(8,128)(2,1)}), bf16[8,128,128]{2,1,0:T(8,128)(2,1)S(1)}, u32[]{:S(2)}, u32[]{:S(2)}) %all-to-all-start.4) | async-done | bytes 262176 | tf_op jit(solution)/shard_map/all_to_all | solution.py:62
  135.2 0.8 shard_map.107
  136.1 13.7 %all_to_all.31 = bf16[16,32,256]{2,1,0:T(8,128)(2,1)S(1)} all-to-all(bf16[16,32,256]{2,1,0:T(8,128)(2,1)S(1)} %shard_map.107), channel_id=1, replica_groups=mesh['ylo'=2,'zh'=4,'zl'=4,'yhi'=2,'x'=4,'core'=2] {'ylo','yhi','x'}, dimensions={0} | all-to-all | bytes 524288 | tf_op jit(solution)/shard_map/all_to_all | solution.py:62
  149.8 0.6 reduce_sum.12
  (3 shorter events, 0.1 us)
Async XLA Ops:
  0.0 0.7 copy-start
  1.4 15.3 %all-to-all-start = ((bf16[16,32,256]{2,1,0:T(8,128)(2,1)}), bf16[16,32,256]{2,1,0:T(8,128)(2,1)S(1)}, u32[]{:S(2)}, u32[]{:S(2)}) async-start(bf16[16,32,256]{2,1,0:T(8,128)(2,1)} %shard_map.100), calls=%async_computation | async-start | bytes 524288 | tf_op jit(solution)/shard_map/all_to_all | solution.py:62
  11.6 10.7 %collective-permute-start = (bf16[272,384]{1,0:T(8,128)(2,1)S(1)}, bf16[272,384]{1,0:T(8,128)(2,1)S(1)}, u32[]{:S(2)}, u32[]{:S(2)}) collective-permute-start(bf16[272,384]{1,0:T(8,128)(2,1)S(1)} %fusion.1), channel_id=1, source_target_pairs={{0,256},{256,0},{1,257},{257,1},{2,258},{258,2},{3,259},{259,3},{4... | collective-permute-start | bytes 626696 | tf_op jit(solution)/shard_map/ppermute | solution.py:285
  22.3 46.5 %copy-start.1 = (bf16[512,256]{1,0:T(8,128)(2,1)S(1)}, bf16[512,256]{1,0:T(8,128)(2,1)}, u32[]{:S(2)}) copy-start(bf16[512,256]{1,0:T(8,128)(2,1)} %param.15) | copy-start | bytes 786436
  23.7 15.3 %all-to-all-start.1 = ((bf16[4,400,128]{2,1,0:T(8,128)(2,1)}), bf16[4,400,128]{2,1,0:T(8,128)(2,1)S(1)}, u32[]{:S(2)}, u32[]{:S(2)}) async-start(bf16[4,400,128]{2,1,0:T(8,128)(2,1)} %shard_map.101), calls=%async_computation.1 | async-start | bytes 819200 | tf_op jit(solution)/shard_map/all_to_all | solution.py:62
  30.5 48.3 %collective-permute-start.1 = (bf16[2,2048,128]{2,1,0:T(8,128)(2,1)S(1)}, bf16[2,2048,128]{2,1,0:T(8,128)(2,1)S(1)}, u32[]{:S(2)}, u32[]{:S(2)}) collective-permute-start(bf16[2,2048,128]{2,1,0:T(8,128)(2,1)S(1)} %pad_maximum_fusion.kv_ref), channel_id=1, source_target_pairs={{0,256},{256,0},{1,257},{257,1},{2,258},{258,2},{3,259},{259,3},{4... | collective-permute-start | bytes 3145736 | tf_op jit(solution)/shard_map/ppermute | solution.py:285
  65.4 14.2 %all-to-all-start.2 = ((bf16[4,256,128]{2,1,0:T(8,128)(2,1)}), bf16[4,256,128]{2,1,0:T(8,128)(2,1)S(1)}, u32[]{:S(2)}, u32[]{:S(2)}) async-start(bf16[4,256,128]{2,1,0:T(8,128)(2,1)} %get-tuple-element.19), calls=%async_computation.2 | async-start | bytes 524288 | tf_op jit(solution)/shard_map/all_to_all | solution.py:62
  68.8 17.5 %collective-permute-start.3 = (bf16[256,256]{1,0:T(8,128)(2,1)S(1)}, bf16[256,256]{1,0:T(8,128)(2,1)S(1)}, u32[]{:S(2)}, u32[]{:S(2)}) collective-permute-start(bf16[256,256]{1,0:T(8,128)(2,1)S(1)} %get-tuple-element.29), channel_id=1, source_target_pairs={{0,256},{256,0},{1,257},{257,1},{2,258},{258,2},{3,259},{259,3},{4... | collective-permute-start | bytes 393224 | tf_op jit(solution)/shard_map/ppermute | solution.py:285
  71.2 8.4 %collective-permute-start.2 = (bf16[32,128]{1,0:T(8,128)(2,1)S(1)}, bf16[32,128]{1,0:T(8,128)(2,1)S(1)}, u32[]{:S(2)}, u32[]{:S(2)}) collective-permute-start(bf16[32,128]{1,0:T(8,128)(2,1)S(1)} %get-tuple-element.21.own_ref), channel_id=1, source_target_pairs={{0,1},{1,0},{2,3},{3,2},{4,5},{5,4},{6,7},{7,6},{8,9},{9,8},{10,11... | collective-permute-start | bytes 24584 | tf_op jit(solution)/shard_map/ppermute | solution.py:285
  116.5 18.8 %all-to-all-start.4 = ((bf16[8,128,128]{2,1,0:T(8,128)(2,1)}), bf16[8,128,128]{2,1,0:T(8,128)(2,1)S(1)}, u32[]{:S(2)}, u32[]{:S(2)}) async-start(bf16[8,128,128]{2,1,0:T(8,128)(2,1)} %shard_map.106), calls=%async_computation.4 | async-start | bytes 524288 | tf_op jit(solution)/shard_map/all_to_all | solution.py:62
  126.5 3.4 %collective-permute-start.4 = (bf16[2,256,256]{2,1,0:T(8,128)(2,1)S(1)}, bf16[2,256,256]{2,1,0:T(8,128)(2,1)S(1)}, u32[]{:S(2)}, u32[]{:S(2)}) collective-permute-start(bf16[2,256,256]{2,1,0:T(8,128)(2,1)S(1)} %pad_maximum_fusion.1.own_ref), channel_id=1, source_target_pairs={{0,1},{1,0},{2,3},{3,2},{4,5},{5,4},{6,7},{7,6},{8,9},{9,8},{10,11... | collective-permute-start | bytes 786440 | tf_op jit(solution)/shard_map/ppermute | solution.py:285

commit v8 on v7

--- a/solution.py
+++ b/solution.py
@@ -117,26 +117,17 @@
         out_ref[i] = x_ref[...]
 
 
-def project_kernel(pair_ref, tok_ref, gain_ref, w_ref, kv_ref, far_ref, out_ref):
+def ordered(tok_ref, side):
+    blocks = [tok_ref[core, side, j] for j in range(CHIPS // PAIR) for core in range(2)]
+    return jnp.concatenate(blocks, axis=0)
+
+
+def own_kernel(pair_ref, tok_ref, gain_ref, w_ref, kv_ref, acc_ref, sums_ref):
     mine = pair_ref[0]
-    gains = [gain_ref[...], far_ref[PANEL : PANEL + 1, :PANEL]]
-    toks = []
-    for side in (mine, 1 - mine):
-        blocks = [tok_ref[core, side, j] for j in range(CHIPS // PAIR) for core in range(2)]
-        toks.append(jnp.concatenate(blocks, axis=0))
-    scaled = [(t.astype(f32) * g.astype(f32)).astype(bf16) for t, g in zip(toks, gains)]
-    panels = [w_ref[...], kv_ref[...]]
-    for i, panel in enumerate(panels):
-        width = panel.shape[1]
-        other = far_ref[:PANEL, HEAD_COLS * i : HEAD_COLS * i + width]
-        part = jnp.dot(scaled[0], panel, preferred_element_type=f32)
-        part = (part + jnp.dot(scaled[1], other, preferred_element_type=f32)).astype(bf16)
-        for j in range(width // HEAD_WIDTH):
-            head = part[:, HEAD_WIDTH * j : HEAD_WIDTH * (j + 1)]
-            row = (2 * i + j) * TOK_NEAR
-            for n in range(NEAR_SIZE):
-                out_ref[n, row : row + TOK_NEAR, :] = head[n * TOK_NEAR : (n + 1) * TOK_NEAR]
-    row = Q_ROWS + TOK_NEAR
+    toks = [ordered(tok_ref, mine), ordered(tok_ref, 1 - mine)]
+    scaled = (toks[0].astype(f32) * gain_ref[...].astype(f32)).astype(bf16)
+    acc_ref[:, :HEAD_COLS] = jnp.dot(scaled, w_ref[...], preferred_element_type=f32)
+    acc_ref[:, HEAD_COLS:] = jnp.dot(scaled, kv_ref[...], preferred_element_type=f32)
     contract = (((1,), (1,)), ((), ()))
     for n in range(NEAR_SIZE):
         sums = jnp.zeros((1, TOK_NEAR), f32)
@@ -145,7 +136,24 @@
             gram = lax.dot_general(x, x, contract, preferred_element_type=f32)
             gram = jnp.where(same(TOK_NEAR, TOK_NEAR), gram, 0.0)
             sums = sums + jnp.sum(gram, axis=0, keepdims=True)
-        out_ref[n, row : row + PAD, :] = pack_rows(parts3(sums))
+        sums_ref[n] = pack_rows(parts3(sums))
+
+
+def project_kernel(pair_ref, tok_ref, far_ref, acc_ref, sums_ref, out_ref):
+    gain = far_ref[PANEL : PANEL + 1, :PANEL].astype(f32)
+    scaled = (ordered(tok_ref, 1 - pair_ref[0]).astype(f32) * gain).astype(bf16)
+    for i, width in enumerate((HEAD_COLS, HEAD_WIDTH)):
+        lanes = slice(HEAD_COLS * i, HEAD_COLS * i + width)
+        part = jnp.dot(scaled, far_ref[:PANEL, lanes], preferred_element_type=f32)
+        part = (acc_ref[:, lanes] + part).astype(bf16)
+        for j in range(width // HEAD_WIDTH):
+            head = part[:, HEAD_WIDTH * j : HEAD_WIDTH * (j + 1)]
+            row = (2 * i + j) * TOK_NEAR
+            for n in range(NEAR_SIZE):
+                out_ref[n, row : row + TOK_NEAR, :] = head[n * TOK_NEAR : (n + 1) * TOK_NEAR]
+    row = Q_ROWS + TOK_NEAR
+    for n in range(NEAR_SIZE):
+        out_ref[n, row : row + PAD, :] = sums_ref[n]
 
 
 def reduce_kernel(got_ref, out_ref):
@@ -306,10 +314,19 @@
     w_far = trade(jnp.concatenate([w_far, gain_row], axis=0), "ylo")
     whole = lax.all_gather(exchange(run(copies_kernel, shape(CHIPS, *tokens.shape), tokens), PLANE), "core", axis=0)
     whole = whole.reshape((2, PAIR, CHIPS // PAIR) + tokens.shape)
+    acc, sums = run(
+        own_kernel,
+        (
+            shape(BLOCK_TOKENS, HEAD_COLS + HEAD_WIDTH, dtype=f32),
+            shape(NEAR_SIZE, PAD, HEAD_WIDTH),
+        ),
+        whole, norm_gain[None], w_own, kv_panel,
+        scalars=place(mine),
+    )
     pay = run(
         project_kernel,
         shape(NEAR_SIZE, Q_ROWS + TOK_NEAR + PAD, HEAD_WIDTH),
-        whole, norm_gain[None], w_own, kv_panel, w_far,
+        whole, w_far, acc, sums,
         scalars=place(mine),
     )
     pay, group = lax.optimization_barrier((pay, group))

time: 151 us -> 151 us (level)
  starting transfers between devices: 42.1 us -> 35.2 us
  blocking collectives: 73 us -> 78.4 us
    ppermute x5, starting transfers between devices: 17.2 us -> 12.7 us  [trade(): return lax.ppermute(x, axis, [(0, 1), (1, 0)])]
    all_gather x1, blocking collectives: 24.9 us -> 28.6 us  [body(): got = lax.all_gather(pay, 'zh', axis=0)]
    all_to_all x4, starting transfers between devices: 24.8 us -> 22.4 us  [exchange(): return lax.all_to_all(x, axes, 0, 0, tiled=True)]
    all_gather x1, blocking collectives: 16.6 us -> 18.7 us  [body(): lax.all_gather(run(mix_near_kernel, shape(Q_ROWS + PAD, HEAD_WIDTH), got)...]
    pallas_call x8 -> x9, Pallas kernels: 12.4 us -> 12.6 us  [run(): pl.pallas_call(kernel, out_shape=shapes, in_specs=[smem] * len(scalars) +...]
  transfers between devices with their start and end apart: 9 -> 9, of which waited for: 5 -> 6; matrix products, arithmetic and copies ran while one was open for 4% -> 4% of each run, Pallas kernels for 6% -> 6%
where the time goes in v8:
time: 151 us; the launch traced here: 150 us
  blocking collectives  78.4 us (52%)
  starting transfers between devices  35.2 us (23%)
  waiting for transfers between devices  16.7 us (11%)
  Pallas kernels  12.6 us (8%)
  local copies, waits for them, and re-layouts  5.31 us (4%)
  other arithmetic  1.93 us (1%)
    all_gather x1, blocking collectives, body(): got = lax.all_gather(pay, 'zh', axis=0)  28.6 us
    all_to_all x2, blocking collectives, exchange(): return lax.all_to_all(x, axes, 0, 0, tiled=True)  25.5 us
    all_to_all x4, starting transfers between devices, exchange(): return lax.all_to_all(x, axes, 0, 0, tiled=True)  22.4 us
    all_gather x1, blocking collectives, body(): lax.all_gather(run(mix_near_kernel, shape(Q_ROWS + PAD, HEAD_WIDTH), got)...  18.7 us
    all_to_all x4, waiting for transfers between devices, exchange(): return lax.all_to_all(x, axes, 0, 0, tiled=True)  14.6 us
    ppermute x5, starting transfers between devices, trade(): return lax.ppermute(x, axis, [(0, 1), (1, 0)])  12.7 us
    pallas_call x9, Pallas kernels, run(): pl.pallas_call(kernel, out_shape=shapes, in_specs=[smem] * len(scalars) +...  12.6 us
    all_gather x1, blocking collectives, body(): lax.all_gather(exchange(run(copies_kernel, shape(CHIPS, *tokens.shape), t...  5.58 us
  transfers between devices with their start and end apart: 9, of which 6 were waited for; matrix products, arithmetic and copies ran while one was open for 4% of the time, Pallas kernels for 6%

profile of v8, /device:TPU:1, one launch (start us, length us, event | category | flops | bytes accessed | tf_op | source)
XLA Modules:
  0.0 150.2 jit_solution(11719643541811302330)
XLA Ops:
  0.0 0.0 copy-start
  0.0 0.7 copy-done
  0.7 0.7 shard_map.100
  1.4 7.6 %all-to-all-start = ((bf16[16,32,256]{2,1,0:T(8,128)(2,1)}), bf16[16,32,256]{2,1,0:T(8,128)(2,1)S(1)}, u32[]{:S(2)}, u32[]{:S(2)}) async-start(bf16[16,32,256]{2,1,0:T(8,128)(2,1)} %shard_map.100), calls=%async_computation | async-start | bytes 524288 | tf_op jit(solution)/shard_map/all_to_all | solution.py:62
  9.0 1.0 constant_dynamic-slice_fusion.6
  10.0 0.9 dynamic-slice_select_fusion.kv_ref
  10.9 0.7 broadcast_in_dim.4.gain_ref
  11.6 3.3 %collective-permute-start = (bf16[272,384]{1,0:T(8,128)(2,1)S(1)}, bf16[272,384]{1,0:T(8,128)(2,1)S(1)}, u32[]{:S(2)}, u32[]{:S(2)}) collective-permute-start(bf16[272,384]{1,0:T(8,128)(2,1)S(1)} %fusion.1), channel_id=1, source_target_pairs={{0,256},{256,0},{1,257},{257,1},{2,258},{258,2},{3,259},{259,3},{4... | collective-permute-start | bytes 626696 | tf_op jit(solution)/shard_map/ppermute | solution.py:293
  14.9 1.8 %all-to-all-done = bf16[16,32,256]{2,1,0:T(8,128)(2,1)S(1)} async-done(((bf16[16,32,256]{2,1,0:T(8,128)(2,1)}), bf16[16,32,256]{2,1,0:T(8,128)(2,1)S(1)}, u32[]{:S(2)}, u32[]{:S(2)}) %all-to-all-start) | async-done | bytes 262176 | tf_op jit(solution)/shard_map/all_to_all | solution.py:62
  16.7 5.6 %all-gather = bf16[32,32,256]{2,1,0:T(8,128)(2,1)S(1)} all-gather(bf16[16,32,256]{2,1,0:T(8,128)(2,1)S(1)} %all-to-all-done), channel_id=2, replica_groups=mesh['ylo'=2,'zh'=4,'zl'=4,'yhi'=2,'x'=4,'core'=2] {'core'}, dimensions={0}, use_global_device_ids=true | all-gather | bytes 786432 | tf_op jit(solution)/shard_map/all_gather | solution.py:315
  22.3 0.5 shard_map.101
  22.8 0.0 collective-permute-done.far_ref
  22.8 1.1 shard_map.102
  23.8 0.0 copy-start.1
  23.8 3.9 %all-to-all-start.1 = ((bf16[4,400,128]{2,1,0:T(8,128)(2,1)}), bf16[4,400,128]{2,1,0:T(8,128)(2,1)S(1)}, u32[]{:S(2)}, u32[]{:S(2)}) async-start(bf16[4,400,128]{2,1,0:T(8,128)(2,1)} %shard_map.102), calls=%async_computation.1 | async-start | bytes 819200 | tf_op jit(solution)/shard_map/all_to_all | solution.py:62
  27.8 0.7 constant_dynamic-slice_fusion.2
  28.5 0.9 constant_dynamic-slice_fusion.4
  29.4 1.3 dynamic-slice_bitcast_fusion
  30.7 0.1 pad_maximum_fusion.kv_ref
  30.8 2.1 %collective-permute-start.1 = (bf16[2,2048,128]{2,1,0:T(8,128)(2,1)S(1)}, bf16[2,2048,128]{2,1,0:T(8,128)(2,1)S(1)}, u32[]{:S(2)}, u32[]{:S(2)}) collective-permute-start(bf16[2,2048,128]{2,1,0:T(8,128)(2,1)S(1)} %pad_maximum_fusion.kv_ref), channel_id=1, source_target_pairs={{0,256},{256,0},{1,257},{257,1},{2,258},{258,2},{3,259},{259,3},{4... | collective-permute-start | bytes 3145736 | tf_op jit(solution)/shard_map/ppermute | solution.py:293
  32.8 0.1 pad_add_fusion.2.place_ref
  32.9 6.4 %all-to-all-done.1.got_ref = bf16[4,400,128]{2,1,0:T(8,128)(2,1)S(1)} async-done(((bf16[4,400,128]{2,1,0:T(8,128)(2,1)}), bf16[4,400,128]{2,1,0:T(8,128)(2,1)S(1)}, u32[]{:S(2)}, u32[]{:S(2)}) %all-to-all-start.1) | async-done | bytes 409632 | tf_op jit(solution)/shard_map/all_to_all | solution.py:62
  39.3 0.1 shard_map.103
  39.4 28.6 %all-gather.1 = bf16[1600,128]{1,0:T(8,128)(2,1)S(1)} all-gather(bf16[400,128]{1,0:T(8,128)(2,1)S(1)} %shard_map.103), channel_id=3, replica_groups=mesh['ylo'=2,'zh'=4,'zl'=4,'yhi'=2,'x'=4,'core'=2] {'zh'}, dimensions={0}, use_global_device_ids=true | all-gather | bytes 512000 | tf_op jit(solution)/shard_map/all_gather | solution.py:337
  68.0 1.4 shard_map.104
  69.4 3.4 %all-to-all-start.2 = ((bf16[4,256,128]{2,1,0:T(8,128)(2,1)}), bf16[4,256,128]{2,1,0:T(8,128)(2,1)S(1)}, u32[]{:S(2)}, u32[]{:S(2)}) async-start(bf16[4,256,128]{2,1,0:T(8,128)(2,1)} %get-tuple-element.23), calls=%async_computation.2 | async-start | bytes 524288 | tf_op jit(solution)/shard_map/all_to_all | solution.py:62
  72.9 0.0 copy-done.1
  72.9 1.9 %collective-permute-start.3 = (bf16[256,256]{1,0:T(8,128)(2,1)S(1)}, bf16[256,256]{1,0:T(8,128)(2,1)S(1)}, u32[]{:S(2)}, u32[]{:S(2)}) collective-permute-start(bf16[256,256]{1,0:T(8,128)(2,1)S(1)} %get-tuple-element.33), channel_id=1, source_target_pairs={{0,256},{256,0},{1,257},{257,1},{2,258},{258,2},{3,259},{259,3},{4... | collective-permute-start | bytes 393224 | tf_op jit(solution)/shard_map/ppermute | solution.py:293
  74.8 3.5 %collective-permute-start.2 = (bf16[32,128]{1,0:T(8,128)(2,1)S(1)}, bf16[32,128]{1,0:T(8,128)(2,1)S(1)}, u32[]{:S(2)}, u32[]{:S(2)}) collective-permute-start(bf16[32,128]{1,0:T(8,128)(2,1)S(1)} %get-tuple-element.25.own_ref), channel_id=1, source_target_pairs={{0,1},{1,0},{2,3},{3,2},{4,5},{5,4},{6,7},{7,6},{8,9},{9,8},{10,11... | collective-permute-start | bytes 24584 | tf_op jit(solution)/shard_map/ppermute | solution.py:293
  78.3 0.1 pad_add_fusion.1.place_ref
  78.4 0.0 collective-permute-done.1.other_ref
  78.4 0.7 collective-permute-done.2.swap_ref
  79.1 1.1 all-to-all-done.2.q_ref
  80.3 6.8 %shard_map.105 = bf16[4,272,128]{2,1,0:T(8,128)(2,1)S(1)} custom-call(s32[2]{0:T(128)S(1)} %pad_add_fusion.1.place_ref, bf16[4,256,128]{2,1,0:T(8,128)(2,1)S(1)} %all-to-all-done.2.q_ref, bf16[2,2048,128]{2,1,0:T(8,128)(2,1)S(1)} %pad_maximum_fusion.kv_ref, bf16[2,2048,128]{2,1,0:T(8,128)(2,1)S(1)} %collective-permute-done.1.other_ref, ...), custom_call_target="tpu_custom_call" | custom-call | tf_op jit(solution)/shard_map/pallas_call | solution.py:68
  87.1 0.0 collective-permute-done.3
  87.1 10.7 %all_to_all.30.got_ref = bf16[4,272,128]{2,1,0:T(8,128)(2,1)S(1)} all-to-all(bf16[4,272,128]{2,1,0:T(8,128)(2,1)S(1)} %shard_map.105), channel_id=1, replica_groups=mesh['ylo'=2,'zh'=4,'zl'=4,'yhi'=2,'x'=4,'core'=2] {'zl'}, dimensions={0} | all-to-all | bytes 557056 | tf_op jit(solution)/shard_map/all_to_all | solution.py:62
  97.8 0.2 shard_map.106
  98.0 18.7 %all-gather.2 = bf16[1088,128]{1,0:T(8,128)(2,1)S(1)} all-gather(bf16[272,128]{1,0:T(8,128)(2,1)S(1)} %shard_map.106), channel_id=4, replica_groups=mesh['ylo'=2,'zh'=4,'zl'=4,'yhi'=2,'x'=4,'core'=2] {'zh'}, dimensions={0}, use_global_device_ids=true | all-gather | bytes 348160 | tf_op jit(solution)/shard_map/all_gather | solution.py:365
  116.8 0.9 shard_map.107
  117.7 7.5 %all-to-all-start.4 = ((bf16[8,128,128]{2,1,0:T(8,128)(2,1)}), bf16[8,128,128]{2,1,0:T(8,128)(2,1)S(1)}, u32[]{:S(2)}, u32[]{:S(2)}) async-start(bf16[8,128,128]{2,1,0:T(8,128)(2,1)} %shard_map.107), calls=%async_computation.4 | async-start | bytes 524288 | tf_op jit(solution)/shard_map/all_to_all | solution.py:62
  125.3 2.0 %collective-permute-start.4 = (bf16[2,256,256]{2,1,0:T(8,128)(2,1)S(1)}, bf16[2,256,256]{2,1,0:T(8,128)(2,1)S(1)}, u32[]{:S(2)}, u32[]{:S(2)}) collective-permute-start(bf16[2,256,256]{2,1,0:T(8,128)(2,1)S(1)} %pad_maximum_fusion.1.own_ref), channel_id=1, source_target_pairs={{0,1},{1,0},{2,3},{3,2},{4,5},{5,4},{6,7},{7,6},{8,9},{9,8},{10,11... | collective-permute-start | bytes 786440 | tf_op jit(solution)/shard_map/ppermute | solution.py:293
  127.3 0.1 pad_add_fusion.place_ref
  127.4 1.3 collective-permute-done.4.swap_ref
  128.7 5.3 %all-to-all-done.4.got_ref = bf16[8,128,128]{2,1,0:T(8,128)(2,1)S(1)} async-done(((bf16[8,128,128]{2,1,0:T(8,128)(2,1)}), bf16[8,128,128]{2,1,0:T(8,128)(2,1)S(1)}, u32[]{:S(2)}, u32[]{:S(2)}) %all-to-all-start.4) | async-done | bytes 262176 | tf_op jit(solution)/shard_map/all_to_all | solution.py:62
  134.0 0.8 shard_map.108
  134.8 14.8 %all_to_all.31 = bf16[16,32,256]{2,1,0:T(8,128)(2,1)S(1)} all-to-all(bf16[16,32,256]{2,1,0:T(8,128)(2,1)S(1)} %shard_map.108), channel_id=1, replica_groups=mesh['ylo'=2,'zh'=4,'zl'=4,'yhi'=2,'x'=4,'core'=2] {'ylo','yhi','x'}, dimensions={0} | all-to-all | bytes 524288 | tf_op jit(solution)/shard_map/all_to_all | solution.py:62
  149.6 0.6 reduce_sum.12
  (3 shorter events, 0.1 us)
Async XLA Ops:
  0.0 0.7 copy-start
  1.4 15.3 %all-to-all-start = ((bf16[16,32,256]{2,1,0:T(8,128)(2,1)}), bf16[16,32,256]{2,1,0:T(8,128)(2,1)S(1)}, u32[]{:S(2)}, u32[]{:S(2)}) async-start(bf16[16,32,256]{2,1,0:T(8,128)(2,1)} %shard_map.100), calls=%async_computation | async-start | bytes 524288 | tf_op jit(solution)/shard_map/all_to_all | solution.py:62
  11.6 11.1 %collective-permute-start = (bf16[272,384]{1,0:T(8,128)(2,1)S(1)}, bf16[272,384]{1,0:T(8,128)(2,1)S(1)}, u32[]{:S(2)}, u32[]{:S(2)}) collective-permute-start(bf16[272,384]{1,0:T(8,128)(2,1)S(1)} %fusion.1), channel_id=1, source_target_pairs={{0,256},{256,0},{1,257},{257,1},{2,258},{258,2},{3,259},{259,3},{4... | collective-permute-start | bytes 626696 | tf_op jit(solution)/shard_map/ppermute | solution.py:293
  23.8 49.0 %copy-start.1 = (bf16[512,256]{1,0:T(8,128)(2,1)S(1)}, bf16[512,256]{1,0:T(8,128)(2,1)}, u32[]{:S(2)}) copy-start(bf16[512,256]{1,0:T(8,128)(2,1)} %param.15) | copy-start | bytes 786436
  23.8 15.5 %all-to-all-start.1 = ((bf16[4,400,128]{2,1,0:T(8,128)(2,1)}), bf16[4,400,128]{2,1,0:T(8,128)(2,1)S(1)}, u32[]{:S(2)}, u32[]{:S(2)}) async-start(bf16[4,400,128]{2,1,0:T(8,128)(2,1)} %shard_map.102), calls=%async_computation.1 | async-start | bytes 819200 | tf_op jit(solution)/shard_map/all_to_all | solution.py:62
  30.8 47.6 %collective-permute-start.1 = (bf16[2,2048,128]{2,1,0:T(8,128)(2,1)S(1)}, bf16[2,2048,128]{2,1,0:T(8,128)(2,1)S(1)}, u32[]{:S(2)}, u32[]{:S(2)}) collective-permute-start(bf16[2,2048,128]{2,1,0:T(8,128)(2,1)S(1)} %pad_maximum_fusion.kv_ref), channel_id=1, source_target_pairs={{0,256},{256,0},{1,257},{257,1},{2,258},{258,2},{3,259},{259,3},{4... | collective-permute-start | bytes 3145736 | tf_op jit(solution)/shard_map/ppermute | solution.py:293
  69.4 10.8 %all-to-all-start.2 = ((bf16[4,256,128]{2,1,0:T(8,128)(2,1)}), bf16[4,256,128]{2,1,0:T(8,128)(2,1)S(1)}, u32[]{:S(2)}, u32[]{:S(2)}) async-start(bf16[4,256,128]{2,1,0:T(8,128)(2,1)} %get-tuple-element.23), calls=%async_computation.2 | async-start | bytes 524288 | tf_op jit(solution)/shard_map/all_to_all | solution.py:62
  72.9 14.2 %collective-permute-start.3 = (bf16[256,256]{1,0:T(8,128)(2,1)S(1)}, bf16[256,256]{1,0:T(8,128)(2,1)S(1)}, u32[]{:S(2)}, u32[]{:S(2)}) collective-permute-start(bf16[256,256]{1,0:T(8,128)(2,1)S(1)} %get-tuple-element.33), channel_id=1, source_target_pairs={{0,256},{256,0},{1,257},{257,1},{2,258},{258,2},{3,259},{259,3},{4... | collective-permute-start | bytes 393224 | tf_op jit(solution)/shard_map/ppermute | solution.py:293
  74.8 4.3 %collective-permute-start.2 = (bf16[32,128]{1,0:T(8,128)(2,1)S(1)}, bf16[32,128]{1,0:T(8,128)(2,1)S(1)}, u32[]{:S(2)}, u32[]{:S(2)}) collective-permute-start(bf16[32,128]{1,0:T(8,128)(2,1)S(1)} %get-tuple-element.25.own_ref), channel_id=1, source_target_pairs={{0,1},{1,0},{2,3},{3,2},{4,5},{5,4},{6,7},{7,6},{8,9},{9,8},{10,11... | collective-permute-start | bytes 24584 | tf_op jit(solution)/shard_map/ppermute | solution.py:293
  117.7 16.3 %all-to-all-start.4 = ((bf16[8,128,128]{2,1,0:T(8,128)(2,1)}), bf16[8,128,128]{2,1,0:T(8,128)(2,1)S(1)}, u32[]{:S(2)}, u32[]{:S(2)}) async-start(bf16[8,128,128]{2,1,0:T(8,128)(2,1)} %shard_map.107), calls=%async_computation.4 | async-start | bytes 524288 | tf_op jit(solution)/shard_map/all_to_all | solution.py:62
  125.3 3.4 %collective-permute-start.4 = (bf16[2,256,256]{2,1,0:T(8,128)(2,1)S(1)}, bf16[2,256,256]{2,1,0:T(8,128)(2,1)S(1)}, u32[]{:S(2)}, u32[]{:S(2)}) collective-permute-start(bf16[2,256,256]{2,1,0:T(8,128)(2,1)S(1)} %pad_maximum_fusion.1.own_ref), channel_id=1, source_target_pairs={{0,1},{1,0},{2,3},{3,2},{4,5},{5,4},{6,7},{7,6},{8,9},{9,8},{10,11... | collective-permute-start | bytes 786440 | tf_op jit(solution)/shard_map/ppermute | solution.py:293
